TPU v7x, 32 devices: a whole 2x2x4 slice. The times are simulated.
32 devices in a mesh: row: 8 (over y, x, core), col: 4 (over z).
Axes of the slice: x: 2, y: 2, z: 4, core: 2. Of those that a mesh axis runs over, the one named last changes fastest.
Arguments:
- inputs: bfloat16 [4096, 2048], P('row', 'col'), may hold values from -6 to 6
- segment_ids: int32 [4096], P('row'), may hold values from 0 to 15, as said below
- norm_gain: float32 [2048], P('col'), may hold values from 0.25 to 1.75
- query_weight: bfloat16 [2048, 2048], P('row', 'col'), may hold values from -0.125 to 0.125
- key_weight: bfloat16 [2048, 2048], P('row', 'col'), may hold values from -0.125 to 0.125
- value_weight: bfloat16 [2048, 4096], P('row', 'col'), may hold values from -0.125 to 0.125
- gate_weight: bfloat16 [2048, 4096], P('row', 'col'), may hold values from -0.125 to 0.125
- decay_weight: bfloat16 [2048, 16], P('row', 'col'), may hold values from -0.125 to 0.125
- beta_weight: bfloat16 [2048, 16], P('row', 'col'), may hold values from -0.125 to 0.125
- query_conv: float32 [4, 2048], P(None, 'col'), may hold values from -3 to 3
- key_conv: float32 [4, 2048], P(None, 'col'), may hold values from -3 to 3
- value_conv: float32 [4, 4096], P(None, 'col'), may hold values from -3 to 3
- decay_log: float32 [16], P('col'), may hold values from -4.5 to 0
- decay_bias: float32 [16], P('col'), may hold values from -6 to -1
- head_gain: float32 [256], replicated, may hold values from 0.25 to 1.75
- out_weight: bfloat16 [4096, 2048], P('col', 'row'), may hold values from -0.125 to 0.125
- second_gain: float32 [2048], P('col'), may hold values from 0.25 to 1.75
- hidden_gate: bfloat16 [2048, 5504], P('row', 'col'), may hold values from -0.125 to 0.125
- hidden_up: bfloat16 [2048, 5504], P('row', 'col'), may hold values from -0.125 to 0.125
- hidden_down: bfloat16 [5504, 2048], P('col', 'row'), may hold values from -0.15625 to 0.15625
- cotangent: bfloat16 [4096, 2048], P('row', 'col'), may hold values from -6 to 6
Outputs:
- result: float32 [4096, 2048], P('row', 'col')
- grad_inputs: float32 [4096, 2048], P('row', 'col')
- grad_norm_gain: float32 [2048], P('col')
- grad_query_weight: float32 [2048, 2048], P('row', 'col')
- grad_key_weight: float32 [2048, 2048], P('row', 'col')
- grad_value_weight: float32 [2048, 4096], P('row', 'col')
- grad_gate_weight: float32 [2048, 4096], P('row', 'col')
- grad_decay_weight: float32 [2048, 16], P('row', 'col')
- grad_beta_weight: float32 [2048, 16], P('row', 'col')
- grad_query_conv: float32 [4, 2048], P(None, 'col')
- grad_key_conv: float32 [4, 2048], P(None, 'col')
- grad_value_conv: float32 [4, 4096], P(None, 'col')
- grad_decay_log: float32 [16], P('col')
- grad_decay_bias: float32 [16], P('col')
- grad_head_gain: float32 [256], replicated
- grad_out_weight: float32 [4096, 2048], P('col', 'row')
- grad_second_gain: float32 [2048], P('col')
- grad_hidden_gate: float32 [2048, 5504], P('row', 'col')
- grad_hidden_up: float32 [2048, 5504], P('row', 'col')
- grad_hidden_down: float32 [5504, 2048], P('col', 'row')
Inputs may be any that keep to these rules, and one draw needn't show every extreme that they name: `segment_ids`: never falling; the tokens i * 512 to (i + 1) * 512 - 1 hold exactly the two segments 2 i and 2 i + 1, in that order, each nonempty, the second of 256 tokens or more.
All inputs are finite; a program needn't handle non-finite values.
Results may differ from a plain program's by a relative error of at most 0.015.
Values may be sent and summed in bfloat16 or wider, within the bound.
No kernel may reach another device: no remote copies, remote signals or barrier semaphores. Data moves between devices by JAX's collectives and lax.ppermute only.
A program may use at most 192 MiB of HBM per device.

v0:
```python
import jax
import jax.numpy as jnp
from jax import lax
from jax.sharding import PartitionSpec as P

D = 2048
CH = 64


HIGH = lax.Precision.HIGHEST


def rms_inverse(values, epsilon):
    return lax.rsqrt(jnp.mean(values * values, axis=-1, keepdims=True) + epsilon)


def causal_conv(series, kernel, segment_ids):
    total = series * kernel[3]
    for shift in (1, 2, 3):
        moved = jnp.concatenate(
            [jnp.zeros((shift, series.shape[1]), series.dtype), series[:-shift]], axis=0
        )
        prior = jnp.concatenate([jnp.full((shift,), -1, jnp.int32), segment_ids[:-shift]], axis=0)
        total = total + jnp.where((prior == segment_ids)[:, None], moved, 0.0) * kernel[3 - shift]
    return total


def delta_rule(queries, keys_in, values, log_decay, betas, segment_ids):
    tokens, heads, key_size = queries.shape
    value_size = values.shape[2]
    groups = tokens // CH

    def by_block(array):
        return jnp.transpose(array.reshape(groups, CH, heads, array.shape[2]), (2, 0, 1, 3))

    query_blocks = by_block(queries)
    key_blocks = by_block(keys_in)
    value_blocks = by_block(values)
    decay_blocks = jnp.transpose(log_decay.reshape(groups, CH, heads), (2, 0, 1))
    beta_blocks = jnp.transpose(betas.reshape(groups, CH, heads), (2, 0, 1))
    seg_blocks = segment_ids.reshape(groups, CH)
    running = jnp.cumsum(decay_blocks, axis=2)
    rows_index = lax.broadcasted_iota(jnp.int32, (CH, CH), 0)
    cols_index = lax.broadcasted_iota(jnp.int32, (CH, CH), 1)
    same_seg = seg_blocks[:, :, None] == seg_blocks[:, None, :]
    keep_incl = same_seg & (rows_index >= cols_index)
    keep_strict = same_seg & (rows_index > cols_index)
    spread_decay = running[..., :, None] - running[..., None, :]
    decay_matrix = jnp.where(keep_incl, jnp.exp(jnp.minimum(spread_decay, 0.0)), 0.0)
    before = jnp.concatenate([seg_blocks[:1, :1] - 1, seg_blocks[:-1, -1:]], axis=0)
    carried = jnp.where(seg_blocks == before, jnp.exp(running), 0.0)
    key_inner = jnp.einsum("hnid,hnjd->hnij", key_blocks, key_blocks, precision=HIGH)
    lower_part = jnp.where(keep_strict, beta_blocks[..., :, None] * decay_matrix * key_inner, 0.0)
    identity = jnp.eye(CH, dtype=jnp.float32)
    right_side = jnp.concatenate(
        [beta_blocks[..., None] * value_blocks, (beta_blocks * carried)[..., None] * key_blocks],
        axis=3,
    )
    solved = jax.scipy.linalg.solve_triangular(
        identity + lower_part, right_side, lower=True, unit_diagonal=True
    )
    fresh = solved[..., :value_size]
    mixing = solved[..., value_size:]
    query_key = (
        jnp.einsum("hnid,hnjd->hnij", query_blocks, key_blocks, precision=HIGH) * decay_matrix
    )
    tail = decay_matrix[..., CH - 1, :]
    tail_state = carried[..., CH - 1]

    def advance(state, item):
        fresh_now, mixing_now, query_now, key_now, score_now, carried_now, tail_now, tail_keep = (
            item
        )
        written = fresh_now - jnp.einsum("hld,hdv->hlv", mixing_now, state, precision=HIGH)
        output = carried_now[..., None] * jnp.einsum(
            "hld,hdv->hlv", query_now, state, precision=HIGH
        )
        output = output + jnp.einsum("hij,hjv->hiv", score_now, written, precision=HIGH)
        state = tail_keep[:, None, None] * state + jnp.einsum(
            "hld,hlv->hdv", key_now * tail_now[..., None], written, precision=HIGH
        )
        return (state, output)

    items = tuple(
        (
            jnp.moveaxis(array, 1, 0)
            for array in (
                fresh,
                mixing,
                query_blocks,
                key_blocks,
                query_key,
                carried,
                tail,
                tail_state,
            )
        )
    )
    start_state = jnp.zeros((heads, key_size, value_size), jnp.float32)
    unused, outputs = lax.scan(advance, start_state, items)
    return jnp.transpose(outputs, (0, 2, 1, 3)).reshape(tokens, heads, value_size)


def mixer(
    query_pre,
    key_pre,
    value_pre,
    gate_pre,
    decay_pre,
    beta_pre,
    query_conv,
    key_conv,
    value_conv,
    decay_log,
    decay_bias,
    head_gain,
    segment_ids,
):
    tokens = query_pre.shape[0]
    heads = decay_pre.shape[1]
    key_size = query_pre.shape[1] // heads
    value_size = value_pre.shape[1] // heads
    query_act = jax.nn.silu(causal_conv(query_pre, query_conv, segment_ids)).reshape(
        tokens, heads, key_size
    )
    key_act = jax.nn.silu(causal_conv(key_pre, key_conv, segment_ids)).reshape(
        tokens, heads, key_size
    )
    value_act = jax.nn.silu(causal_conv(value_pre, value_conv, segment_ids)).reshape(
        tokens, heads, value_size
    )
    queries = (
        query_act
        * lax.rsqrt(jnp.sum(query_act * query_act, axis=-1, keepdims=True) + 1e-06)
        / jnp.sqrt(key_size * 1.0)
    )
    keys_in = key_act * lax.rsqrt(jnp.sum(key_act * key_act, axis=-1, keepdims=True) + 1e-06)
    log_decay = -jnp.exp(decay_log) * jax.nn.softplus(decay_pre + decay_bias)
    betas = jax.nn.sigmoid(beta_pre)
    heads_out = delta_rule(queries, keys_in, value_act, log_decay, betas, segment_ids)
    heads_normed = heads_out * rms_inverse(heads_out, 1e-05) * head_gain
    return heads_normed.reshape(tokens, heads * value_size) * jax.nn.silu(gate_pre)


def contract_tokens(left, right):
    return lax.dot_general(
        left, right, (((0,), (0,)), ((), ())), preferred_element_type=jnp.float32
    )


def contract_features(left, right):
    return lax.dot_general(
        left, right, (((1,), (1,)), ((), ())), preferred_element_type=jnp.float32
    )


def per_device(
    inputs,
    segment_ids,
    norm_gain,
    query_weight,
    key_weight,
    value_weight,
    gate_weight,
    decay_weight,
    beta_weight,
    query_conv,
    key_conv,
    value_conv,
    decay_log,
    decay_bias,
    head_gain,
    out_weight,
    second_gain,
    hidden_gate,
    hidden_up,
    hidden_down,
    cotangent,
):
    token_rows = inputs.shape[0]

    def spread_cols(values):
        return lax.all_gather(values, "col", axis=1, tiled=True)

    def total_cols(partial_value):
        return lax.psum_scatter(partial_value, "col", scatter_dimension=1, tiled=True)

    def stat_cols(values):
        return lax.psum(values, "col")

    def fold_in(update, initial):
        return update(
            initial,
            (
                lax.all_gather(query_weight, "row", axis=0, tiled=True),
                lax.all_gather(key_weight, "row", axis=0, tiled=True),
                lax.all_gather(value_weight, "row", axis=0, tiled=True),
                lax.all_gather(gate_weight, "row", axis=0, tiled=True),
                lax.all_gather(decay_weight, "row", axis=0, tiled=True),
                lax.all_gather(beta_weight, "row", axis=0, tiled=True),
            ),
            jnp.int32(0),
        )

    def fold_out(update, initial):
        return update(initial, lax.all_gather(out_weight, "row", axis=1, tiled=True), jnp.int32(0))

    def fold_mlp(update, initial):
        return update(
            initial,
            (
                lax.all_gather(hidden_gate, "row", axis=0, tiled=True),
                lax.all_gather(hidden_up, "row", axis=0, tiled=True),
            ),
            jnp.int32(0),
        )

    def fold_down(update, initial):
        return update(initial, lax.all_gather(hidden_down, "row", axis=1, tiled=True), jnp.int32(0))

    def apply_mlp(source):

        def update(totals, pieces, offset):
            return (
                jnp.dot(source, pieces[0], preferred_element_type=jnp.float32),
                jnp.dot(source, pieces[1], preferred_element_type=jnp.float32),
            )

        empty = jnp.zeros((token_rows, hidden_gate.shape[1]), jnp.float32)
        return fold_mlp(update, (empty, empty))

    def return_mlp(gradients):

        def update(totals, pieces, offset):
            term = contract_features(gradients[0], pieces[0]) + contract_features(
                gradients[1], pieces[1]
            )
            return term

        return fold_mlp(update, jnp.zeros((token_rows, D), jnp.float32))

    def apply_down(source):

        def update(totals, pieces, offset):
            term = jnp.dot(source, pieces, preferred_element_type=jnp.float32)
            return term

        return fold_down(update, jnp.zeros((token_rows, D), jnp.float32))

    def return_down(gradient):

        def update(totals, pieces, offset):
            return contract_features(gradient, pieces)

        return fold_down(update, jnp.zeros((token_rows, hidden_down.shape[0]), jnp.float32))

    wide_inputs = inputs.astype(jnp.float32)
    first_scale = lax.rsqrt(stat_cols(jnp.sum(wide_inputs * wide_inputs, axis=1)) / D + 1e-05)[
        :, None
    ]
    hidden = spread_cols((wide_inputs * first_scale * norm_gain).astype(jnp.bfloat16))

    def update(totals, pieces, offset):
        return tuple(
            (
                jnp.dot(hidden, piece_block, preferred_element_type=jnp.float32)
                for piece_block in pieces
            )
        )

    initial = tuple(
        (
            jnp.zeros((token_rows, weight_block.shape[1]), jnp.float32)
            for weight_block in (
                query_weight,
                key_weight,
                value_weight,
                gate_weight,
                decay_weight,
                beta_weight,
            )
        )
    )
    query_pre, key_pre, value_pre, gate_pre, decay_pre, beta_pre = fold_in(update, initial)

    def mix_local(
        query_in,
        key_in,
        value_in,
        gate_in,
        decay_in,
        beta_in,
        query_taps,
        key_taps,
        value_taps,
        decay_rates,
        decay_shift,
        gain_heads,
    ):
        return mixer(
            query_in,
            key_in,
            value_in,
            gate_in,
            decay_in,
            beta_in,
            query_taps,
            key_taps,
            value_taps,
            decay_rates,
            decay_shift,
            gain_heads,
            segment_ids,
        )

    mixed, mix_back = jax.vjp(
        mix_local,
        query_pre,
        key_pre,
        value_pre,
        gate_pre,
        decay_pre,
        beta_pre,
        query_conv,
        key_conv,
        value_conv,
        decay_log,
        decay_bias,
        head_gain,
    )
    mixed_low = mixed.astype(jnp.bfloat16)

    def apply_update(totals, pieces, offset):
        term = jnp.dot(mixed_low, pieces, preferred_element_type=jnp.float32)
        return term

    residual = wide_inputs + total_cols(
        fold_out(apply_update, jnp.zeros((token_rows, D), jnp.float32))
    )
    second_scale = lax.rsqrt(stat_cols(jnp.sum(residual * residual, axis=1)) / D + 1e-05)[:, None]
    second = spread_cols((residual * second_scale * second_gain).astype(jnp.bfloat16))
    gate_value, up_value = apply_mlp(second)
    gate_sigmoid = jax.nn.sigmoid(gate_value)
    product = (gate_value * gate_sigmoid * up_value).astype(jnp.bfloat16)
    result = residual + total_cols(apply_down(product))
    grad_rows = spread_cols(cotangent)
    down_grad = contract_tokens(product, grad_rows)
    grad_product = return_down(grad_rows)
    grad_up = (grad_product * gate_value * gate_sigmoid).astype(jnp.bfloat16)
    grad_gate = (
        grad_product * up_value * gate_sigmoid * (1.0 + gate_value * (1.0 - gate_sigmoid))
    ).astype(jnp.bfloat16)
    gate_grad = contract_tokens(second, grad_gate)
    up_grad = contract_tokens(second, grad_up)
    grad_second = total_cols(return_mlp((grad_gate, grad_up)))
    scaled_second = grad_second * second_gain
    second_gain_part = jnp.sum(grad_second * residual * second_scale, axis=0)
    second_inner = stat_cols(jnp.sum(scaled_second * residual, axis=1))[:, None]
    grad_residual = (
        cotangent.astype(jnp.float32)
        + second_scale * scaled_second
        - residual * second_scale * second_scale * second_scale * second_inner / D
    )
    residual_rows = spread_cols(grad_residual.astype(jnp.bfloat16))
    out_grad = contract_tokens(mixed_low, residual_rows)

    def return_update(totals, pieces, offset):
        return contract_features(residual_rows, pieces)

    grad_mixed = fold_out(return_update, jnp.zeros((token_rows, out_weight.shape[0]), jnp.float32))
    mixer_grads = mix_back(grad_mixed)
    pre_low = tuple((grad_block.astype(jnp.bfloat16) for grad_block in mixer_grads[:6]))
    in_grads = tuple((contract_tokens(hidden, grad_block) for grad_block in pre_low))

    def update(totals, pieces, offset):
        term = jnp.zeros((token_rows, pieces[0].shape[0]), jnp.float32)
        for grad_block, piece_block in zip(pre_low, pieces):
            term = term + contract_features(grad_block, piece_block)
        return term

    grad_hidden = total_cols(fold_in(update, jnp.zeros((token_rows, D), jnp.float32)))
    scaled_first = grad_hidden * norm_gain
    first_gain_part = jnp.sum(grad_hidden * wide_inputs * first_scale, axis=0)
    first_inner, head_part = lax.psum(
        (jnp.sum(scaled_first * wide_inputs, axis=1), mixer_grads[11]), "col"
    )
    grad_inputs = (
        grad_residual
        + first_scale * scaled_first
        - wide_inputs * first_scale * first_scale * first_scale * first_inner[:, None] / D
    )
    small = lax.psum(
        (
            first_gain_part,
            second_gain_part,
            mixer_grads[6],
            mixer_grads[7],
            mixer_grads[8],
            mixer_grads[9],
            mixer_grads[10],
            head_part,
        ),
        "row",
    )
    blocks_out = (
        lax.psum_scatter(
            in_grads[0].astype(jnp.bfloat16), "row", scatter_dimension=0, tiled=True
        ).astype(jnp.float32),
        lax.psum_scatter(
            in_grads[1].astype(jnp.bfloat16), "row", scatter_dimension=0, tiled=True
        ).astype(jnp.float32),
        lax.psum_scatter(
            in_grads[2].astype(jnp.bfloat16), "row", scatter_dimension=0, tiled=True
        ).astype(jnp.float32),
        lax.psum_scatter(
            in_grads[3].astype(jnp.bfloat16), "row", scatter_dimension=0, tiled=True
        ).astype(jnp.float32),
        lax.psum_scatter(
            in_grads[4].astype(jnp.bfloat16), "row", scatter_dimension=0, tiled=True
        ).astype(jnp.float32),
        lax.psum_scatter(
            in_grads[5].astype(jnp.bfloat16), "row", scatter_dimension=0, tiled=True
        ).astype(jnp.float32),
        lax.psum_scatter(
            out_grad.astype(jnp.bfloat16), "row", scatter_dimension=1, tiled=True
        ).astype(jnp.float32),
        lax.psum_scatter(
            gate_grad.astype(jnp.bfloat16), "row", scatter_dimension=0, tiled=True
        ).astype(jnp.float32),
        lax.psum_scatter(
            up_grad.astype(jnp.bfloat16), "row", scatter_dimension=0, tiled=True
        ).astype(jnp.float32),
        lax.psum_scatter(
            down_grad.astype(jnp.bfloat16), "row", scatter_dimension=1, tiled=True
        ).astype(jnp.float32),
    )
    return (
        result,
        grad_inputs,
        small[0],
        blocks_out[0],
        blocks_out[1],
        blocks_out[2],
        blocks_out[3],
        blocks_out[4],
        blocks_out[5],
        small[2],
        small[3],
        small[4],
        small[5],
        small[6],
        small[7],
        blocks_out[6],
        small[1],
        blocks_out[7],
        blocks_out[8],
        blocks_out[9],
    )


def solution(mesh):
    placed = (
        P("row", "col"),
        P("row"),
        P("col"),
        P("row", "col"),
        P("row", "col"),
        P("row", "col"),
        P("row", "col"),
        P("row", "col"),
        P("row", "col"),
        P(None, "col"),
        P(None, "col"),
        P(None, "col"),
        P("col"),
        P("col"),
        P(),
        P("col", "row"),
        P("col"),
        P("row", "col"),
        P("row", "col"),
        P("col", "row"),
        P("row", "col"),
    )
    return jax.shard_map(
        per_device,
        mesh=mesh,
        in_specs=placed,
        out_specs=(
            P("row", "col"),
            P("row", "col"),
            P("col"),
            P("row", "col"),
            P("row", "col"),
            P("row", "col"),
            P("row", "col"),
            P("row", "col"),
            P("row", "col"),
            P(None, "col"),
            P(None, "col"),
            P(None, "col"),
            P("col"),
            P("col"),
            P(),
            P("col", "row"),
            P("col"),
            P("row", "col"),
            P("row", "col"),
            P("col", "row"),
        ),
        check_vma=False,
    )
```

profile of v0, /device:TPU:0, one launch (start us, length us, event | category | flops | bytes accessed | tf_op | source)
XLA Modules:
  0.0 1663.2 jit_solution(4023837727813419286)
XLA Ops:
  8.6 13.5 psum.91
  28.3 8.9 all_gather.53
  37.3 8.9 all_gather.55
  47.5 20.9 %all-gather.13.cloned.1.call-done = bf16[512,2048]{1,0:T(8,128)(2,1)} async-done(((bf16[512,512]{1,0:T(8,128)(2,1)}), bf16[512,2048]{1,0:T(8,128)(2,1)}) %all-gather.13.cloned.1.call-update) | async-done | bytes 2097168 | tf_op jit(solution)/shard_map/all_gather | solution.py:183
  75.0 22.0 %all-gather.19.cloned.1.call-done = bf16[2048,512]{1,0:T(8,128)(2,1)} async-done(((bf16[256,512]{1,0:T(8,128)(2,1)}), bf16[2048,512]{1,0:T(8,128)(2,1)}) %all-gather.19.cloned.1.call-update) | async-done | bytes 2097168 | tf_op jit(solution)/shard_map/all_gather | solution.py:195
  100.6 26.3 %all-gather.15.cloned.1.call-done = bf16[2048,512]{1,0:T(8,128)(2,1)} async-done(((bf16[256,512]{1,0:T(8,128)(2,1)}), bf16[2048,512]{1,0:T(8,128)(2,1)}) %all-gather.15.cloned.1.call-update) | async-done | bytes 2097168 | tf_op jit(solution)/shard_map/all_gather | solution.py:196
  157.0 158.8 %custom-call.10 = f32[4,8,1,64,64]{3,4,2,1,0:T(8,128)} custom-call(f32[4,8,1,64,64]{4,3,2,1,0:T(8,128)} %get-tuple-element.1048), custom_call_target="InvertDiagBlocksLowerTriangular" | custom-call | tf_op jit(solution)/shard_map/jvp(jit(_solve_triangular))/vmap(vmap())/triangular_solve | solution.py:59
  319.6 5.1 fusion.216
  346.2 69.5 %while.58 = (s32[]{:T(128)}, f32[4,128,256]{2,1,0:T(8,128)S(1)}, f32[8,4,64,256]{3,2,1,0:T(8,128)}, f32[8,4,128,256]{3,2,1,0:T(8,128)}, f32[8,4,64,256]{3,2,1,0:...) while((s32[]{:T(128)}, f32[4,128,256]{2,1,0:T(8,128)S(1)}, ...), condition=%wide.region_6.7_spmd.clone, body=%wide.region_5.6_spmd.clone.sunk | while | flops 353370112 | bytes 6313722 | solution.py:100
  424.0 8.4 multiply_convert_fusion.3
  432.4 6.9 fusion.218
  440.2 76.1 %reduce-scatter.19.cloned.1.call-done = f32[512,512]{1,0:T(8,128)} async-done(((f32[512,2048]{1,0:T(8,128)}), f32[512,512]{1,0:T(8,128)}) %reduce-scatter.19.cloned.1.call-update) | async-done | bytes 1048592 | tf_op jit(solution)/shard_map/reduce_scatter | solution.py:186
  517.7 11.0 psum.92
  531.8 30.8 %all-gather.27.cloned.1.call-done = bf16[2048,1376]{0,1:T(8,128)(2,1)} async-done(((bf16[256,1376]{0,1:T(8,128)(2,1)}), bf16[2048,1376]{0,1:T(8,128)(2,1)}) %all-gather.27.cloned.1.call-update) | async-done | bytes 5636112 | tf_op jit(solution)/shard_map/all_gather | solution.py:212
  562.6 48.2 %all-gather.25.cloned.1.call-done = bf16[512,2048]{1,0:T(8,128)(2,1)} async-done(((bf16[512,512]{1,0:T(8,128)(2,1)}), bf16[512,2048]{1,0:T(8,128)(2,1)}) %all-gather.25.cloned.1.call-update) | async-done | bytes 2097168 | tf_op jit(solution)/shard_map/all_gather | solution.py:183
  610.8 7.9 fusion.219
  618.7 36.5 %all-gather.29.cloned.1.call-done = bf16[2048,1376]{0,1:T(8,128)(2,1)} async-done(((bf16[256,1376]{0,1:T(8,128)(2,1)}), bf16[2048,1376]{0,1:T(8,128)(2,1)}) %all-gather.29.cloned.1.call-update) | async-done | bytes 5636112 | tf_op jit(solution)/shard_map/all_gather | solution.py:213
  655.2 7.9 fusion.220
  663.2 39.7 %all-gather.33.cloned.1.call-done = bf16[512,2048]{1,0:T(8,128)(2,1)} async-done(((bf16[512,512]{1,0:T(8,128)(2,1)}), bf16[512,2048]{1,0:T(8,128)(2,1)}) %all-gather.33.cloned.1.call-update) | async-done | bytes 2097168 | tf_op jit(solution)/shard_map/all_gather | solution.py:183
  702.9 44.4 %all-gather.31.cloned.1.call-done = bf16[1376,2048]{1,0:T(8,128)(2,1)} async-done(((bf16[1376,256]{1,0:T(8,128)(2,1)}), bf16[1376,2048]{1,0:T(8,128)(2,1)}) %all-gather.31.cloned.1.call-update) | async-done | bytes 5636112 | tf_op jit(solution)/shard_map/all_gather | solution.py:219
  747.3 10.3 multiply_convert_fusion
  757.6 6.8 fusion.222
  764.4 5.0 convolution_add_fusion.5
  769.5 8.5 fusion.221
  778.0 68.3 %reduce-scatter.23.cloned.1.call-done = f32[512,512]{1,0:T(8,128)} async-done(((f32[512,2048]{1,0:T(8,128)}), f32[512,512]{1,0:T(8,128)}) %reduce-scatter.23.cloned.1.call-update) | async-done | bytes 1048592 | tf_op jit(solution)/shard_map/reduce_scatter | solution.py:186
  848.0 11.1 psum.93
  859.1 66.8 %reduce-scatter.21.cloned.1.call-done = f32[512,512]{1,0:T(8,128)} async-done(((f32[512,2048]{1,0:T(8,128)}), f32[512,512]{1,0:T(8,128)}) %reduce-scatter.21.cloned.1.call-update) | async-done | bytes 1048592 | tf_op jit(solution)/shard_map/reduce_scatter | solution.py:186
  929.3 7.6 convolution_convert_fusion.1
  938.3 6.4 convolution_convert_fusion
  946.1 6.4 convolution_convert_fusion.2
  953.0 22.9 %all-gather.35.cloned.1.call-done = bf16[512,2048]{1,0:T(8,128)(2,1)} async-done(((bf16[512,512]{1,0:T(8,128)(2,1)}), bf16[512,2048]{1,0:T(8,128)(2,1)}) %all-gather.35.cloned.1.call-update) | async-done | bytes 2097168 | tf_op jit(solution)/shard_map/all_gather | solution.py:183
  975.9 8.9 multiply_reduce_fusion
  999.2 152.0 %while.59 = (s32[]{:T(128)}, f32[4,128,256]{2,1,0:T(8,128)S(1)}, f32[8,4,64,256]{3,2,1,0:T(8,128)}, f32[8,4,64,128]{3,2,1,0:T(8,128)S(1)}, f32[8,4,64,128]{3,2,0...) while((s32[]{:T(128)}, f32[4,128,256]{2,1,0:T(8,128)S(1)}, ...), condition=%wide.region_20.21_spmd.clone, body=%wide.region_16.20_spmd.clone.sunk | while | flops 706379264 | bytes 10377084 | solution.py:100
  1152.2 4.4 broadcast_multiply_fusion
  1159.4 4.5 fusion.83
  1204.5 4.6 multiply_reduce_fusion.15
  1230.8 6.1 convolution_convert_fusion.3
  1247.9 4.3 convolution_convert_fusion.5
  1253.5 4.4 convolution_convert_fusion.4
  1281.0 4.8 reduce-scatter.43.cloned.1.call-done
  1287.4 43.4 %reduce-scatter.29.cloned.1.call-done = bf16[256,512]{1,0:T(8,128)(2,1)} async-done(((bf16[2048,512]{1,0:T(8,128)(2,1)}), bf16[256,512]{1,0:T(8,128)(2,1)}) %reduce-scatter.29.cloned.1.call-update) | async-done | bytes 262160 | tf_op jit(solution)/shard_map/reduce_scatter | solution.py:409
  1332.6 42.7 %reduce-scatter.27.cloned.1.call-done = bf16[256,512]{1,0:T(8,128)(2,1)} async-done(((bf16[2048,512]{1,0:T(8,128)(2,1)}), bf16[256,512]{1,0:T(8,128)(2,1)}) %reduce-scatter.27.cloned.1.call-update) | async-done | bytes 262160 | tf_op jit(solution)/shard_map/reduce_scatter | solution.py:406
  1377.1 53.3 %reduce-scatter.35.cloned.1.call-done = bf16[1024,256]{1,0:T(8,128)(2,1)} async-done(((bf16[1024,2048]{1,0:T(8,128)(2,1)}), bf16[1024,256]{1,0:T(8,128)(2,1)}) %reduce-scatter.35.cloned.1.call-update) | async-done | bytes 524304 | tf_op jit(solution)/shard_map/reduce_scatter | solution.py:424
  1432.4 52.5 %reduce-scatter.31.cloned.1.call-done = bf16[256,1024]{1,0:T(8,128)(2,1)} async-done(((bf16[2048,1024]{1,0:T(8,128)(2,1)}), bf16[256,1024]{1,0:T(8,128)(2,1)}) %reduce-scatter.31.cloned.1.call-update) | async-done | bytes 524304 | tf_op jit(solution)/shard_map/reduce_scatter | solution.py:412
  1487.0 53.0 %reduce-scatter.33.cloned.1.call-done = bf16[256,1024]{1,0:T(8,128)(2,1)} async-done(((bf16[2048,1024]{1,0:T(8,128)(2,1)}), bf16[256,1024]{1,0:T(8,128)(2,1)}) %reduce-scatter.33.cloned.1.call-update) | async-done | bytes 524304 | tf_op jit(solution)/shard_map/reduce_scatter | solution.py:415
  1542.1 76.8 %reduce-scatter.25.cloned.1.call-done = f32[512,512]{1,0:T(8,128)} async-done(((f32[512,2048]{1,0:T(8,128)}), f32[512,512]{1,0:T(8,128)}) %reduce-scatter.25.cloned.1.call-update) | async-done | bytes 1048592 | tf_op jit(solution)/shard_map/reduce_scatter | solution.py:186
  1620.7 10.9 all-reduce.37
  1631.7 23.5 %all-reduce.36 = (f32[512]{0:T(512)}, f32[4,512]{1,0:T(4,128)}, f32[4,512]{1,0:T(4,128)}, f32[4,1024]{1,0:T(4,128)}, f32[4]{0:T(128)}, /*index=5*/f32[4]{0:T(128)}, f32[256]{0:T(256)}, f32[512]{0:T(512)}) all-reduce(f32[512]{0:T(512)S(1)} %get-tuple-element.900, ...), channel_id=1, replica_groups=mesh['row'=8,'col'=4] {'row'}, use_global_device_ids=true, to_apply=%region_33.34 | all-reduce | flops 9480 | bytes 75840 | tf_op jit(solution)/shard_map/psum | solution.py:392
  (681 shorter events, 445.1 us)
Async XLA Ops:
  7.2 61.2 %all-gather.13.cloned.1.call-start = ((), (), s32[]{:S(2)}) async-start(), calls=%async_computation.14 | async-start | bytes 2621440 | tf_op jit(solution)/shard_map/all_gather | solution.py:183
  7.3 39.9 %copy-start.103 = (f32[256]{0:T(256)S(1)}, f32[256]{0:T(256)}, u32[]{:S(2)}) copy-start(f32[256]{0:T(256)} %param.39) | copy-start | bytes 3076
  8.6 59.8 %copy-start.110 = (f32[4]{0:T(128)S(1)}, f32[4]{0:T(128)}, u32[]{:S(2)}) copy-start(f32[4]{0:T(128)} %param.38) | copy-start | bytes 52
  22.1 49.2 %copy-start.79 = (f32[512]{0:T(512)}, f32[512]{0:T(512)S(1)}, u32[]{:S(2)}) copy-start(f32[512]{0:T(512)S(1)} %add_rsqrt_fusion.3) | copy-start | bytes 6148
  24.1 72.9 %all-gather.19.cloned.1.call-start = ((), (), s32[]{:S(2)}) async-start(), calls=%async_computation.17 | async-start | bytes 2359296 | tf_op jit(solution)/shard_map/all_gather | solution.py:195
  24.9 102.0 %all-gather.15.cloned.1.call-start = ((), (), s32[]{:S(2)}) async-start(), calls=%async_computation.15 | async-start | bytes 2359296 | tf_op jit(solution)/shard_map/all_gather | solution.py:196
  25.6 294.0 %all-gather.17.cloned.1.call-start = ((), (), s32[]{:S(2)}) async-start(), calls=%async_computation.16 | async-start | bytes 4718592 | tf_op jit(solution)/shard_map/all_gather | solution.py:197
  26.2 397.7 %all-gather.21.cloned.1.call-start = ((), (), s32[]{:S(2)}) async-start(), calls=%async_computation.18 | async-start | bytes 4718592 | tf_op jit(solution)/shard_map/all_gather | solution.py:198
  26.8 405.7 %all-gather.23.cloned.1.call-start = ((), (), s32[]{:S(2)}) async-start(), calls=%async_computation.19 | async-start | bytes 4718592 | tf_op jit(solution)/shard_map/all_gather | solution.py:206
  27.3 488.9 %reduce-scatter.19.cloned.1.call-start = ((), (), s32[]{:S(2)}) async-start(), calls=%async_computation.20 | async-start | bytes 5242880 | tf_op jit(solution)/shard_map/reduce_scatter | solution.py:186
  28.2 102.2 %copy-start.84 = (f32[1,512]{1,0:T(1,128)}, f32[1,512]{1,0:T(1,128)S(1)}, u32[]{:S(2)}) copy-start(f32[1,512]{1,0:T(1,128)S(1)} %get-tuple-element.1060) | copy-start | bytes 6148
  28.2 102.2 %copy-start.86 = (f32[1,512]{1,0:T(1,128)}, f32[1,512]{1,0:T(1,128)S(1)}, u32[]{:S(2)}) copy-start(f32[1,512]{1,0:T(1,128)S(1)} %get-tuple-element.1062) | copy-start | bytes 6148
  28.2 102.2 %copy-start.90 = (f32[1,512]{1,0:T(1,128)}, f32[1,512]{1,0:T(1,128)S(1)}, u32[]{:S(2)}) copy-start(f32[1,512]{1,0:T(1,128)S(1)} %get-tuple-element.1061) | copy-start | bytes 6148
  28.2 102.2 %copy-start.96 = (f32[1,512]{1,0:T(1,128)}, f32[1,512]{1,0:T(1,128)S(1)}, u32[]{:S(2)}) copy-start(f32[1,512]{1,0:T(1,128)S(1)} %get-tuple-element.1059) | copy-start | bytes 6148
  28.3 102.1 %copy-start.88 = (f32[1,512]{1,0:T(1,128)}, f32[1,512]{1,0:T(1,128)S(1)}, u32[]{:S(2)}) copy-start(f32[1,512]{1,0:T(1,128)S(1)} %get-tuple-element.1064) | copy-start | bytes 6148
  28.3 102.1 %copy-start.92 = (f32[1,512]{1,0:T(1,128)}, f32[1,512]{1,0:T(1,128)S(1)}, u32[]{:S(2)}) copy-start(f32[1,512]{1,0:T(1,128)S(1)} %get-tuple-element.1066) | copy-start | bytes 6148
  28.3 102.1 %copy-start.94 = (f32[1,512]{1,0:T(1,128)}, f32[1,512]{1,0:T(1,128)S(1)}, u32[]{:S(2)}) copy-start(f32[1,512]{1,0:T(1,128)S(1)} %get-tuple-element.1065) | copy-start | bytes 6148
  28.3 102.1 %copy-start.98 = (f32[1,512]{1,0:T(1,128)}, f32[1,512]{1,0:T(1,128)S(1)}, u32[]{:S(2)}) copy-start(f32[1,512]{1,0:T(1,128)S(1)} %get-tuple-element.1063) | copy-start | bytes 6148
  47.2 277.6 %copy-start.71 = (f32[1,1024]{1,0:T(1,128)}, f32[1,1024]{1,0:T(1,128)S(1)}, u32[]{:S(2)}) copy-start(f32[1,1024]{1,0:T(1,128)S(1)} %get-tuple-element.1053) | copy-start | bytes 12292
  47.2 277.6 %copy-start.73 = (f32[1,1024]{1,0:T(1,128)}, f32[1,1024]{1,0:T(1,128)S(1)}, u32[]{:S(2)}) copy-start(f32[1,1024]{1,0:T(1,128)S(1)} %get-tuple-element.1054) | copy-start | bytes 12292
  47.2 277.6 %copy-start.75 = (f32[1,1024]{1,0:T(1,128)}, f32[1,1024]{1,0:T(1,128)S(1)}, u32[]{:S(2)}) copy-start(f32[1,1024]{1,0:T(1,128)S(1)} %get-tuple-element.1055) | copy-start | bytes 12292
  47.2 277.6 %copy-start.77 = (f32[1,1024]{1,0:T(1,128)}, f32[1,1024]{1,0:T(1,128)S(1)}, u32[]{:S(2)}) copy-start(f32[1,1024]{1,0:T(1,128)S(1)} %get-tuple-element.1056) | copy-start | bytes 12292
  439.4 76.9 %copy-start.26 = (bf16[512,512]{1,0:T(8,128)(2,1)S(1)}, bf16[512,512]{1,0:T(8,128)(2,1)}, u32[]{:S(2)}) copy-start(bf16[512,512]{1,0:T(8,128)(2,1)} %param.25) | copy-start | bytes 1572868
  439.4 89.3 %copy-start.82 = (f32[512]{0:T(512)S(1)}, f32[512]{0:T(512)}, u32[]{:S(2)}) copy-start(f32[512]{0:T(512)} %param.41) | copy-start | bytes 6148
  439.4 123.2 %all-gather.27.cloned.1.call-start = ((), (), s32[]{:S(2)}) async-start(), calls=%async_computation.22 | async-start | bytes 6340608 | tf_op jit(solution)/shard_map/all_gather | solution.py:212
  440.1 170.7 %all-gather.25.cloned.1.call-start = ((), (), s32[]{:S(2)}) async-start(), calls=%async_computation.21 | async-start | bytes 2621440 | tf_op jit(solution)/shard_map/all_gather | solution.py:183
  529.7 125.6 %all-gather.29.cloned.1.call-start = ((), (), s32[]{:S(2)}) async-start(), calls=%async_computation.23 | async-start | bytes 6340608 | tf_op jit(solution)/shard_map/all_gather | solution.py:213
  530.3 172.6 %all-gather.33.cloned.1.call-start = ((), (), s32[]{:S(2)}) async-start(), calls=%async_computation.26 | async-start | bytes 2621440 | tf_op jit(solution)/shard_map/all_gather | solution.py:183
  531.0 216.3 %all-gather.31.cloned.1.call-start = ((), (), s32[]{:S(2)}) async-start(), calls=%async_computation.24 | async-start | bytes 6340608 | tf_op jit(solution)/shard_map/all_gather | solution.py:219
  531.6 314.8 %reduce-scatter.23.cloned.1.call-start = ((), (), s32[]{:S(2)}) async-start(), calls=%async_computation.27 | async-start | bytes 5242880 | tf_op jit(solution)/shard_map/reduce_scatter | solution.py:186
  769.5 156.5 %reduce-scatter.21.cloned.1.call-start = ((), (), s32[]{:S(2)}) async-start(), calls=%async_computation.25 | async-start | bytes 5242880 | tf_op jit(solution)/shard_map/reduce_scatter | solution.py:186
  778.0 197.9 %all-gather.35.cloned.1.call-start = ((), (), s32[]{:S(2)}) async-start(), calls=%async_computation.28 | async-start | bytes 2621440 | tf_op jit(solution)/shard_map/all_gather | solution.py:183
  846.4 79.6 %copy-start.38 = (f32[512,512]{1,0:T(8,128)S(1)}, f32[512,512]{1,0:T(8,128)}, u32[]{:S(2)}) copy-start(f32[512,512]{1,0:T(8,128)} %reduce-scatter.23.cloned.1.call-done) | copy-start | bytes 3145732
  929.3 343.1 %reduce-scatter.37.cloned.1.call-start = ((), (), s32[]{:S(2)}) async-start(), calls=%async_computation.35 | async-start | bytes 6340608 | tf_op jit(solution)/shard_map/reduce_scatter | solution.py:427
  937.0 337.8 %reduce-scatter.39.cloned.1.call-start = ((), (), s32[]{:S(2)}) async-start(), calls=%async_computation.36 | async-start | bytes 6340608 | tf_op jit(solution)/shard_map/reduce_scatter | solution.py:430
  944.8 332.3 %reduce-scatter.41.cloned.1.call-start = ((), (), s32[]{:S(2)}) async-start(), calls=%async_computation.37 | async-start | bytes 6340608 | tf_op jit(solution)/shard_map/reduce_scatter | solution.py:433
  952.5 327.0 %reduce-scatter.45.cloned.1.call-start = ((), (), s32[]{:S(2)}) async-start(), calls=%async_computation.39 | async-start | bytes 589824
  1215.6 70.3 %reduce-scatter.43.cloned.1.call-start = ((), (), s32[]{:S(2)}) async-start(), calls=%async_computation.38 | async-start | bytes 589824
  1217.1 113.7 %reduce-scatter.29.cloned.1.call-start = ((), (), s32[]{:S(2)}) async-start(), calls=%async_computation.31 | async-start | bytes 2359296 | tf_op jit(solution)/shard_map/reduce_scatter | solution.py:409
  1222.9 152.4 %reduce-scatter.27.cloned.1.call-start = ((), (), s32[]{:S(2)}) async-start(), calls=%async_computation.30 | async-start | bytes 2359296 | tf_op jit(solution)/shard_map/reduce_scatter | solution.py:406
  1229.6 200.7 %reduce-scatter.35.cloned.1.call-start = ((), (), s32[]{:S(2)}) async-start(), calls=%async_computation.34 | async-start | bytes 4718592 | tf_op jit(solution)/shard_map/reduce_scatter | solution.py:424
  1236.9 248.0 %reduce-scatter.31.cloned.1.call-start = ((), (), s32[]{:S(2)}) async-start(), calls=%async_computation.32 | async-start | bytes 4718592 | tf_op jit(solution)/shard_map/reduce_scatter | solution.py:412
  1252.3 287.7 %reduce-scatter.33.cloned.1.call-start = ((), (), s32[]{:S(2)}) async-start(), calls=%async_computation.33 | async-start | bytes 4718592 | tf_op jit(solution)/shard_map/reduce_scatter | solution.py:415
  1258.0 360.9 %reduce-scatter.25.cloned.1.call-start = ((), (), s32[]{:S(2)}) async-start(), calls=%async_computation.29 | async-start | bytes 5242880 | tf_op jit(solution)/shard_map/reduce_scatter | solution.py:186
  1377.1 241.9 %copy-start.27 = (bf16[512,512]{1,0:T(8,128)(2,1)S(1)}, bf16[512,512]{1,0:T(8,128)(2,1)}, u32[]{:S(2)}) copy-start(bf16[512,512]{1,0:T(8,128)(2,1)} %param.25) | copy-start | bytes 1572868
  1377.1 241.9 %copy-start.80 = (f32[512]{0:T(512)S(1)}, f32[512]{0:T(512)}, u32[]{:S(2)}) copy-start(f32[512]{0:T(512)} %copy-done.79) | copy-start | bytes 6148
  1377.1 241.9 %copy-start.83 = (f32[512]{0:T(512)S(1)}, f32[512]{0:T(512)}, u32[]{:S(2)}) copy-start(f32[512]{0:T(512)} %param.27) | copy-start | bytes 6148
  1432.4 222.7 %copy-start.40 = (f32[512,512]{1,0:T(8,128)S(1)}, f32[512,512]{1,0:T(8,128)}, u32[]{:S(2)}) copy-start(f32[512,512]{1,0:T(8,128)} %get-tuple-element.1014) | copy-start | bytes 3145732
  (98 other events, 689.5 us)
Sparse Core Ops, SparseCore 0:
  24.2 44.1 all-gather.12
  70.3 26.6 all-gather.18
  98.9 27.8 all-gather.14
  128.6 36.7 all-gather.16
  167.1 37.6 all-gather.20
  206.5 38.5 all-gather.22
  439.5 76.7 reduce-scatter.18
  518.3 44.2 all-gather.26
  564.9 45.9 all-gather.24
  612.7 42.4 all-gather.28
  656.9 45.9 all-gather.32
  704.8 42.4 all-gather.30
  769.6 76.7 reduce-scatter.22
  848.5 77.3 reduce-scatter.20
  929.4 46.3 all-gather.34
  979.6 57.1 reduce-scatter.36
  1040.5 58.4 reduce-scatter.38
  1102.7 58.4 reduce-scatter.40
  1215.7 33.0 reduce-scatter.44
  1251.7 34.0 reduce-scatter.42
  1289.5 41.2 reduce-scatter.28
  1334.0 41.1 reduce-scatter.26
  1379.0 51.3 reduce-scatter.34
  1433.6 51.2 reduce-scatter.30
  1488.6 51.3 reduce-scatter.32
  1542.2 76.7 reduce-scatter.24
where the time goes:
time: 1670 us; the launch traced here: 1660 us
  waiting for transfers between devices  835 us (50%)
  matrix products  355 us (21%)
  other arithmetic  286 us (17%)
  blocking collectives  87.7 us (5%)
  local copies, waits for them, and re-layouts  79.4 us (5%)
  between operations  16.7 us (1%)
    reduce_scatter x4, waiting for transfers between devices, total_cols(): lax.psum_scatter(partial_value, 'col', scatter_dimension=1, tiled=True)  288 us
    another operation x5, other arithmetic, delta_rule(): jax.scipy.linalg.solve_triangular(identity + lower_part, right_side, lowe...  160 us
    all_gather x4, waiting for transfers between devices, spread_cols(): return lax.all_gather(values, 'col', axis=1, tiled=True)  132 us
    reduce_scatter x1, waiting for transfers between devices, per_device(): lax.psum_scatter(out_grad.astype(jnp.bfloat16), 'row', scatter_dimension=...  53.3 us
    reduce_scatter x1, waiting for transfers between devices, per_device(): lax.psum_scatter(in_grads[3].astype(jnp.bfloat16), 'row', scatter_dimensi...  53 us
    reduce_scatter x1, waiting for transfers between devices, per_device(): lax.psum_scatter(in_grads[2].astype(jnp.bfloat16), 'row', scatter_dimensi...  52.5 us
    dot_general x24, matrix products, advance(): jnp.einsum('hld,hdv->hlv', query_now, state, precision=HIGH)  50.6 us
    dot_general x24, matrix products, advance(): jnp.einsum('hij,hjv->hiv', score_now, written, precision=HIGH)  49.8 us
  transfers between devices with their start and end apart: 26, of which 19 were waited for; matrix products, arithmetic and copies ran while one was open for 40% of the time, Pallas kernels for 0%

commit v1 on v0

v1 whole, which is shorter than its diff:
```python
import functools
import jax
import jax.numpy as jnp
from jax import lax
from jax.experimental import pallas as pl
from jax.experimental.pallas import tpu as pltpu
from jax.sharding import PartitionSpec as P

BF = jnp.bfloat16
F32 = jnp.float32
BLOCK = 128
VMEM = 56 * 1024 * 1024


def dot(left, right, lc=1, rc=0):
    return lax.dot_general(left, right, (((lc,), (rc,)), ((), ())), preferred_element_type=F32)


def split(x):
    high = x.astype(BF)
    return high, (x - high.astype(F32)).astype(BF)


def dot3(left, right, lc=1, rc=0):
    return (
        dot(left[0], right[0], lc, rc) + dot(left[0], right[1], lc, rc) + dot(left[1], right[0], lc, rc)
    )


def dotx(left, right, lc=1, rc=0):
    first = right.astype(BF)
    rest = right - first.astype(F32)
    second = rest.astype(BF)
    third = (rest - second.astype(F32)).astype(BF)
    return dot(left, first, lc, rc) + dot(left, second, lc, rc) + dot(left, third, lc, rc)


def sigmoid(x):
    return 0.5 + 0.5 * jnp.tanh(0.5 * x)


def lane_pick(block, lane):
    index = lax.broadcasted_iota(jnp.int32, block.shape, 1)
    return jnp.sum(jnp.where(index == lane, block, 0.0), axis=1, keepdims=True)


def row_pick(block, row):
    index = lax.broadcasted_iota(jnp.int32, block.shape, 0)
    return jnp.sum(jnp.where(index == row, block, 0.0), axis=0, keepdims=True)


def softplus(x):
    return jnp.maximum(x, 0.0) + jnp.log1p(jnp.exp(-jnp.abs(x)))


def conv_act(x, taps, marks):
    total = x * taps[3:4]
    for shift in (1, 2, 3):
        total = total + (marks[:, shift - 1 : shift] * pltpu.roll(x, shift, 0)) * taps[3 - shift : 4 - shift]
    gate = sigmoid(total)
    return total, gate


def grids():
    rows = lax.broadcasted_iota(jnp.int32, (BLOCK, BLOCK), 0)
    cols = lax.broadcasted_iota(jnp.int32, (BLOCK, BLOCK), 1)
    return rows, cols


def decays(small, params, head, heads):
    rate = jnp.exp(params[0:1])
    log_decay = -rate * softplus(small + params[1:2])
    beta = sigmoid(lane_pick(small, heads + head))
    return log_decay, beta


def block_decay(log_decay, head, rows, cols, seg_col, seg_row, last_seg):
    lower = (rows >= cols).astype(BF)
    running = dotx(lower, log_decay)
    column = lane_pick(running, head)
    line = row_pick(running.T, head)
    same = (seg_col == seg_row) & (rows >= cols)
    decay = jnp.where(same, jnp.exp(jnp.minimum(column - line, 0.0)), 0.0)
    carried = None
    if last_seg is not None:
        carried = jnp.where(seg_col == last_seg, jnp.exp(column), 0.0)
    return decay, carried


def unit_inverse(lower, rows, cols):
    identity = (rows == cols).astype(F32)
    base = 16
    near = jnp.where((rows // base) == (cols // base), -lower, 0.0)
    power = split(near)
    total = identity + near
    width = 2
    while width < base:
        power = split(dot3(power, power))
        total = total + dot3(split(total), power)
        width *= 2
    while base < BLOCK:
        pair = (rows // (2 * base) == cols // (2 * base)) & (rows // base != cols // base)
        off = split(jnp.where(pair, lower, 0.0))
        parts = split(total)
        total = total - dot3(parts, split(dot3(off, parts)))
        base *= 2
    return total


def heads_inputs(pre, taps, marks, dk):
    total, gate = conv_act(pre[:, : taps.shape[1]], taps, marks)
    act = total * gate
    query_act, key_act, values = act[:, :dk], act[:, dk : 2 * dk], act[:, 2 * dk :]
    query_scale = lax.rsqrt(jnp.sum(query_act * query_act, axis=1, keepdims=True) + 1e-06)
    key_scale = lax.rsqrt(jnp.sum(key_act * key_act, axis=1, keepdims=True) + 1e-06)
    return total, gate, query_act, key_act, values, query_scale, key_scale


def forward_kernel(heads, dk, dv, pre_ref, small_ref, taps_ref, marks_ref, segs_ref, params_ref, gain_ref,
                   mixed_ref, out_ref, fresh_ref, mats_ref, states_ref):
    head = pl.program_id(0)
    marks = marks_ref[...]
    pre = pre_ref[...]
    tokens = pre.shape[0]
    _, _, query_act, key_act, values, query_scale, key_scale = heads_inputs(pre, taps_ref[...], marks, dk)
    queries = query_act * (query_scale * dk ** -0.5)
    keys = key_act * key_scale
    log_decay, beta = decays(small_ref[...], params_ref[...], head, heads)
    rows, cols = grids()
    state = None
    for index in range(tokens // BLOCK):
        at = slice(index * BLOCK, (index + 1) * BLOCK)
        seg_col, seg_row = marks[at, 6:7], segs_ref[0:1, at]
        last_seg = marks[index * BLOCK - 1 : index * BLOCK, 6:7] if index else None
        decay, carried = block_decay(log_decay[at], head, rows, cols, seg_col, seg_row, last_seg)
        key, query, value, strength = keys[at], queries[at], values[at], beta[at]
        key_parts, query_parts = split(key), split(query)
        inner = jnp.where(rows > cols, dot3(key_parts, key_parts, 1, 1) * decay, 0.0)
        score = dot3(query_parts, key_parts, 1, 1) * decay
        inverse = unit_inverse(strength * inner, rows, cols)
        if index:
            state_parts = split(state)
            seen = dot3(key_parts, state_parts)
            asked = dot3(query_parts, state_parts)
            source = strength * (value - carried * seen)
        else:
            source = strength * value
        fresh = dot3(split(inverse), split(source))
        fresh_parts = split(fresh)
        output = dot3(split(score), fresh_parts)
        if index:
            output = output + carried * asked
        if index + 1 < tokens // BLOCK:
            tail = lane_pick_row(decay)
            grown = dot3(split(key * tail), fresh_parts, 0, 0)
            state = grown if state is None else carried[BLOCK - 1 : BLOCK] * state + grown
            states_ref[index * dk : (index + 1) * dk, :] = state
        fresh_ref[at, :] = fresh
        mats_ref[at, 0:BLOCK] = inner
        mats_ref[at, BLOCK : 2 * BLOCK] = score
        mats_ref[at, 2 * BLOCK :] = inverse
        out_ref[at, :] = output
        scale = lax.rsqrt(jnp.mean(output * output, axis=1, keepdims=True) + 1e-05)
        gate_pre = pre[at, 2 * dk + dv :]
        mixed_ref[at, :] = (output * scale * gain_ref[0:1] * (gate_pre * sigmoid(gate_pre))).astype(BF)


def lane_pick_row(decay):
    return decay.T[:, BLOCK - 1 : BLOCK]


def backward_kernel(heads, dk, dv, pre_ref, small_ref, taps_ref, marks_ref, segs_ref, params_ref, gain_ref,
                    grad_ref, out_ref, fresh_ref, mats_ref, states_ref,
                    low_ref, low_small_ref, taps_grad_ref, params_grad_ref, gain_grad_ref):
    head = pl.program_id(0)

    @pl.when(head == 0)
    def _():
        low_small_ref[...] = jnp.zeros_like(low_small_ref)
        params_grad_ref[...] = jnp.zeros_like(params_grad_ref)
        gain_grad_ref[...] = jnp.zeros_like(gain_grad_ref)

    marks = marks_ref[...]
    pre = pre_ref[...]
    taps = taps_ref[...]
    tokens = pre.shape[0]
    total, gate, query_act, key_act, values, query_scale, key_scale = heads_inputs(pre, taps, marks, dk)
    queries = query_act * (query_scale * dk ** -0.5)
    keys = key_act * key_scale
    small = small_ref[...]
    params = params_ref[...]
    log_decay, beta = decays(small, params, head, heads)
    rows, cols = grids()
    gain = gain_ref[0:1]
    blocks = tokens // BLOCK
    upper = (rows <= cols).astype(BF)
    d_state = None
    d_query, d_key, d_value, d_beta, d_decay = [None] * blocks, [None] * blocks, [None] * blocks, [None] * blocks, [None] * blocks
    d_gain = jnp.zeros((1, dv), F32)
    for index in reversed(range(blocks)):
        at = slice(index * BLOCK, (index + 1) * BLOCK)
        grad = grad_ref[at, :]
        output = out_ref[at, :]
        gate_pre = pre[at, 2 * dk + dv :]
        gate_sig = sigmoid(gate_pre)
        gate_act = gate_pre * gate_sig
        scale = lax.rsqrt(jnp.mean(output * output, axis=1, keepdims=True) + 1e-05)
        normed = output * scale
        both = grad * normed
        d_gain = d_gain + jnp.sum(both * gate_act, axis=0, keepdims=True)
        low_ref[at, 2 * dk + dv :] = (
            both * gain * (gate_sig + gate_act * (1.0 - gate_sig))
        ).astype(BF)
        pulled = grad * gate_act * gain
        d_out = scale * (pulled - normed * jnp.mean(pulled * normed, axis=1, keepdims=True))

        seg_col, seg_row = marks[at, 6:7], segs_ref[0:1, at]
        last_seg = marks[index * BLOCK - 1 : index * BLOCK, 6:7] if index else None
        decay, carried = block_decay(log_decay[at], head, rows, cols, seg_col, seg_row, last_seg)
        key, query, value, strength = keys[at], queries[at], values[at], beta[at]
        inner, score, inverse = mats_ref[at, 0:BLOCK], mats_ref[at, BLOCK : 2 * BLOCK], mats_ref[at, 2 * BLOCK :]
        fresh_parts = split(fresh_ref[at, :])
        key_parts, query_parts = split(key), split(query)
        out_parts = split(d_out)
        d_fresh = dot3(split(score), out_parts, 0, 0)
        if d_state is not None:
            tail = lane_pick_row(decay)
            state_grad_parts = split(d_state)
            d_fresh = d_fresh + dot3(split(key * tail), state_grad_parts)
        d_source = dot3(split(inverse), split(d_fresh), 0, 0)
        source_parts = split(d_source)
        d_score = dot3(out_parts, fresh_parts, 1, 1)
        d_lower = jnp.where(rows > cols, -dot3(source_parts, fresh_parts, 1, 1), 0.0)
        d_value[index] = strength * d_source
        d_strength = jnp.sum(d_source * value, axis=1, keepdims=True) + jnp.sum(d_lower * inner, axis=1, keepdims=True)
        change = d_score * score + d_lower * (strength * inner)
        d_run = jnp.sum(change, axis=1, keepdims=True) - jnp.sum(change.T, axis=1, keepdims=True)
        d_scores = split(d_score * decay)
        d_inners = split(d_lower * (strength * decay))
        dq = dot3(d_scores, key_parts)
        dk_ = dot3(d_inners, key_parts) + dot3(d_inners, key_parts, 0, 0) + dot3(d_scores, query_parts, 0, 0)
        last_extra = None
        if d_state is not None:
            moved = dot3(fresh_parts, state_grad_parts, 1, 1)
            dk_ = dk_ + tail * moved
            d_tail = jnp.sum(key * moved, axis=1, keepdims=True) * tail
            d_run = d_run - d_tail
            last_extra = jnp.sum(d_tail, axis=0, keepdims=True)
        if index:
            state = states_ref[(index - 1) * dk : index * dk, :]
            state_parts = split(state)
            out_back = dot3(out_parts, state_parts, 1, 1)
            source_back = dot3(source_parts, state_parts, 1, 1)
            key_source = jnp.sum(key * source_back, axis=1, keepdims=True)
            d_carried = jnp.sum(query * out_back, axis=1, keepdims=True) - strength * key_source
            d_strength = d_strength - carried * key_source
            dq = dq + carried * out_back
            dk_ = dk_ - (strength * carried) * source_back
            d_run = d_run + d_carried * carried
            keep = carried[BLOCK - 1 : BLOCK]
            new_state = dot3(query_parts, split(carried * d_out), 0, 0) - dot3(
                key_parts, split((strength * carried) * d_source), 0, 0
            )
            if d_state is not None:
                kept = jnp.sum(jnp.sum(state * d_state, axis=1, keepdims=True), axis=0, keepdims=True)
                last_extra = last_extra + kept * keep
                new_state = new_state + keep * d_state
            d_state = new_state
        if last_extra is not None:
            at_last = lax.broadcasted_iota(jnp.int32, (BLOCK, 1), 0) == BLOCK - 1
            d_run = d_run + jnp.where(at_last, last_extra, 0.0)
        d_decay[index] = dotx(upper, jnp.broadcast_to(d_run, (BLOCK, BLOCK)))[:, 0:1]
        d_query[index], d_key[index], d_beta[index] = dq, dk_, d_strength

    dq = jnp.concatenate(d_query, axis=0) * dk ** -0.5
    dk_ = jnp.concatenate(d_key, axis=0)
    dv_ = jnp.concatenate(d_value, axis=0)
    query_pull = jnp.sum(dq * query_act, axis=1, keepdims=True)
    key_pull = jnp.sum(dk_ * key_act, axis=1, keepdims=True)
    d_query_act = query_scale * (dq - query_act * (query_scale * query_scale * query_pull))
    d_key_act = key_scale * (dk_ - key_act * (key_scale * key_scale * key_pull))
    d_act = jnp.concatenate([d_query_act, d_key_act, dv_], axis=1)
    d_total = d_act * (gate * (1.0 + total * (1.0 - gate)))
    x = pre[:, : taps.shape[1]]
    d_pre = d_total * taps[3:4]
    taps_grad_ref[3:4, :] = jnp.sum(d_total * x, axis=0, keepdims=True)
    for shift in (1, 2, 3):
        moved = marks[:, 2 + shift : 3 + shift] * pltpu.roll(d_total, tokens - shift, 0)
        d_pre = d_pre + moved * taps[3 - shift : 4 - shift]
        taps_grad_ref[3 - shift : 4 - shift, :] = jnp.sum(moved * x, axis=0, keepdims=True)
    low_ref[:, : taps.shape[1]] = d_pre.astype(BF)

    d_log = jnp.concatenate(d_decay, axis=0)
    d_str = jnp.concatenate(d_beta, axis=0)
    lane = lax.broadcasted_iota(jnp.int32, small.shape, 1)
    rate = jnp.exp(params[0:1])
    d_decay_pre = jnp.where(lane == head, d_log * (-rate) * sigmoid(small + params[1:2]), 0.0)
    d_beta_pre = jnp.where(lane == heads + head, d_str * beta * (1.0 - beta), 0.0)
    low_small_ref[...] += (d_decay_pre + d_beta_pre).astype(BF)
    params_grad_ref[0:1, :] += jnp.sum(jnp.where(lane == head, d_log * log_decay, 0.0), axis=0, keepdims=True)
    params_grad_ref[1:2, :] += jnp.sum(d_decay_pre, axis=0, keepdims=True)
    gain_grad_ref[0:1, :] += d_gain


def mixer_specs(tokens, heads, dk, dv):
    wide = 2 * dk + 2 * dv
    taps = 2 * dk + dv
    return [
        pl.BlockSpec((tokens, wide), lambda h: (0, h)),
        pl.BlockSpec((tokens, 128), lambda h: (0, heads * wide // 128)),
        pl.BlockSpec((4, taps), lambda h: (0, h)),
        pl.BlockSpec((tokens, 8), lambda h: (0, 0)),
        pl.BlockSpec((8, tokens), lambda h: (0, 0)),
        pl.BlockSpec((8, 128), lambda h: (0, 0)),
        pl.BlockSpec((8, dv), lambda h: (0, 0)),
    ]


def saved_specs(tokens, dk, dv):
    blocks = tokens // BLOCK
    return [
        pl.BlockSpec((tokens, dv), lambda h: (0, h)),
        pl.BlockSpec((tokens, dv), lambda h: (0, h)),
        pl.BlockSpec((tokens, 3 * BLOCK), lambda h: (0, h)),
        pl.BlockSpec(((blocks - 1) * dk, dv), lambda h: (0, h)),
    ]


def mixer_forward(tokens, heads, dk, dv, operands):
    blocks = tokens // BLOCK
    return pl.pallas_call(
        functools.partial(forward_kernel, heads, dk, dv),
        grid=(heads,),
        in_specs=mixer_specs(tokens, heads, dk, dv),
        out_specs=[pl.BlockSpec((tokens, dv), lambda h: (0, h))] + saved_specs(tokens, dk, dv),
        out_shape=[
            jax.ShapeDtypeStruct((tokens, heads * dv), BF),
            jax.ShapeDtypeStruct((tokens, heads * dv), F32),
            jax.ShapeDtypeStruct((tokens, heads * dv), F32),
            jax.ShapeDtypeStruct((tokens, heads * 3 * BLOCK), F32),
            jax.ShapeDtypeStruct(((blocks - 1) * dk, heads * dv), F32),
        ],
        compiler_params=pltpu.CompilerParams(vmem_limit_bytes=VMEM),
        name="mixer_forward",
    )(*operands)


def mixer_backward(tokens, heads, dk, dv, operands, grad, saved):
    wide = 2 * dk + 2 * dv
    taps = 2 * dk + dv
    return pl.pallas_call(
        functools.partial(backward_kernel, heads, dk, dv),
        grid=(heads,),
        in_specs=mixer_specs(tokens, heads, dk, dv)
        + [pl.BlockSpec((tokens, dv), lambda h: (0, h))]
        + saved_specs(tokens, dk, dv),
        out_specs=[
            pl.BlockSpec((tokens, wide), lambda h: (0, h)),
            pl.BlockSpec((tokens, 128), lambda h: (0, 0)),
            pl.BlockSpec((4, taps), lambda h: (0, h)),
            pl.BlockSpec((8, 128), lambda h: (0, 0)),
            pl.BlockSpec((8, dv), lambda h: (0, 0)),
        ],
        out_shape=[
            jax.ShapeDtypeStruct((tokens, heads * wide), BF),
            jax.ShapeDtypeStruct((tokens, 128), BF),
            jax.ShapeDtypeStruct((4, heads * taps), F32),
            jax.ShapeDtypeStruct((8, 128), F32),
            jax.ShapeDtypeStruct((8, dv), F32),
        ],
        compiler_params=pltpu.CompilerParams(vmem_limit_bytes=VMEM),
        name="mixer_backward",
    )(*operands, grad, *saved)


def wide_dot(left, right):
    return jnp.dot(left, right, preferred_element_type=F32)


def contract_tokens(left, right):
    return dot(left, right, 0, 0)


def contract_features(left, right):
    return dot(left, right, 1, 1)


def hop(values, step, size):
    return lax.ppermute(values, "col", [(at, (at + step) % size) for at in range(size)])


def gather_cols(values, place, size):
    width = values.shape[1]
    whole = jnp.zeros((values.shape[0], size * width), values.dtype)
    whole = lax.dynamic_update_slice(whole, values, (0, place * width))
    for step in range(1, size):
        origin = (place + size - step) % size
        whole = lax.dynamic_update_slice(whole, hop(values, step, size), (0, origin * width))
    return whole


def scatter_cols(partial_sum, place, size):
    rows, width = partial_sum.shape[0], partial_sum.shape[1] // size
    total = lax.dynamic_slice(partial_sum, (0, place * width), (rows, width))
    for step in range(1, size):
        target = (place + step) % size
        block = lax.dynamic_slice(partial_sum, (0, target * width), (rows, width)).astype(BF)
        total = total + hop(block, step, size).astype(F32)
    return total


def total_cols(values, size):
    total = values
    for step in range(1, size):
        total = total + hop(values, step, size)
    return total


def by_head(arrays, heads):
    lead = arrays[0].shape[0]
    return jnp.concatenate([a.reshape(lead, heads, -1) for a in arrays], axis=2).reshape(lead, -1)


def per_device(
    inputs,
    segment_ids,
    norm_gain,
    query_weight,
    key_weight,
    value_weight,
    gate_weight,
    decay_weight,
    beta_weight,
    query_conv,
    key_conv,
    value_conv,
    decay_log,
    decay_bias,
    head_gain,
    out_weight,
    second_gain,
    hidden_gate,
    hidden_up,
    hidden_down,
    cotangent,
):
    tokens, width = inputs.shape
    size = lax.axis_size("col")
    place = lax.axis_index("col")
    model = size * width
    heads = decay_weight.shape[1]
    dk = query_weight.shape[1] // heads
    dv = value_weight.shape[1] // heads
    depth = query_weight.shape[0]
    hidden_units = hidden_gate.shape[1]
    wide = 2 * dk + 2 * dv

    in_weight = jnp.concatenate(
        [
            by_head([query_weight, key_weight, value_weight, gate_weight], heads),
            decay_weight,
            beta_weight,
            jnp.zeros((depth, 128 - 2 * heads), BF),
        ],
        axis=1,
    )
    in_all = lax.all_gather(in_weight, "row", axis=0, tiled=True)
    out_all = lax.all_gather(out_weight, "row", axis=1, tiled=True)
    mlp_all = lax.all_gather(jnp.concatenate([hidden_gate, hidden_up], axis=1), "row", axis=0, tiled=True)
    down_all = lax.all_gather(hidden_down, "row", axis=1, tiled=True)

    inputs_all = gather_cols(inputs, place, size)
    gains_all = gather_cols(jnp.stack([norm_gain, second_gain]), place, size)
    grad_all = gather_cols(cotangent, place, size)

    wide_all = inputs_all.astype(F32)
    first_scale = lax.rsqrt(jnp.mean(wide_all * wide_all, axis=1, keepdims=True) + 1e-05)
    hidden = (wide_all * first_scale * gains_all[0:1]).astype(BF)
    pre = wide_dot(hidden, in_all)

    times = jnp.arange(tokens)
    marks = [
        jnp.where((times >= shift) & (jnp.roll(segment_ids, shift) == segment_ids), 1.0, 0.0) for shift in (1, 2, 3)
    ]
    marks = marks + [jnp.roll(mark, -shift) for mark, shift in zip(marks, (1, 2, 3))]
    seg = segment_ids.astype(F32)
    marks = jnp.stack(marks + [seg, seg], axis=1)
    segs = jnp.broadcast_to(seg[None], (8, tokens))
    params = jnp.pad(jnp.stack([decay_log, decay_bias]), ((0, 6), (0, 128 - heads)))
    gain = jnp.broadcast_to(head_gain[None], (8, dv))
    taps = by_head([query_conv, key_conv, value_conv], heads)
    operands = (pre, pre, taps, marks, segs, params, gain)
    mixed, *saved = mixer_forward(tokens, heads, dk, dv, operands)

    wide_inputs = inputs.astype(F32)
    residual = wide_inputs + scatter_cols(wide_dot(mixed, out_all), place, size)
    residual_all = gather_cols(residual.astype(BF), place, size).astype(F32)
    second_scale = lax.rsqrt(jnp.mean(residual_all * residual_all, axis=1, keepdims=True) + 1e-05)
    second = (residual_all * second_scale * gains_all[1:2]).astype(BF)
    both = wide_dot(second, mlp_all)
    gate_value, up_value = both[:, :hidden_units], both[:, hidden_units:]
    gate_sig = jax.nn.sigmoid(gate_value)
    gate_act = gate_value * gate_sig
    product = (gate_act * up_value).astype(BF)
    grad_product = contract_features(grad_all, down_all)
    grad_both = jnp.concatenate(
        [grad_product * up_value * (gate_sig * (1.0 + gate_value * (1.0 - gate_sig))), grad_product * gate_act], axis=1
    ).astype(BF)
    second_part = contract_features(grad_both, mlp_all)
    second_inner = total_cols(jnp.sum(second_part * gains_all[1:2] * residual_all, axis=1), size)[:, None]
    grad_second = scatter_cols(second_part, place, size)
    grad_residual = (
        cotangent.astype(F32)
        + second_scale * second_gain * grad_second
        - residual * (second_scale * second_scale * second_scale * second_inner / model)
    )
    second_gain_part = jnp.sum(grad_second * residual * second_scale, axis=0)
    residual_rows = gather_cols(grad_residual.astype(BF), place, size)
    grad_mixed = contract_features(residual_rows, out_all)
    low, low_small, taps_part, params_part, gain_part = mixer_backward(
        tokens, heads, dk, dv, operands, grad_mixed, saved
    )
    low_all = jnp.concatenate([low, low_small], axis=1)
    in_part = contract_tokens(hidden, low_all).astype(BF)
    hidden_part = contract_features(low_all, in_all)
    first_inner = total_cols(jnp.sum(hidden_part * gains_all[0:1] * wide_all, axis=1), size)[:, None]
    grad_hidden = scatter_cols(hidden_part, place, size)
    grad_inputs = (
        grad_residual
        + first_scale * norm_gain * grad_hidden
        - wide_inputs * (first_scale * first_scale * first_scale * first_inner / model)
    )
    first_gain_part = jnp.sum(grad_hidden * wide_inputs * first_scale, axis=0)

    result = residual + scatter_cols(wide_dot(product, down_all), place, size)
    down_part = contract_tokens(product, grad_all).astype(BF)
    mlp_part = contract_tokens(second, grad_both).astype(BF)
    out_part = contract_tokens(mixed, residual_rows).astype(BF)
    down_grad = lax.psum_scatter(down_part, "row", scatter_dimension=1, tiled=True).astype(F32)
    mlp_grad = lax.psum_scatter(mlp_part, "row", scatter_dimension=0, tiled=True).astype(F32)
    out_grad = lax.psum_scatter(out_part, "row", scatter_dimension=1, tiled=True).astype(F32)
    in_grad = lax.psum_scatter(in_part, "row", scatter_dimension=0, tiled=True).astype(F32)

    taps_grad, params_grad, second_gain_grad = lax.psum(
        (taps_part, params_part[0:2, :heads], second_gain_part), "row"
    )
    gain_grad = lax.psum(gain_part[0], ("row", "col"))
    norm_gain_grad = lax.psum(first_gain_part, "row")

    head_grads = in_grad[:, : heads * wide].reshape(depth, heads, wide)
    tap_grads = taps_grad.reshape(4, heads, 2 * dk + dv)
    return (
        result,
        grad_inputs,
        norm_gain_grad,
        head_grads[:, :, :dk].reshape(depth, -1),
        head_grads[:, :, dk : 2 * dk].reshape(depth, -1),
        head_grads[:, :, 2 * dk : 2 * dk + dv].reshape(depth, -1),
        head_grads[:, :, 2 * dk + dv :].reshape(depth, -1),
        in_grad[:, heads * wide : heads * wide + heads],
        in_grad[:, heads * wide + heads : heads * wide + 2 * heads],
        tap_grads[:, :, :dk].reshape(4, -1),
        tap_grads[:, :, dk : 2 * dk].reshape(4, -1),
        tap_grads[:, :, 2 * dk :].reshape(4, -1),
        params_grad[0],
        params_grad[1],
        gain_grad,
        out_grad,
        second_gain_grad,
        mlp_grad[:, :hidden_units],
        mlp_grad[:, hidden_units:],
        down_grad,
    )


ROW_COL = P("row", "col")
COL_ROW = P("col", "row")
PLACED = (
    ROW_COL, P("row"), P("col"),
    ROW_COL, ROW_COL, ROW_COL, ROW_COL, ROW_COL, ROW_COL,
    P(None, "col"), P(None, "col"), P(None, "col"),
    P("col"), P("col"), P(),
    COL_ROW, P("col"), ROW_COL, ROW_COL, COL_ROW, ROW_COL,
)
MADE = (
    ROW_COL, ROW_COL, P("col"),
    ROW_COL, ROW_COL, ROW_COL, ROW_COL, ROW_COL, ROW_COL,
    P(None, "col"), P(None, "col"), P(None, "col"),
    P("col"), P("col"), P(),
    COL_ROW, P("col"), ROW_COL, ROW_COL, COL_ROW,
)


def solution(mesh):
    return jax.shard_map(per_device, mesh=mesh, in_specs=PLACED, out_specs=MADE, check_vma=False)
```

time: 1670 us -> 755 us (0.45)
  waiting for transfers between devices: 835 us -> 307 us
  other arithmetic: 286 us -> 17.6 us
  matrix products: 355 us -> 103 us
  starting transfers between devices: 2.01 us -> 98.8 us
  Pallas kernels: 0 us -> 79.6 us
  local copies, waits for them, and re-layouts: 79.4 us -> 45 us
    reduce_scatter x12 -> x4, waiting for transfers between devices: 533 us -> 67 us  [the longest x1 67 us: per_device(): lax.psum_scatter(in_part, 'row', scatter_dimension=0, tiled=True)]
    all_gather x12 -> x4, waiting for transfers between devices: 292 us -> 20 us  [the longest x1 20 us: per_device(): in_all = lax.all_gather(in_weight, 'row', axis=0, tiled=True)]
    dot_general x133 -> x12, matrix products: 343 us -> 103 us  [the longest x8 67.6 us: dot(): lax.dot_general(left, right, (((lc,), (rc,)), ((), ())), preferred_elemen...]
    ppermute x0 -> x33, waiting for transfers between devices: none -> 219 us  [hop(): lax.ppermute(values, 'col', [(at, (at + step) % size) for at in range(siz...]
    another operation x9 -> x2, other arithmetic: 163 us -> 0.62 us  [the longest x1 0.6 us: per_device(): jnp.stack([decay_log, decay_bias])]
    ppermute x0 -> x33, starting transfers between devices: none -> 98.5 us  [hop(): lax.ppermute(values, 'col', [(at, (at + step) % size) for at in range(siz...]
    pallas_call x0 -> x2, Pallas kernels: none -> 79.6 us  [the longest x1 44.3 us: mixer_forward(): pl.pallas_call(functools.partial(forward_kernel, heads, dk, dv), grid=(he...]
    reduce_sum x37 -> x2, other arithmetic: 55 us -> 0.97 us  [the longest x1 0.48 us: per_device(): jnp.mean(wide_all * wide_all, axis=1, keepdims=True) + 1e-05]
  transfers between devices with their start and end apart: 26 -> 41, of which waited for: 19 -> 14; matrix products, arithmetic and copies ran while one was open for 40% -> 15% of each run, Pallas kernels for 0% -> 11%
where the time goes in v1:
time: 755 us; the launch traced here: 751 us
  waiting for transfers between devices  307 us (41%)
  matrix products  103 us (14%)
  starting transfers between devices  98.8 us (13%)
  blocking collectives  84.5 us (11%)
  Pallas kernels  79.6 us (11%)
  local copies, waits for them, and re-layouts  45 us (6%)
  other arithmetic  17.6 us (2%)
  between operations  15.3 us (2%)
    ppermute x33, waiting for transfers between devices, hop(): lax.ppermute(values, 'col', [(at, (at + step) % size) for at in range(siz...  219 us
    ppermute x33, starting transfers between devices, hop(): lax.ppermute(values, 'col', [(at, (at + step) % size) for at in range(siz...  98.5 us
    dot_general x8, matrix products, dot(): lax.dot_general(left, right, (((lc,), (rc,)), ((), ())), preferred_elemen...  67.6 us
    reduce_scatter x1, waiting for transfers between devices, per_device(): lax.psum_scatter(in_part, 'row', scatter_dimension=0, tiled=True)  67 us
    psum x1, blocking collectives, per_device(): gain_grad = lax.psum(gain_part[0], ('row', 'col'))  60.3 us
    pallas_call x1, Pallas kernels, mixer_forward(): pl.pallas_call(functools.partial(forward_kernel, heads, dk, dv), grid=(he...  44.3 us
    pallas_call x1, Pallas kernels, mixer_backward(): pl.pallas_call(functools.partial(backward_kernel, heads, dk, dv), grid=(h...  35.4 us
    dot_general x4, matrix products, wide_dot(): return jnp.dot(left, right, preferred_element_type=F32)  34.9 us
  transfers between devices with their start and end apart: 41, of which 14 were waited for; matrix products, arithmetic and copies ran while one was open for 15% of the time, Pallas kernels for 11%

profile of v1, /device:TPU:0, one launch (start us, length us, event | category | flops | bytes accessed | tf_op | source)
XLA Modules:
  0.0 750.7 jit_solution(5701407822269003182)
XLA Ops:
  18.4 3.1 collective-permute-start
  21.4 2.6 collective-permute-start.1
  32.1 26.1 %collective-permute-done.3 = f32[2,512]{1,0:T(2,128)S(1)} collective-permute-done((f32[2,512]{1,0:T(2,128)S(1)}, f32[2,512]{1,0:T(2,128)S(1)}, u32[]{:S(2)}, u32[]{:S(2)}) %collective-permute-start.3) | collective-permute-done | bytes 4128 | tf_op jit(solution)/shard_map/ppermute | solution.py:389
  58.4 11.0 %collective-permute-done.4 = f32[2,512]{1,0:T(2,128)S(1)} collective-permute-done((f32[2,512]{1,0:T(2,128)S(1)}, f32[2,512]{1,0:T(2,128)S(1)}, u32[]{:S(2)}, u32[]{:S(2)}) %collective-permute-start.4) | collective-permute-done | bytes 4128 | tf_op jit(solution)/shard_map/ppermute | solution.py:389
  72.8 20.0 %all-gather.5.cloned.1.call-done = bf16[2048,3200]{1,0:T(8,128)(2,1)} async-done(((bf16[256,3200]{1,0:T(8,128)(2,1)}), bf16[2048,3200]{1,0:T(8,128)(2,1)}) %all-gather.5.cloned.1.call-update) | async-done | bytes 13107216 | tf_op jit(solution)/shard_map/all_gather | solution.py:467
  92.8 12.7 %fusion.17.pre_ref.small_ref = f32[512,3200]{1,0:T(8,128)} fusion(bf16[2048,3200]{1,0:T(8,128)(2,1)} %all-gather.5.cloned.1.call-done, bf16[512,2048]{1,0:T(8,128)(2,1)S(1)} %constant_dynamic-update-slice_fusion.16, f32[2048]{0:T(1024)S(1)} %bitcast.89, f32[512]{0:T(512)S(1)} %add_rsqrt_fusion.1), kind=kOutput, calls=%fused_computation.51 | convolution fusion | flops 6715080704 | bytes 21768192 | tf_op jit(solution)/shard_map/dot_general | solution.py:377
  106.7 44.3 %mixer_forward.1 = (bf16[512,1024]{1,0:T(8,128)(2,1)}, f32[512,1024]{1,0:T(8,128)}, f32[512,1024]{1,0:T(8,128)}, f32[512,1536]{1,0:T(8,128)}, f32[384,1024]{1,0:T(8,128)}) custom-call(f32[512,3200]{1,0:T(8,128)} %fusion.17.pre_ref.small_ref, f32[512,3200]{1,0:T(8,128)} %fusion.17.pre_ref.small_ref, f32[4,2048]{1,0:T(4,128)} %bitcast.73, ...), custom_call_target="tpu_custom_call" | custom-call | tf_op jit(solution)/shard_map/mixer_forward/pallas_call | solution.py:331
  151.0 4.8 fusion.36
  156.1 3.4 collective-permute-start.8
  160.6 2.4 collective-permute-start.15
  163.8 8.0 %collective-permute-done.8 = bf16[512,512]{1,0:T(8,128)(2,1)S(1)} collective-permute-done((bf16[512,512]{1,0:T(8,128)(2,1)S(1)}, bf16[512,512]{1,0:T(8,128)(2,1)S(1)}, u32[]{:S(2)}, u32[]{:S(2)}) %collective-permute-start.8) | collective-permute-done | bytes 524320 | tf_op jit(solution)/shard_map/ppermute | solution.py:389
  171.8 4.3 collective-permute-start.17
  176.1 51.9 %collective-permute-done.7 = bf16[512,512]{1,0:T(8,128)(2,1)S(1)} collective-permute-done((bf16[512,512]{1,0:T(8,128)(2,1)S(1)}, bf16[512,512]{1,0:T(8,128)(2,1)S(1)}, u32[]{:S(2)}, u32[]{:S(2)}) %collective-permute-start.7) | collective-permute-done | bytes 524320 | tf_op jit(solution)/shard_map/ppermute | solution.py:389
  229.6 3.8 collective-permute-start.11
  233.4 28.3 %collective-permute-done.16 = bf16[512,512]{1,0:T(8,128)(2,1)S(1)} collective-permute-done((bf16[512,512]{1,0:T(8,128)(2,1)S(1)}, bf16[512,512]{1,0:T(8,128)(2,1)S(1)}, u32[]{:S(2)}, u32[]{:S(2)}) %collective-permute-start.16) | collective-permute-done | bytes 524320 | tf_op jit(solution)/shard_map/ppermute | solution.py:389
  262.0 22.2 %collective-permute-done.10 = bf16[512,512]{1,0:T(8,128)(2,1)S(1)} collective-permute-done((bf16[512,512]{1,0:T(8,128)(2,1)S(1)}, bf16[512,512]{1,0:T(8,128)(2,1)S(1)}, u32[]{:S(2)}, u32[]{:S(2)}) %collective-permute-start.10) | collective-permute-done | bytes 524320 | tf_op jit(solution)/shard_map/ppermute | solution.py:389
  284.9 10.6 %fusion.14 = f32[512,2752]{0,1:T(8,128)} fusion(bf16[2048,2752]{0,1:T(8,128)(2,1)} %all-gather.9.cloned.1.call-done, bf16[512,2048]{1,0:T(8,128)(2,1)S(1)} %constant_dynamic-update-slice_fusion.8, f32[2048]{0:T(1024)S(1)} %bitcast.92, f32[512]{0:T(512)S(1)} %add_rsqrt_fusion), kind=kOutput, calls=%fused_computation.50 | convolution fusion | flops 5775556608 | bytes 19015680 | tf_op jit(solution)/shard_map/dot_general | solution.py:377
  295.5 10.5 %multiply_convert_fusion.1 = (bf16[512,1376]{0,1:T(8,128)(2,1)S(1)}, bf16[512,1376]{0,1:T(8,128)(2,1)S(1)}, bf16[512,1376]{0,1:T(8,128)(2,1)}) fusion(f32[512,2752]{0,1:T(8,128)} %fusion.14, bf16[512,2048]{1,0:T(8,128)(2,1)} %copy-done.11, bf16[1376,2048]{1,0:T(8,128)(2,1)} %all-gather.11.cloned.1.call-done), kind=kOutput, calls=%fused_computation.20 | convolution fusion | flops 2896248832 | bytes 17596416 | tf_op jit(solution)/shard_map/dot_general | solution.py:16
  306.0 6.7 fusion.7
  313.0 14.2 %collective-permute-start.20 = (bf16[512,512]{1,0:T(8,128)(2,1)S(1)}, bf16[512,512]{1,0:T(8,128)(2,1)S(1)}, u32[]{:S(2)}, u32[]{:S(2)}) collective-permute-start(bf16[512,512]{1,0:T(8,128)(2,1)S(1)} %get-tuple-element.119), channel_id=1, source_target_pairs={{0,3},{1,0},{2,1},{3,2},{4,7},{5,4},{6,5},{7,6},{8,11},{9,8},{10,9... | collective-permute-start | bytes 1572872 | tf_op jit(solution)/shard_map/ppermute | solution.py:389
  327.8 3.2 collective-permute-start.23
  332.1 28.4 %collective-permute-done.23 = f32[512]{0:T(512)S(1)} collective-permute-done((f32[512]{0:T(512)S(1)}, f32[512]{0:T(512)S(1)}, u32[]{:S(2)}, u32[]{:S(2)}) %collective-permute-start.23) | collective-permute-done | bytes 2080 | tf_op jit(solution)/shard_map/ppermute | solution.py:389
  360.5 10.9 %collective-permute-start.21 = (f32[512]{0:T(512)S(1)}, f32[512]{0:T(512)S(1)}, u32[]{:S(2)}, u32[]{:S(2)}) collective-permute-start(f32[512]{0:T(512)S(1)} %get-tuple-element.148), channel_id=1, source_target_pairs={{0,1},{1,2},{2,3},{3,0},{4,5},{5,6},{6,7},{7,4},{8,9},{9,10},{10,1... | collective-permute-start | bytes 6152 | tf_op jit(solution)/shard_map/ppermute | solution.py:389
  374.5 2.3 collective-permute-start.24
  379.5 11.9 %collective-permute-done.24 = bf16[512,512]{1,0:T(8,128)(2,1)S(1)} collective-permute-done((bf16[512,512]{1,0:T(8,128)(2,1)S(1)}, bf16[512,512]{1,0:T(8,128)(2,1)S(1)}, u32[]{:S(2)}, u32[]{:S(2)}) %collective-permute-start.24) | collective-permute-done | bytes 524320 | tf_op jit(solution)/shard_map/ppermute | solution.py:389
  391.4 19.2 %collective-permute-done.25 = bf16[512,512]{1,0:T(8,128)(2,1)S(1)} collective-permute-done((bf16[512,512]{1,0:T(8,128)(2,1)S(1)}, bf16[512,512]{1,0:T(8,128)(2,1)S(1)}, u32[]{:S(2)}, u32[]{:S(2)}) %collective-permute-start.25) | collective-permute-done | bytes 524320 | tf_op jit(solution)/shard_map/ppermute | solution.py:389
  412.1 4.4 convolution_convert_fusion.3
  416.6 7.6 %convolution_convert_fusion.2 = bf16[1376,2048]{1,0:T(8,128)(2,1)} fusion(bf16[512,1376]{0,1:T(8,128)(2,1)} %get-tuple-element.114, bf16[512,2048]{1,0:T(8,128)(2,1)} %copy-done.11), kind=kOutput, calls=%fused_computation.2 | convolution fusion | flops 2888499200 | bytes 9142272 | tf_op jit(solution)/shard_map/dot_general | solution.py:16
  424.3 10.7 %convolution_convert_fusion.1 = bf16[2048,2752]{0,1:T(8,128)(2,1)} fusion(bf16[512,1376]{0,1:T(8,128)(2,1)} %copy-done.41, bf16[512,1376]{0,1:T(8,128)(2,1)} %copy-done.40, bf16[512,2048]{1,0:T(8,128)(2,1)S(1)} %constant_dynamic-update-slice_fusion.8, f32[2048]{0:T(1024)S(1)} %bitcast.94, f32[512]{0:T(512)S(1)} %add_rsqrt_fusion), kind=kOutput, calls=%fused_computation.1 | convolution fusion | flops 5786828800 | bytes 16197632 | tf_op jit(solution)/shard_map/dot_general | solution.py:16
  436.9 6.3 fusion.38.grad_ref
  443.2 35.4 %mixer_backward.1 = (bf16[512,3072]{1,0:T(8,128)(2,1)}, bf16[512,128]{1,0:T(8,128)(2,1)}, f32[4,2048]{1,0:T(4,128)}, f32[8,128]{1,0:T(8,128)}, f32[8,256]{1,0:T(8,128)}) custom-call(f32[512,3200]{1,0:T(8,128)} %fusion.17.pre_ref.small_ref, f32[512,3200]{1,0:T(8,128)} %fusion.17.pre_ref.small_ref, f32[4,2048]{1,0:T(4,128)} %bitcast.74, ...), custom_call_target="tpu_custom_call" | custom-call | tf_op jit(solution)/shard_map/mixer_backward/pallas_call | solution.py:351
  478.6 2.2 constant_dynamic-update-slice_fusion.21
  482.6 10.9 %convolution_convert_fusion = bf16[2048,3200]{1,0:T(8,128)(2,1)} fusion(bf16[512,3200]{1,0:T(8,128)(2,1)S(1)} %constant_dynamic-update-slice_fusion.20, bf16[512,2048]{1,0:T(8,128)(2,1)S(1)} %copy-done.1, f32[2048]{0:T(1024)S(1)} %bitcast.90, f32[512]{0:T(512)S(1)} %add_rsqrt_fusion.1), kind=kOutput, calls=%fused_computation | convolution fusion | flops 6721634304 | bytes 18491392 | tf_op jit(solution)/shard_map/dot_general | solution.py:16
  493.5 6.7 fusion.37
  500.4 12.3 %collective-permute-start.14 = (bf16[512,512]{1,0:T(8,128)(2,1)S(1)}, bf16[512,512]{1,0:T(8,128)(2,1)S(1)}, u32[]{:S(2)}, u32[]{:S(2)}) collective-permute-start(bf16[512,512]{1,0:T(8,128)(2,1)S(1)} %get-tuple-element.122), channel_id=1, source_target_pairs={{0,3},{1,0},{2,1},{3,2},{4,7},{5,4},{6,5},{7,6},{8,11},{9,8},{10,9... | collective-permute-start | bytes 1572872 | tf_op jit(solution)/shard_map/ppermute | solution.py:389
  513.4 10.5 %fusion.3 = (f32[512]{0:T(512)S(1)}, f32[512,2048]{1,0:T(8,128)S(1)}) fusion(bf16[512,2048]{1,0:T(8,128)(2,1)S(1)} %copy-done.1, f32[2048]{0:T(1024)S(1)} %bitcast.91, bf16[512,3200]{1,0:T(8,128)(2,1)S(1)} %copy-done.8, bf16[2048,3200]{1,0:T(8,128)(2,1)} %all-gather.5.cloned.1.call-done), kind=kOutput, calls=%fused_computation.12 | convolution fusion | flops 6715080192 | bytes 22685696 | tf_op jit(solution)/shard_map/dot_general | solution.py:16
  523.9 3.5 collective-permute-start.32
  529.6 19.3 %collective-permute-start.30 = (f32[512]{0:T(512)S(1)}, f32[512]{0:T(512)S(1)}, u32[]{:S(2)}, u32[]{:S(2)}) collective-permute-start(f32[512]{0:T(512)S(1)} %get-tuple-element.150), channel_id=1, source_target_pairs={{0,1},{1,2},{2,3},{3,0},{4,5},{5,6},{6,7},{7,4},{8,9},{9,10},{10,1... | collective-permute-start | bytes 6152 | tf_op jit(solution)/shard_map/ppermute | solution.py:389
  548.9 10.0 %collective-permute-done.13 = bf16[512,512]{1,0:T(8,128)(2,1)S(1)} collective-permute-done((bf16[512,512]{1,0:T(8,128)(2,1)S(1)}, bf16[512,512]{1,0:T(8,128)(2,1)S(1)}, u32[]{:S(2)}, u32[]{:S(2)}) %collective-permute-start.13) | collective-permute-done | bytes 524320 | tf_op jit(solution)/shard_map/ppermute | solution.py:389
  561.0 2.9 multiply_reduce_fusion
  565.3 60.3 %psum.38 = f32[256]{0:T(256)} all-reduce(f32[256]{0:T(256)S(1)} %bitcast.95), channel_id=1, replica_groups=mesh['row'=8,'col'=4] {'row','col'}, use_global_device_ids=true, to_apply=%region_9.10 | all-reduce | flops 256 | bytes 2048 | tf_op jit(solution)/shard_map/psum | solution.py:547
  625.7 3.3 fusion.12
  629.0 24.2 %all-reduce.1 = (f32[512]{0:T(512)}, f32[4,4,512]{2,1,0:T(4,128)S(1)}, f32[2,4]{1,0:T(2,128)S(1)}, f32[512]{0:T(512)}) all-reduce(f32[512]{0:T(512)S(1)} %get-tuple-element.112, f32[4,4,512]{2,1,0:T(4,128)S(1)} %reshape.138, f32[2,4]{1,0:T(2,128)S(1)} %slice.136, f32[512]{0:T(512)S(1)} %get-tuple-element.135), channel_id=1, replica_groups=mesh['row'=8,'col'=4] {'row'}, use_global_device_ids=true, to_apply=%region_5.6 | all-reduce | flops 9224 | bytes 73792 | tf_op jit(solution)/shard_map/psum | solution.py:548
  657.1 2.3 convert_element_type.170
  659.4 3.1 fusion.34
  662.4 67.0 %reduce-scatter.5.cloned.1.call-done = bf16[256,3200]{1,0:T(8,128)(2,1)} async-done(((bf16[2048,3200]{1,0:T(8,128)(2,1)}), bf16[256,3200]{1,0:T(8,128)(2,1)}) %reduce-scatter.5.cloned.1.call-update) | async-done | bytes 1638416 | tf_op jit(solution)/shard_map/reduce_scatter | solution.py:542
  729.4 3.4 slice.146
  732.8 3.5 reshape.133
  (238 shorter events, 58.8 us)
Async XLA Ops:
  7.2 85.6 %all-gather.5.cloned.1.call-start = ((), (), s32[]{:S(2)}) async-start(), calls=%async_computation.4 | async-start | bytes 14745600 | tf_op jit(solution)/shard_map/all_gather | solution.py:467
  15.7 135.3 %all-gather.7.cloned.1.call-start = ((), (), s32[]{:S(2)}) async-start(), calls=%async_computation.5 | async-start | bytes 4718592 | tf_op jit(solution)/shard_map/all_gather | solution.py:468
  16.4 268.5 %all-gather.9.cloned.1.call-start = ((), (), s32[]{:S(2)}) async-start(), calls=%async_computation.6 | async-start | bytes 12681216 | tf_op jit(solution)/shard_map/all_gather | solution.py:469
  17.7 277.8 %all-gather.11.cloned.1.call-start = ((), (), s32[]{:S(2)}) async-start(), calls=%async_computation.7 | async-start | bytes 6340608 | tf_op jit(solution)/shard_map/all_gather | solution.py:470
  18.3 636.6 %reduce-scatter.7.cloned.1.call-start = ((), (), s32[]{:S(2)}) async-start(), calls=%async_computation.9 | async-start | bytes 4718592 | tf_op jit(solution)/shard_map/reduce_scatter | solution.py:541
  18.4 51.6 %collective-permute-start = (bf16[512,512]{1,0:T(8,128)(2,1)S(1)}, bf16[512,512]{1,0:T(8,128)(2,1)}, u32[]{:S(2)}, u32[]{:S(2)}) collective-permute-start(bf16[512,512]{1,0:T(8,128)(2,1)S(1)} %copy-done.2), channel_id=1, source_target_pairs={{0,1},{1,2},{2,3},{3,0},{4,5},{5,6},{6,7},{7,4},{8,9},{9,10},{10,1... | collective-permute-start | bytes 1572872 | tf_op jit(solution)/shard_map/ppermute | solution.py:389
  21.4 49.7 %collective-permute-start.1 = (bf16[512,512]{1,0:T(8,128)(2,1)S(1)}, bf16[512,512]{1,0:T(8,128)(2,1)}, u32[]{:S(2)}, u32[]{:S(2)}) collective-permute-start(bf16[512,512]{1,0:T(8,128)(2,1)S(1)} %copy-done.2), channel_id=1, source_target_pairs={{0,2},{1,3},{2,0},{3,1},{4,6},{5,7},{6,4},{7,5},{8,10},{9,11},{10,... | collective-permute-start | bytes 1572872 | tf_op jit(solution)/shard_map/ppermute | solution.py:389
  24.0 48.2 %collective-permute-start.2 = (bf16[512,512]{1,0:T(8,128)(2,1)S(1)}, bf16[512,512]{1,0:T(8,128)(2,1)S(1)}, u32[]{:S(2)}, u32[]{:S(2)}) collective-permute-start(bf16[512,512]{1,0:T(8,128)(2,1)S(1)} %copy-done.2), channel_id=1, source_target_pairs={{0,3},{1,0},{2,1},{3,2},{4,7},{5,4},{6,5},{7,6},{8,11},{9,8},{10,9... | collective-permute-start | bytes 1572872 | tf_op jit(solution)/shard_map/ppermute | solution.py:389
  25.4 32.8 %collective-permute-start.3 = (f32[2,512]{1,0:T(2,128)S(1)}, f32[2,512]{1,0:T(2,128)S(1)}, u32[]{:S(2)}, u32[]{:S(2)}) collective-permute-start(f32[2,512]{1,0:T(2,128)S(1)} %get-tuple-element.141), channel_id=1, source_target_pairs={{0,1},{1,2},{2,3},{3,0},{4,5},{5,6},{6,7},{7,4},{8,9},{9,10},{10,1... | collective-permute-start | bytes 12296 | tf_op jit(solution)/shard_map/ppermute | solution.py:389
  26.1 43.2 %collective-permute-start.4 = (f32[2,512]{1,0:T(2,128)S(1)}, f32[2,512]{1,0:T(2,128)S(1)}, u32[]{:S(2)}, u32[]{:S(2)}) collective-permute-start(f32[2,512]{1,0:T(2,128)S(1)} %get-tuple-element.141), channel_id=1, source_target_pairs={{0,2},{1,3},{2,0},{3,1},{4,6},{5,7},{6,4},{7,5},{8,10},{9,11},{10,... | collective-permute-start | bytes 12296 | tf_op jit(solution)/shard_map/ppermute | solution.py:389
  58.2 11.8 %collective-permute-start.5 = (f32[2,512]{1,0:T(2,128)S(1)}, f32[2,512]{1,0:T(2,128)S(1)}, u32[]{:S(2)}, u32[]{:S(2)}) collective-permute-start(f32[2,512]{1,0:T(2,128)S(1)} %get-tuple-element.141), channel_id=1, source_target_pairs={{0,3},{1,0},{2,1},{3,2},{4,7},{5,4},{6,5},{7,6},{8,11},{9,8},{10,9... | collective-permute-start | bytes 12296 | tf_op jit(solution)/shard_map/ppermute | solution.py:389
  155.8 72.4 %copy-start.3 = (bf16[512,512]{1,0:T(8,128)(2,1)S(1)}, bf16[512,512]{1,0:T(8,128)(2,1)}, u32[]{:S(2)}) copy-start(bf16[512,512]{1,0:T(8,128)(2,1)} %param.21) | copy-start | bytes 1572868
  156.1 15.7 %collective-permute-start.8 = (bf16[512,512]{1,0:T(8,128)(2,1)S(1)}, bf16[512,512]{1,0:T(8,128)(2,1)S(1)}, u32[]{:S(2)}, u32[]{:S(2)}) collective-permute-start(bf16[512,512]{1,0:T(8,128)(2,1)S(1)} %get-tuple-element.125), channel_id=1, source_target_pairs={{0,3},{1,0},{2,1},{3,2},{4,7},{5,4},{6,5},{7,6},{8,11},{9,8},{10,9... | collective-permute-start | bytes 1572872 | tf_op jit(solution)/shard_map/ppermute | solution.py:389
  159.5 68.6 %collective-permute-start.7 = (bf16[512,512]{1,0:T(8,128)(2,1)S(1)}, bf16[512,512]{1,0:T(8,128)(2,1)S(1)}, u32[]{:S(2)}, u32[]{:S(2)}) collective-permute-start(bf16[512,512]{1,0:T(8,128)(2,1)S(1)} %get-tuple-element.126), channel_id=1, source_target_pairs={{0,2},{1,3},{2,0},{3,1},{4,6},{5,7},{6,4},{7,5},{8,10},{9,11},{10,... | collective-permute-start | bytes 1572872 | tf_op jit(solution)/shard_map/ppermute | solution.py:389
  159.5 68.6 %collective-permute-start.6 = (bf16[512,512]{1,0:T(8,128)(2,1)S(1)}, bf16[512,512]{1,0:T(8,128)(2,1)S(1)}, u32[]{:S(2)}, u32[]{:S(2)}) collective-permute-start(bf16[512,512]{1,0:T(8,128)(2,1)S(1)} %get-tuple-element.124), channel_id=1, source_target_pairs={{0,1},{1,2},{2,3},{3,0},{4,5},{5,6},{6,7},{7,4},{8,9},{9,10},{10,1... | collective-permute-start | bytes 1572872 | tf_op jit(solution)/shard_map/ppermute | solution.py:389
  160.6 69.0 %collective-permute-start.15 = (bf16[512,512]{1,0:T(8,128)(2,1)S(1)}, bf16[512,512]{1,0:T(8,128)(2,1)S(1)}, u32[]{:S(2)}, u32[]{:S(2)}) collective-permute-start(bf16[512,512]{1,0:T(8,128)(2,1)S(1)} %copy-done.20), channel_id=1, source_target_pairs={{0,1},{1,2},{2,3},{3,0},{4,5},{5,6},{6,7},{7,4},{8,9},{9,10},{10,1... | collective-permute-start | bytes 1572872 | tf_op jit(solution)/shard_map/ppermute | solution.py:389
  162.9 98.8 %collective-permute-start.16 = (bf16[512,512]{1,0:T(8,128)(2,1)S(1)}, bf16[512,512]{1,0:T(8,128)(2,1)S(1)}, u32[]{:S(2)}, u32[]{:S(2)}) collective-permute-start(bf16[512,512]{1,0:T(8,128)(2,1)S(1)} %copy-done.20), channel_id=1, source_target_pairs={{0,2},{1,3},{2,0},{3,1},{4,6},{5,7},{6,4},{7,5},{8,10},{9,11},{10,... | collective-permute-start | bytes 1572872 | tf_op jit(solution)/shard_map/ppermute | solution.py:389
  171.8 90.0 %collective-permute-start.17 = (bf16[512,512]{1,0:T(8,128)(2,1)S(1)}, bf16[512,512]{1,0:T(8,128)(2,1)S(1)}, u32[]{:S(2)}, u32[]{:S(2)}) collective-permute-start(bf16[512,512]{1,0:T(8,128)(2,1)S(1)} %copy-done.20), channel_id=1, source_target_pairs={{0,3},{1,0},{2,1},{3,2},{4,7},{5,4},{6,5},{7,6},{8,11},{9,8},{10,9... | collective-permute-start | bytes 1572872 | tf_op jit(solution)/shard_map/ppermute | solution.py:389
  228.7 33.2 %collective-permute-start.9 = (bf16[512,512]{1,0:T(8,128)(2,1)S(1)}, bf16[512,512]{1,0:T(8,128)(2,1)S(1)}, u32[]{:S(2)}, u32[]{:S(2)}) collective-permute-start(bf16[512,512]{1,0:T(8,128)(2,1)S(1)} %get-tuple-element.108), channel_id=1, source_target_pairs={{0,1},{1,2},{2,3},{3,0},{4,5},{5,6},{6,7},{7,4},{8,9},{9,10},{10,1... | collective-permute-start | bytes 1572872 | tf_op jit(solution)/shard_map/ppermute | solution.py:389
  229.2 55.1 %collective-permute-start.10 = (bf16[512,512]{1,0:T(8,128)(2,1)S(1)}, bf16[512,512]{1,0:T(8,128)(2,1)S(1)}, u32[]{:S(2)}, u32[]{:S(2)}) collective-permute-start(bf16[512,512]{1,0:T(8,128)(2,1)S(1)} %get-tuple-element.108), channel_id=1, source_target_pairs={{0,2},{1,3},{2,0},{3,1},{4,6},{5,7},{6,4},{7,5},{8,10},{9,11},{10,... | collective-permute-start | bytes 1572872 | tf_op jit(solution)/shard_map/ppermute | solution.py:389
  229.6 54.7 %collective-permute-start.11 = (bf16[512,512]{1,0:T(8,128)(2,1)S(1)}, bf16[512,512]{1,0:T(8,128)(2,1)S(1)}, u32[]{:S(2)}, u32[]{:S(2)}) collective-permute-start(bf16[512,512]{1,0:T(8,128)(2,1)S(1)} %get-tuple-element.108), channel_id=1, source_target_pairs={{0,3},{1,0},{2,1},{3,2},{4,7},{5,4},{6,5},{7,6},{8,11},{9,8},{10,9... | collective-permute-start | bytes 1572872 | tf_op jit(solution)/shard_map/ppermute | solution.py:389
  312.7 61.8 %copy-start.6 = (f32[512,2048]{1,0:T(8,128)}, f32[512,2048]{1,0:T(8,128)S(1)}, u32[]{:S(2)}) copy-start(f32[512,2048]{1,0:T(8,128)S(1)} %get-tuple-element.149) | copy-start | bytes 12582916
  312.8 60.3 %copy-start.21 = (bf16[512,512]{1,0:T(8,128)(2,1)S(1)}, bf16[512,512]{1,0:T(8,128)(2,1)}, u32[]{:S(2)}) copy-start(bf16[512,512]{1,0:T(8,128)(2,1)} %param.41) | copy-start | bytes 1572868
  313.0 59.8 %collective-permute-start.20 = (bf16[512,512]{1,0:T(8,128)(2,1)S(1)}, bf16[512,512]{1,0:T(8,128)(2,1)S(1)}, u32[]{:S(2)}, u32[]{:S(2)}) collective-permute-start(bf16[512,512]{1,0:T(8,128)(2,1)S(1)} %get-tuple-element.119), channel_id=1, source_target_pairs={{0,3},{1,0},{2,1},{3,2},{4,7},{5,4},{6,5},{7,6},{8,11},{9,8},{10,9... | collective-permute-start | bytes 1572872 | tf_op jit(solution)/shard_map/ppermute | solution.py:389
  327.2 45.6 %collective-permute-start.19 = (bf16[512,512]{1,0:T(8,128)(2,1)S(1)}, bf16[512,512]{1,0:T(8,128)(2,1)S(1)}, u32[]{:S(2)}, u32[]{:S(2)}) collective-permute-start(bf16[512,512]{1,0:T(8,128)(2,1)S(1)} %get-tuple-element.120), channel_id=1, source_target_pairs={{0,2},{1,3},{2,0},{3,1},{4,6},{5,7},{6,4},{7,5},{8,10},{9,11},{10,... | collective-permute-start | bytes 1572872 | tf_op jit(solution)/shard_map/ppermute | solution.py:389
  327.2 45.6 %collective-permute-start.18 = (bf16[512,512]{1,0:T(8,128)(2,1)S(1)}, bf16[512,512]{1,0:T(8,128)(2,1)S(1)}, u32[]{:S(2)}, u32[]{:S(2)}) collective-permute-start(bf16[512,512]{1,0:T(8,128)(2,1)S(1)} %get-tuple-element.118), channel_id=1, source_target_pairs={{0,1},{1,2},{2,3},{3,0},{4,5},{5,6},{6,7},{7,4},{8,9},{9,10},{10,1... | collective-permute-start | bytes 1572872 | tf_op jit(solution)/shard_map/ppermute | solution.py:389
  327.8 32.7 %collective-permute-start.23 = (f32[512]{0:T(512)S(1)}, f32[512]{0:T(512)S(1)}, u32[]{:S(2)}, u32[]{:S(2)}) collective-permute-start(f32[512]{0:T(512)S(1)} %get-tuple-element.148), channel_id=1, source_target_pairs={{0,3},{1,0},{2,1},{3,2},{4,7},{5,4},{6,5},{7,6},{8,11},{9,8},{10,9... | collective-permute-start | bytes 6152 | tf_op jit(solution)/shard_map/ppermute | solution.py:389
  331.0 40.4 %collective-permute-start.22 = (f32[512]{0:T(512)S(1)}, f32[512]{0:T(512)S(1)}, u32[]{:S(2)}, u32[]{:S(2)}) collective-permute-start(f32[512]{0:T(512)S(1)} %get-tuple-element.148), channel_id=1, source_target_pairs={{0,2},{1,3},{2,0},{3,1},{4,6},{5,7},{6,4},{7,5},{8,10},{9,11},{10,... | collective-permute-start | bytes 6152 | tf_op jit(solution)/shard_map/ppermute | solution.py:389
  360.5 12.2 %collective-permute-start.21 = (f32[512]{0:T(512)S(1)}, f32[512]{0:T(512)S(1)}, u32[]{:S(2)}, u32[]{:S(2)}) collective-permute-start(f32[512]{0:T(512)S(1)} %get-tuple-element.148), channel_id=1, source_target_pairs={{0,1},{1,2},{2,3},{3,0},{4,5},{5,6},{6,7},{7,4},{8,9},{9,10},{10,1... | collective-permute-start | bytes 6152 | tf_op jit(solution)/shard_map/ppermute | solution.py:389
  374.5 37.6 %copy-start.39 = (bf16[512,1024]{1,0:T(8,128)(2,1)S(1)}, bf16[512,1024]{1,0:T(8,128)(2,1)}, u32[]{:S(2)}) copy-start(bf16[512,1024]{1,0:T(8,128)(2,1)} %get-tuple-element.30) | copy-start | bytes 3145732
  374.5 16.8 %collective-permute-start.24 = (bf16[512,512]{1,0:T(8,128)(2,1)S(1)}, bf16[512,512]{1,0:T(8,128)(2,1)S(1)}, u32[]{:S(2)}, u32[]{:S(2)}) collective-permute-start(bf16[512,512]{1,0:T(8,128)(2,1)S(1)} %get-tuple-element.105), channel_id=1, source_target_pairs={{0,1},{1,2},{2,3},{3,0},{4,5},{5,6},{6,7},{7,4},{8,9},{9,10},{10,1... | collective-permute-start | bytes 1572872 | tf_op jit(solution)/shard_map/ppermute | solution.py:389
  376.9 33.8 %collective-permute-start.25 = (bf16[512,512]{1,0:T(8,128)(2,1)S(1)}, bf16[512,512]{1,0:T(8,128)(2,1)S(1)}, u32[]{:S(2)}, u32[]{:S(2)}) collective-permute-start(bf16[512,512]{1,0:T(8,128)(2,1)S(1)} %get-tuple-element.105), channel_id=1, source_target_pairs={{0,2},{1,3},{2,0},{3,1},{4,6},{5,7},{6,4},{7,5},{8,10},{9,11},{10,... | collective-permute-start | bytes 1572872 | tf_op jit(solution)/shard_map/ppermute | solution.py:389
  377.7 33.0 %collective-permute-start.26 = (bf16[512,512]{1,0:T(8,128)(2,1)S(1)}, bf16[512,512]{1,0:T(8,128)(2,1)S(1)}, u32[]{:S(2)}, u32[]{:S(2)}) collective-permute-start(bf16[512,512]{1,0:T(8,128)(2,1)S(1)} %get-tuple-element.105), channel_id=1, source_target_pairs={{0,3},{1,0},{2,1},{3,2},{4,7},{5,4},{6,5},{7,6},{8,11},{9,8},{10,9... | collective-permute-start | bytes 1572872 | tf_op jit(solution)/shard_map/ppermute | solution.py:389
  416.6 240.5 %reduce-scatter.11.cloned.1.call-start = ((), (), s32[]{:S(2)}) async-start(), calls=%async_computation.11 | async-start | bytes 6340608 | tf_op jit(solution)/shard_map/reduce_scatter | solution.py:539
  424.2 235.1 %reduce-scatter.9.cloned.1.call-start = ((), (), s32[]{:S(2)}) async-start(), calls=%async_computation.10 | async-start | bytes 12681216 | tf_op jit(solution)/shard_map/reduce_scatter | solution.py:540
  435.1 294.3 %reduce-scatter.5.cloned.1.call-start = ((), (), s32[]{:S(2)}) async-start(), calls=%async_computation.8 | async-start | bytes 14745600 | tf_op jit(solution)/shard_map/reduce_scatter | solution.py:542
  500.4 29.2 %collective-permute-start.14 = (bf16[512,512]{1,0:T(8,128)(2,1)S(1)}, bf16[512,512]{1,0:T(8,128)(2,1)S(1)}, u32[]{:S(2)}, u32[]{:S(2)}) collective-permute-start(bf16[512,512]{1,0:T(8,128)(2,1)S(1)} %get-tuple-element.122), channel_id=1, source_target_pairs={{0,3},{1,0},{2,1},{3,2},{4,7},{5,4},{6,5},{7,6},{8,11},{9,8},{10,9... | collective-permute-start | bytes 1572872 | tf_op jit(solution)/shard_map/ppermute | solution.py:389
  512.7 46.1 %collective-permute-start.13 = (bf16[512,512]{1,0:T(8,128)(2,1)S(1)}, bf16[512,512]{1,0:T(8,128)(2,1)S(1)}, u32[]{:S(2)}, u32[]{:S(2)}) collective-permute-start(bf16[512,512]{1,0:T(8,128)(2,1)S(1)} %get-tuple-element.123), channel_id=1, source_target_pairs={{0,2},{1,3},{2,0},{3,1},{4,6},{5,7},{6,4},{7,5},{8,10},{9,11},{10,... | collective-permute-start | bytes 1572872 | tf_op jit(solution)/shard_map/ppermute | solution.py:389
  513.0 45.9 %collective-permute-start.12 = (bf16[512,512]{1,0:T(8,128)(2,1)S(1)}, bf16[512,512]{1,0:T(8,128)(2,1)S(1)}, u32[]{:S(2)}, u32[]{:S(2)}) collective-permute-start(bf16[512,512]{1,0:T(8,128)(2,1)S(1)} %get-tuple-element.121), channel_id=1, source_target_pairs={{0,1},{1,2},{2,3},{3,0},{4,5},{5,6},{6,7},{7,4},{8,9},{9,10},{10,1... | collective-permute-start | bytes 1572872 | tf_op jit(solution)/shard_map/ppermute | solution.py:389
  523.9 40.0 %copy-start.22 = (f32[512,2048]{1,0:T(8,128)}, f32[512,2048]{1,0:T(8,128)S(1)}, u32[]{:S(2)}) copy-start(f32[512,2048]{1,0:T(8,128)S(1)} %get-tuple-element.151) | copy-start | bytes 12582916
  523.9 35.0 %collective-permute-start.32 = (f32[512]{0:T(512)S(1)}, f32[512]{0:T(512)S(1)}, u32[]{:S(2)}, u32[]{:S(2)}) collective-permute-start(f32[512]{0:T(512)S(1)} %get-tuple-element.150), channel_id=1, source_target_pairs={{0,3},{1,0},{2,1},{3,2},{4,7},{5,4},{6,5},{7,6},{8,11},{9,8},{10,9... | collective-permute-start | bytes 6152 | tf_op jit(solution)/shard_map/ppermute | solution.py:389
  527.4 98.2 %collective-permute-start.31 = (f32[512]{0:T(512)S(1)}, f32[512]{0:T(512)S(1)}, u32[]{:S(2)}, u32[]{:S(2)}) collective-permute-start(f32[512]{0:T(512)S(1)} %get-tuple-element.150), channel_id=1, source_target_pairs={{0,2},{1,3},{2,0},{3,1},{4,6},{5,7},{6,4},{7,5},{8,10},{9,11},{10,... | collective-permute-start | bytes 6152 | tf_op jit(solution)/shard_map/ppermute | solution.py:389
  529.6 96.0 %collective-permute-start.30 = (f32[512]{0:T(512)S(1)}, f32[512]{0:T(512)S(1)}, u32[]{:S(2)}, u32[]{:S(2)}) collective-permute-start(f32[512]{0:T(512)S(1)} %get-tuple-element.150), channel_id=1, source_target_pairs={{0,1},{1,2},{2,3},{3,0},{4,5},{5,6},{6,7},{7,4},{8,9},{9,10},{10,1... | collective-permute-start | bytes 6152 | tf_op jit(solution)/shard_map/ppermute | solution.py:389
  558.9 66.8 %collective-permute-start.29 = (bf16[512,512]{1,0:T(8,128)(2,1)}, bf16[512,512]{1,0:T(8,128)(2,1)}, u32[]{:S(2)}, u32[]{:S(2)}) collective-permute-start(bf16[512,512]{1,0:T(8,128)(2,1)} %get-tuple-element.116), channel_id=1, source_target_pairs={{0,3},{1,0},{2,1},{3,2},{4,7},{5,4},{6,5},{7,6},{8,11},{9,8},{10,9... | collective-permute-start | bytes 1572872 | tf_op jit(solution)/shard_map/ppermute | solution.py:389
  558.9 66.8 %collective-permute-start.28 = (bf16[512,512]{1,0:T(8,128)(2,1)}, bf16[512,512]{1,0:T(8,128)(2,1)}, u32[]{:S(2)}, u32[]{:S(2)}) collective-permute-start(bf16[512,512]{1,0:T(8,128)(2,1)} %get-tuple-element.117), channel_id=1, source_target_pairs={{0,2},{1,3},{2,0},{3,1},{4,6},{5,7},{6,4},{7,5},{8,10},{9,11},{10,... | collective-permute-start | bytes 1572872 | tf_op jit(solution)/shard_map/ppermute | solution.py:389
  559.0 66.7 %copy-start.4 = (bf16[512,512]{1,0:T(8,128)(2,1)S(1)}, bf16[512,512]{1,0:T(8,128)(2,1)}, u32[]{:S(2)}) copy-start(bf16[512,512]{1,0:T(8,128)(2,1)} %param.21) | copy-start | bytes 1572868
  559.0 66.7 %copy-start.5 = (f32[512,512]{1,0:T(8,128)S(1)}, f32[512,512]{1,0:T(8,128)}, u32[]{:S(2)}) copy-start(f32[512,512]{1,0:T(8,128)} %get-tuple-element.106) | copy-start | bytes 3145732
  559.0 66.7 %collective-permute-start.27 = (bf16[512,512]{1,0:T(8,128)(2,1)S(1)}, bf16[512,512]{1,0:T(8,128)(2,1)}, u32[]{:S(2)}, u32[]{:S(2)}) collective-permute-start(bf16[512,512]{1,0:T(8,128)(2,1)S(1)} %get-tuple-element.115), channel_id=1, source_target_pairs={{0,1},{1,2},{2,3},{3,0},{4,5},{5,6},{6,7},{7,4},{8,9},{9,10},{10,1... | collective-permute-start | bytes 1572872 | tf_op jit(solution)/shard_map/ppermute | solution.py:389
  (35 other events, 367.8 us)
Sparse Core Ops, SparseCore 0:
  15.7 77.0 all-gather.4
  94.7 37.6 all-gather.6
  134.8 68.9 all-gather.8
  205.5 43.7 all-gather.10
  416.7 61.1 reduce-scatter.6
  481.6 58.4 reduce-scatter.10
  544.2 86.3 reduce-scatter.8
  634.2 95.1 reduce-scatter.4

commit v2 on v1

v2 whole, which is shorter than its diff:
```python
import functools
import jax
import jax.numpy as jnp
from jax import lax
from jax.experimental import pallas as pl
from jax.experimental.pallas import tpu as pltpu
from jax.sharding import PartitionSpec as P

BF = jnp.bfloat16
F32 = jnp.float32
BLOCK = 128
COST = pl.CostEstimate(flops=20_000_000_000, bytes_accessed=20_000_000, transcendentals=4_000_000)
VMEM = 56 * 1024 * 1024


def dot(left, right, lc=1, rc=0):
    return lax.dot_general(left, right, (((lc,), (rc,)), ((), ())), preferred_element_type=F32)


def split(x):
    high = x.astype(BF)
    return high, (x - high.astype(F32)).astype(BF)


def dot3(left, right, lc=1, rc=0):
    return (
        dot(left[0], right[0], lc, rc) + dot(left[0], right[1], lc, rc) + dot(left[1], right[0], lc, rc)
    )


def dotx(left, right, lc=1, rc=0):
    first = right.astype(BF)
    rest = right - first.astype(F32)
    second = rest.astype(BF)
    third = (rest - second.astype(F32)).astype(BF)
    return dot(left, first, lc, rc) + dot(left, second, lc, rc) + dot(left, third, lc, rc)


def sigmoid(x):
    return 0.5 + 0.5 * jnp.tanh(0.5 * x)


def lane_pick(block, lane):
    index = lax.broadcasted_iota(jnp.int32, block.shape, 1)
    return jnp.sum(jnp.where(index == lane, block, 0.0), axis=1, keepdims=True)


def row_pick(block, row):
    index = lax.broadcasted_iota(jnp.int32, block.shape, 0)
    return jnp.sum(jnp.where(index == row, block, 0.0), axis=0, keepdims=True)


def softplus(x):
    return jnp.maximum(x, 0.0) + jnp.log1p(jnp.exp(-jnp.abs(x)))


def conv_act(x, taps, marks):
    total = x * taps[3:4]
    for shift in (1, 2, 3):
        total = total + (marks[:, shift - 1 : shift] * pltpu.roll(x, shift, 0)) * taps[3 - shift : 4 - shift]
    gate = sigmoid(total)
    return total, gate


def grids():
    rows = lax.broadcasted_iota(jnp.int32, (BLOCK, BLOCK), 0)
    cols = lax.broadcasted_iota(jnp.int32, (BLOCK, BLOCK), 1)
    return rows, cols


def decays(small, params, head, heads):
    rate = jnp.exp(params[0:1])
    log_decay = -rate * softplus(small + params[1:2])
    beta = sigmoid(lane_pick(small, heads + head))
    return log_decay, beta


def block_decay(log_decay, head, rows, cols, seg_col, seg_row, last_seg):
    lower = (rows >= cols).astype(BF)
    running = dotx(lower, log_decay)
    column = lane_pick(running, head)
    line = row_pick(running.T, head)
    same = (seg_col == seg_row) & (rows >= cols)
    decay = jnp.where(same, jnp.exp(jnp.minimum(column - line, 0.0)), 0.0)
    carried = None
    if last_seg is not None:
        carried = jnp.where(seg_col == last_seg, jnp.exp(column), 0.0)
    return decay, carried


def unit_inverses(lowers, rows, cols):
    identity = (rows == cols).astype(F32)
    base = 16
    same = (rows // base) == (cols // base)
    nears = [jnp.where(same, -lower, 0.0) for lower in lowers]
    powers = [split(near) for near in nears]
    totals = [identity + near for near in nears]
    width = 2
    while width < base:
        powers = [split(dot3(power, power)) for power in powers]
        totals = [total + dot3(split(total), power) for total, power in zip(totals, powers)]
        width *= 2
    while base < BLOCK:
        pair_at = (rows // (2 * base) == cols // (2 * base)) & (rows // base != cols // base)
        offs = [split(jnp.where(pair_at, lower, 0.0)) for lower in lowers]
        parts = [split(total) for total in totals]
        middles = [split(dot3(off, part)) for off, part in zip(offs, parts)]
        totals = [total - dot3(part, middle) for total, part, middle in zip(totals, parts, middles)]
        base *= 2
    return totals


def head_inputs(pres, taps_refs, marks):
    query_taps, key_taps, value_taps = taps_refs
    dk = pres[0].shape[1]
    x = jnp.concatenate(pres, axis=1)
    taps = jnp.concatenate([query_taps[...], key_taps[...], value_taps[...]], axis=1)
    total, gate = conv_act(x, taps, marks)
    act = total * gate
    query_act, key_act, values = act[:, :dk], act[:, dk : 2 * dk], act[:, 2 * dk :]
    query_scale = lax.rsqrt(jnp.sum(query_act * query_act, axis=1, keepdims=True) + 1e-06)
    key_scale = lax.rsqrt(jnp.sum(key_act * key_act, axis=1, keepdims=True) + 1e-06)
    return x, taps, total, gate, query_act, key_act, values, query_scale, key_scale


def forward_kernel(heads, hidden_ref, query_weight, key_weight, value_weight, gate_weight, small_weight,
                   query_taps, key_taps, value_taps, marks_ref, segs_ref, params_ref, gain_ref,
                   query_ref, key_ref, value_ref, gate_ref, small_ref,
                   mixed_ref, out_ref, fresh_ref, mats_ref, states_ref):
    head = pl.program_id(0)
    hidden = hidden_ref[...]

    @pl.when(head == 0)
    def _():
        small_ref[...] = dot(hidden, small_weight[...])

    query_ref[...] = dot(hidden, query_weight[...])
    key_ref[...] = dot(hidden, key_weight[...])
    value_ref[...] = dot(hidden, value_weight[...])
    gate_ref[...] = dot(hidden, gate_weight[...])
    marks = marks_ref[...]
    _, _, _, _, query_act, key_act, values, query_scale, key_scale = head_inputs(
        [query_ref[...], key_ref[...], value_ref[...]], (query_taps, key_taps, value_taps), marks
    )
    tokens, dk = query_act.shape
    queries = query_act * (query_scale * dk ** -0.5)
    keys = key_act * key_scale
    log_decay, beta = decays(small_ref[...], params_ref[...], head, heads)
    rows, cols = grids()
    blocks = tokens // BLOCK
    cuts = [slice(index * BLOCK, (index + 1) * BLOCK) for index in range(blocks)]
    key_parts = [split(keys[at]) for at in cuts]
    query_parts = [split(queries[at]) for at in cuts]
    decay_pairs = [
        block_decay(
            log_decay[at], head, rows, cols, marks[at, 6:7], segs_ref[0:1, at],
            marks[index * BLOCK - 1 : index * BLOCK, 6:7] if index else None,
        )
        for index, at in enumerate(cuts)
    ]
    inners = [
        jnp.where(rows > cols, dot3(key, key, 1, 1) * pair_of[0], 0.0) for key, pair_of in zip(key_parts, decay_pairs)
    ]
    scores = [dot3(query, key, 1, 1) * pair_of[0] for query, key, pair_of in zip(query_parts, key_parts, decay_pairs)]
    inverses = unit_inverses([beta[at] * inner for at, inner in zip(cuts, inners)], rows, cols)
    state = None
    for index, at in enumerate(cuts):
        decay, carried = decay_pairs[index]
        inner, score, inverse = inners[index], scores[index], inverses[index]
        value, strength = values[at], beta[at]
        mats_ref[at, 0:BLOCK] = inner
        mats_ref[at, BLOCK : 2 * BLOCK] = score
        mats_ref[at, 2 * BLOCK :] = inverse
        if index:
            state_parts = split(state)
            source = strength * (value - carried * dot3(key_parts[index], state_parts))
        else:
            source = strength * value
        fresh = dot3(split(inverse), split(source))
        fresh_parts = split(fresh)
        output = dot3(split(score), fresh_parts)
        if index:
            output = output + carried * dot3(query_parts[index], state_parts)
        if index + 1 < blocks:
            grown = dot3(split(keys[at] * lane_pick_row(decay)), fresh_parts, 0, 0)
            state = grown if state is None else carried[BLOCK - 1 : BLOCK] * state + grown
            states_ref[index * dk : (index + 1) * dk, :] = state
        fresh_ref[at, :] = fresh
        out_ref[at, :] = output
        scale = lax.rsqrt(jnp.mean(output * output, axis=1, keepdims=True) + 1e-05)
        gate_pre = gate_ref[at, :]
        mixed_ref[at, :] = (output * scale * gain_ref[0:1] * (gate_pre * sigmoid(gate_pre))).astype(BF)


def lane_pick_row(decay):
    return decay.T[:, BLOCK - 1 : BLOCK]


def backward_kernel(heads, first, query_ref, key_ref, value_ref, gate_ref, small_ref, query_taps, key_taps, value_taps,
                    marks_ref, segs_ref, params_ref, gain_ref, grad_ref, out_ref, fresh_ref, mats_ref, states_ref,
                    low_query_ref, low_key_ref, low_value_ref, low_gate_ref, low_small_ref,
                    query_taps_grad, key_taps_grad, value_taps_grad, params_grad_ref, gain_grad_ref):
    head = first + pl.program_id(0)

    @pl.when(pl.program_id(0) == 0)
    def _():
        low_small_ref[...] = jnp.zeros_like(low_small_ref)
        params_grad_ref[...] = jnp.zeros_like(params_grad_ref)
        gain_grad_ref[...] = jnp.zeros_like(gain_grad_ref)

    marks = marks_ref[...]
    x, taps, total, gate, query_act, key_act, values, query_scale, key_scale = head_inputs(
        [query_ref[...], key_ref[...], value_ref[...]], (query_taps, key_taps, value_taps), marks
    )
    tokens, dk = query_act.shape
    dv = values.shape[1]
    queries = query_act * (query_scale * dk ** -0.5)
    keys = key_act * key_scale
    small = small_ref[...]
    params = params_ref[...]
    log_decay, beta = decays(small, params, head, heads)
    rows, cols = grids()
    gain = gain_ref[0:1]
    blocks = tokens // BLOCK
    upper = (rows <= cols).astype(BF)
    d_state = None
    d_query, d_key, d_value, d_beta, d_decay = [None] * blocks, [None] * blocks, [None] * blocks, [None] * blocks, [None] * blocks
    d_gain = jnp.zeros((1, dv), F32)
    for index in reversed(range(blocks)):
        at = slice(index * BLOCK, (index + 1) * BLOCK)
        grad = grad_ref[at, :]
        output = out_ref[at, :]
        gate_pre = gate_ref[at, :]
        gate_sig = sigmoid(gate_pre)
        gate_act = gate_pre * gate_sig
        scale = lax.rsqrt(jnp.mean(output * output, axis=1, keepdims=True) + 1e-05)
        normed = output * scale
        both = grad * normed
        d_gain = d_gain + jnp.sum(both * gate_act, axis=0, keepdims=True)
        low_gate_ref[at, :] = (
            both * gain * (gate_sig + gate_act * (1.0 - gate_sig))
        ).astype(BF)
        pulled = grad * gate_act * gain
        d_out = scale * (pulled - normed * jnp.mean(pulled * normed, axis=1, keepdims=True))

        seg_col, seg_row = marks[at, 6:7], segs_ref[0:1, at]
        last_seg = marks[index * BLOCK - 1 : index * BLOCK, 6:7] if index else None
        decay, carried = block_decay(log_decay[at], head, rows, cols, seg_col, seg_row, last_seg)
        key, query, value, strength = keys[at], queries[at], values[at], beta[at]
        inner, score, inverse = mats_ref[at, 0:BLOCK], mats_ref[at, BLOCK : 2 * BLOCK], mats_ref[at, 2 * BLOCK :]
        fresh_parts = split(fresh_ref[at, :])
        key_parts, query_parts = split(key), split(query)
        out_parts = split(d_out)
        d_fresh = dot3(split(score), out_parts, 0, 0)
        if d_state is not None:
            tail = lane_pick_row(decay)
            state_grad_parts = split(d_state)
            d_fresh = d_fresh + dot3(split(key * tail), state_grad_parts)
        d_source = dot3(split(inverse), split(d_fresh), 0, 0)
        source_parts = split(d_source)
        d_score = dot3(out_parts, fresh_parts, 1, 1)
        d_lower = jnp.where(rows > cols, -dot3(source_parts, fresh_parts, 1, 1), 0.0)
        d_value[index] = strength * d_source
        d_strength = jnp.sum(d_source * value, axis=1, keepdims=True) + jnp.sum(d_lower * inner, axis=1, keepdims=True)
        change = d_score * score + d_lower * (strength * inner)
        d_run = jnp.sum(change, axis=1, keepdims=True) - jnp.sum(change.T, axis=1, keepdims=True)
        d_scores = split(d_score * decay)
        d_inners = split(d_lower * (strength * decay))
        dq = dot3(d_scores, key_parts)
        dk_ = dot3(d_inners, key_parts) + dot3(d_inners, key_parts, 0, 0) + dot3(d_scores, query_parts, 0, 0)
        last_extra = None
        if d_state is not None:
            moved = dot3(fresh_parts, state_grad_parts, 1, 1)
            dk_ = dk_ + tail * moved
            d_tail = jnp.sum(key * moved, axis=1, keepdims=True) * tail
            d_run = d_run - d_tail
            last_extra = jnp.sum(d_tail, axis=0, keepdims=True)
        if index:
            state = states_ref[(index - 1) * dk : index * dk, :]
            state_parts = split(state)
            out_back = dot3(out_parts, state_parts, 1, 1)
            source_back = dot3(source_parts, state_parts, 1, 1)
            key_source = jnp.sum(key * source_back, axis=1, keepdims=True)
            d_carried = jnp.sum(query * out_back, axis=1, keepdims=True) - strength * key_source
            d_strength = d_strength - carried * key_source
            dq = dq + carried * out_back
            dk_ = dk_ - (strength * carried) * source_back
            d_run = d_run + d_carried * carried
            keep = carried[BLOCK - 1 : BLOCK]
            new_state = dot3(query_parts, split(carried * d_out), 0, 0) - dot3(
                key_parts, split((strength * carried) * d_source), 0, 0
            )
            if d_state is not None:
                kept = jnp.sum(jnp.sum(state * d_state, axis=1, keepdims=True), axis=0, keepdims=True)
                last_extra = last_extra + kept * keep
                new_state = new_state + keep * d_state
            d_state = new_state
        if last_extra is not None:
            at_last = lax.broadcasted_iota(jnp.int32, (BLOCK, 1), 0) == BLOCK - 1
            d_run = d_run + jnp.where(at_last, last_extra, 0.0)
        d_decay[index] = dotx(upper, jnp.broadcast_to(d_run, (BLOCK, BLOCK)))[:, 0:1]
        d_query[index], d_key[index], d_beta[index] = dq, dk_, d_strength

    dq = jnp.concatenate(d_query, axis=0) * dk ** -0.5
    dk_ = jnp.concatenate(d_key, axis=0)
    dv_ = jnp.concatenate(d_value, axis=0)
    query_pull = jnp.sum(dq * query_act, axis=1, keepdims=True)
    key_pull = jnp.sum(dk_ * key_act, axis=1, keepdims=True)
    d_query_act = query_scale * (dq - query_act * (query_scale * query_scale * query_pull))
    d_key_act = key_scale * (dk_ - key_act * (key_scale * key_scale * key_pull))
    d_act = jnp.concatenate([d_query_act, d_key_act, dv_], axis=1)
    d_total = d_act * (gate * (1.0 + total * (1.0 - gate)))
    d_pre = d_total * taps[3:4]
    tap_sums = [None, None, None, jnp.sum(d_total * x, axis=0, keepdims=True)]
    for shift in (1, 2, 3):
        moved = marks[:, 2 + shift : 3 + shift] * pltpu.roll(d_total, tokens - shift, 0)
        d_pre = d_pre + moved * taps[3 - shift : 4 - shift]
        tap_sums[3 - shift] = jnp.sum(moved * x, axis=0, keepdims=True)
    d_pre = d_pre.astype(BF)
    low_query_ref[...] = d_pre[:, :dk]
    low_key_ref[...] = d_pre[:, dk : 2 * dk]
    low_value_ref[...] = d_pre[:, 2 * dk :]
    for tap in range(4):
        query_taps_grad[tap : tap + 1, :] = tap_sums[tap][:, :dk]
        key_taps_grad[tap : tap + 1, :] = tap_sums[tap][:, dk : 2 * dk]
        value_taps_grad[tap : tap + 1, :] = tap_sums[tap][:, 2 * dk :]

    d_log = jnp.concatenate(d_decay, axis=0)
    d_str = jnp.concatenate(d_beta, axis=0)
    lane = lax.broadcasted_iota(jnp.int32, small.shape, 1)
    rate = jnp.exp(params[0:1])
    d_decay_pre = jnp.where(lane == head, d_log * (-rate) * sigmoid(small + params[1:2]), 0.0)
    d_beta_pre = jnp.where(lane == heads + head, d_str * beta * (1.0 - beta), 0.0)
    low_small_ref[...] += (d_decay_pre + d_beta_pre).astype(BF)
    params_grad_ref[0:1, :] += jnp.sum(jnp.where(lane == head, d_log * log_decay, 0.0), axis=0, keepdims=True)
    params_grad_ref[1:2, :] += jnp.sum(d_decay_pre, axis=0, keepdims=True)
    gain_grad_ref[0:1, :] += d_gain


def whole(h):
    return (0, 0)


def of_head(first):
    return lambda h: (0, first + h)


def shared_specs(tokens, dk, dv, first):
    own = of_head(first)
    return [
        pl.BlockSpec((4, dk), own),
        pl.BlockSpec((4, dk), own),
        pl.BlockSpec((4, dv), own),
        pl.BlockSpec((tokens, 8), whole),
        pl.BlockSpec((8, tokens), whole),
        pl.BlockSpec((8, 128), whole),
        pl.BlockSpec((8, dv), whole),
    ]


def pre_specs(tokens, dk, dv, first):
    own = of_head(first)
    return [
        pl.BlockSpec((tokens, dk), own),
        pl.BlockSpec((tokens, dk), own),
        pl.BlockSpec((tokens, dv), own),
        pl.BlockSpec((tokens, dv), own),
        pl.BlockSpec((tokens, 128), whole),
    ]


def saved_specs(tokens, dk, dv, first):
    own = of_head(first)
    blocks = tokens // BLOCK
    return [
        pl.BlockSpec((tokens, dv), own),
        pl.BlockSpec((tokens, dv), own),
        pl.BlockSpec((tokens, 3 * BLOCK), own),
        pl.BlockSpec(((blocks - 1) * dk, dv), own),
    ]


def mixer_forward(heads, dk, dv, hidden, weight, shared):
    tokens, model = hidden.shape
    blocks = tokens // BLOCK
    each = heads // 2
    wide = 2 * dk + 2 * dv

    def columns(size, before):
        return lambda h: (0, (h // each * each * wide + each * before) // size + h % each)

    return pl.pallas_call(
        functools.partial(forward_kernel, heads),
        grid=(heads,),
        in_specs=[
            pl.BlockSpec((tokens, model), whole),
            pl.BlockSpec((model, dk), columns(dk, 0)),
            pl.BlockSpec((model, dk), columns(dk, dk)),
            pl.BlockSpec((model, dv), columns(dv, 2 * dk)),
            pl.BlockSpec((model, dv), columns(dv, 2 * dk + dv)),
            pl.BlockSpec((model, 128), lambda h: (0, heads * wide // 128)),
        ]
        + shared_specs(tokens, dk, dv, 0),
        out_specs=pre_specs(tokens, dk, dv, 0)
        + [pl.BlockSpec((tokens, dv), of_head(0))]
        + saved_specs(tokens, dk, dv, 0),
        out_shape=[
            jax.ShapeDtypeStruct((tokens, heads * dk), F32),
            jax.ShapeDtypeStruct((tokens, heads * dk), F32),
            jax.ShapeDtypeStruct((tokens, heads * dv), F32),
            jax.ShapeDtypeStruct((tokens, heads * dv), F32),
            jax.ShapeDtypeStruct((tokens, 128), F32),
            jax.ShapeDtypeStruct((tokens, heads * dv), BF),
            jax.ShapeDtypeStruct((tokens, heads * dv), F32),
            jax.ShapeDtypeStruct((tokens, heads * dv), F32),
            jax.ShapeDtypeStruct((tokens, heads * 3 * BLOCK), F32),
            jax.ShapeDtypeStruct(((blocks - 1) * dk, heads * dv), F32),
        ],
        compiler_params=pltpu.CompilerParams(vmem_limit_bytes=VMEM),
        cost_estimate=COST,
        name="mixer_forward",
    )(hidden, weight, weight, weight, weight, weight, *shared)


def mixer_backward(heads, dk, dv, pres, shared, grad, saved, first, count):
    tokens = grad.shape[0]
    own = of_head(0)
    return pl.pallas_call(
        functools.partial(backward_kernel, heads, first),
        grid=(count,),
        in_specs=pre_specs(tokens, dk, dv, first)
        + shared_specs(tokens, dk, dv, first)
        + [pl.BlockSpec((tokens, dv), of_head(first))]
        + saved_specs(tokens, dk, dv, first),
        out_specs=[
            pl.BlockSpec((tokens, dk), own),
            pl.BlockSpec((tokens, dk), own),
            pl.BlockSpec((tokens, dv), own),
            pl.BlockSpec((tokens, dv), own),
            pl.BlockSpec((tokens, 128), whole),
            pl.BlockSpec((4, dk), own),
            pl.BlockSpec((4, dk), own),
            pl.BlockSpec((4, dv), own),
            pl.BlockSpec((8, 128), whole),
            pl.BlockSpec((8, dv), whole),
        ],
        out_shape=[
            jax.ShapeDtypeStruct((tokens, count * dk), BF),
            jax.ShapeDtypeStruct((tokens, count * dk), BF),
            jax.ShapeDtypeStruct((tokens, count * dv), BF),
            jax.ShapeDtypeStruct((tokens, count * dv), BF),
            jax.ShapeDtypeStruct((tokens, 128), BF),
            jax.ShapeDtypeStruct((4, count * dk), F32),
            jax.ShapeDtypeStruct((4, count * dk), F32),
            jax.ShapeDtypeStruct((4, count * dv), F32),
            jax.ShapeDtypeStruct((8, 128), F32),
            jax.ShapeDtypeStruct((8, dv), F32),
        ],
        compiler_params=pltpu.CompilerParams(vmem_limit_bytes=VMEM),
        cost_estimate=COST,
        name="mixer_backward",
    )(*pres, *shared, grad, *saved)


def wide_dot(left, right):
    return jnp.dot(left, right, preferred_element_type=F32)


def contract_tokens(left, right):
    return dot(left, right, 0, 0)


def contract_features(left, right):
    return dot(left, right, 1, 1)


def after(values, *first):
    return lax.optimization_barrier((values, first))[0]


def fence(*values):
    return lax.optimization_barrier(values)


def hop(values, step, size):
    return lax.ppermute(values, "col", [(at, (at + step) % size) for at in range(size)])


def hops(values, size):
    return [values] + [hop(values, step, size) for step in range(1, size)]


def lay(pieces, spots, width):
    whole = jnp.zeros((pieces[0].shape[0], len(pieces) * width), pieces[0].dtype)
    for piece, spot in zip(pieces, spots):
        whole = lax.dynamic_update_slice(whole, piece, (0, spot * width))
    return whole


def gather_cols(values, place, size):
    return lay_cols(hops(values, size), place, size)


def lay_cols(pieces, place, size):
    return lay(pieces, [(place + size - step) % size for step in range(size)], pieces[0].shape[1])


def send_cols(pieces, size):
    return [hop(piece, step + 1, size) for step, piece in enumerate(pieces)]


def add_cols(own, received):
    for piece in received:
        own = own + piece.astype(F32)
    return own


def cut_cols(partial_sum, place, size):
    rows, width = partial_sum.shape[0], partial_sum.shape[1] // size
    own = lax.dynamic_slice(partial_sum, (0, place * width), (rows, width))
    return own, [
        lax.dynamic_slice(partial_sum, (0, (place + step) % size * width), (rows, width)).astype(BF)
        for step in range(1, size)
    ]


def pair(values, mask, rows):
    return lax.ppermute(values, "row", [(at, at ^ mask) for at in range(rows)])


def chips(rows):
    return rows == 8


def order_features(values, rows):
    if not chips(rows):
        return [values]
    here = lax.axis_index("row")
    depth = values.shape[1] // rows
    return [
        jnp.concatenate(
            [
                lax.dynamic_slice(values, (0, (here ^ chip ^ core) * depth), (values.shape[0], depth))
                for chip in (0, 2, 4, 6)
            ],
            axis=1,
        )
        for core in (0, 1)
    ]


def away_part(left, right, rows):
    return contract_tokens(left[1], right).astype(BF) if chips(rows) else None


def near_part(left, right, away, rows):
    if not chips(rows):
        return contract_tokens(left[0], right).astype(BF), None
    return (left[0], right), pair(away, 1, rows)


def hold(near, given, rows):
    return near if given is None else (contract_tokens(*near) + given.astype(F32)).astype(BF)


def send_chips(held, rows):
    if not chips(rows):
        return None, None
    depth = held.shape[0] // 4
    half = depth // 2
    own, x, y, far = (held[at * depth : (at + 1) * depth] for at in range(4))
    from_x = pair(jnp.concatenate([far[:half], x[:half]], axis=0), 2, rows)
    from_y = pair(jnp.concatenate([far[half:], y[half:]], axis=0), 4, rows)
    return from_x, from_y


def last_step(held, from_x, from_y, rows):
    if from_x is None:
        return lax.psum_scatter(held, "row", scatter_dimension=0, tiled=True), None, None, None
    depth = held.shape[0] // 4
    half = depth // 2
    own, x, y, far = (held[at * depth : (at + 1) * depth] for at in range(4))
    last_x = pair((x[half:].astype(F32) + from_y[:half].astype(F32)).astype(BF), 2, rows)
    last_y = pair((y[:half].astype(F32) + from_x[:half].astype(F32)).astype(BF), 4, rows)
    mine = own.astype(F32) + jnp.concatenate([from_x[half:], from_y[half:]], axis=0).astype(F32)
    return mine, last_x, last_y, rows


def finish(mine, last_x, last_y, rows):
    if last_x is None:
        return mine.astype(F32)
    return mine + jnp.concatenate([last_y, last_x], axis=0).astype(F32)


def per_device(
    inputs,
    segment_ids,
    norm_gain,
    query_weight,
    key_weight,
    value_weight,
    gate_weight,
    decay_weight,
    beta_weight,
    query_conv,
    key_conv,
    value_conv,
    decay_log,
    decay_bias,
    head_gain,
    out_weight,
    second_gain,
    hidden_gate,
    hidden_up,
    hidden_down,
    cotangent,
):
    tokens, width = inputs.shape
    size = lax.axis_size("col")
    rows = lax.axis_size("row")
    place = lax.axis_index("col")
    model = size * width
    heads = decay_weight.shape[1]
    dk = query_weight.shape[1] // heads
    dv = value_weight.shape[1] // heads
    depth = query_weight.shape[0]
    hidden_units = hidden_gate.shape[1]
    wide = 2 * dk + 2 * dv
    each = heads // 2
    span = each * wide

    def per_half(arrays, sizes):
        return [
            array[:, half * each * size : (half + 1) * each * size] for half in (0, 1) for array, size in zip(arrays, sizes)
        ]

    in_weight = jnp.concatenate(
        per_half([query_weight, key_weight, value_weight, gate_weight], [dk, dk, dv, dv])
        + [decay_weight, beta_weight, jnp.zeros((depth, 128 - 2 * heads), BF)],
        axis=1,
    )
    inputs_all = gather_cols(inputs, place, size)
    gains_all = gather_cols(jnp.stack([norm_gain, second_gain]), place, size)
    in_all = lax.all_gather(in_weight, "row", axis=0, tiled=True)
    out_all = lax.all_gather(out_weight, "row", axis=1, tiled=True)
    hidden_gate, hidden_up, hidden_down = after((hidden_gate, hidden_up, hidden_down), in_weight)
    stacked = jnp.concatenate([hidden_gate.T, hidden_up.T, hidden_down], axis=0)
    stacked = lax.all_gather(stacked, "row", axis=1, tiled=True)
    mlp_all, down_all = stacked[: 2 * hidden_units], stacked[2 * hidden_units :]
    first_gains, second_gains = gains_all[0:1], gains_all[1:2]

    wide_all = inputs_all.astype(F32)
    first_scale = lax.rsqrt(jnp.mean(wide_all * wide_all, axis=1, keepdims=True) + 1e-05)
    hidden, in_all, cotangent_late = fence((wide_all * first_scale * first_gains).astype(BF), in_all, cotangent)
    grad_all = gather_cols(cotangent_late, place, size)

    times = jnp.arange(tokens)
    marks = [
        jnp.where((times >= shift) & (jnp.roll(segment_ids, shift) == segment_ids), 1.0, 0.0) for shift in (1, 2, 3)
    ]
    marks = marks + [jnp.roll(mark, -shift) for mark, shift in zip(marks, (1, 2, 3))]
    seg = segment_ids.astype(F32)
    marks = jnp.stack(marks + [seg, seg], axis=1)
    segs = jnp.broadcast_to(seg[None], (8, tokens))
    params = jnp.pad(jnp.stack([decay_log, decay_bias]), ((0, 6), (0, 128 - heads)))
    gain = jnp.broadcast_to(head_gain[None], (8, dv))
    shared = (query_conv, key_conv, value_conv, marks, segs, params, gain)
    made = mixer_forward(heads, dk, dv, hidden, in_all, shared)
    pres, mixed, saved = made[:5], made[5], made[6:]
    mixed, grad_all = fence(mixed, grad_all)

    wide_inputs = inputs.astype(F32)

    half = tokens // 2
    first, last = slice(0, half), slice(half, tokens)

    cut_a = cut_cols(wide_dot(mixed[first], out_all), place, size)
    cut_b = cut_cols(wide_dot(after(mixed[last], cut_a), out_all), place, size)
    got_a = send_cols(cut_a[1], size)
    got_a, cut_b = fence(got_a, cut_b)

    got_b = send_cols(cut_b[1], size)
    residual_a = wide_inputs[first] + add_cols(cut_a[0], got_a)
    grad_sides = order_features(grad_all, rows)
    got_b, residual_a, grad_sides = fence(got_b, residual_a, grad_sides)

    all_a = hops(residual_a.astype(BF), size)
    residual_b = wide_inputs[last] + add_cols(cut_b[0], got_b)
    all_a, residual_b = fence(all_a, residual_b)

    def feed_forward(pieces, grad_rows):
        residual_all = lay_cols(pieces, place, size).astype(F32)
        scale = lax.rsqrt(jnp.mean(residual_all * residual_all, axis=1, keepdims=True) + 1e-05)
        (second,) = fence((residual_all * scale * second_gains).astype(BF))
        both = contract_features(second, mlp_all)
        gate_value, up_value = both[:, :hidden_units], both[:, hidden_units:]
        gate_sig = jax.nn.sigmoid(gate_value)
        gate_act = gate_value * gate_sig
        product = (gate_act * up_value).astype(BF)
        grad_product = contract_features(grad_rows, down_all)
        grad_both = jnp.concatenate(
            [grad_product * up_value * (gate_sig * (1.0 + gate_value * (1.0 - gate_sig))), grad_product * gate_act],
            axis=1,
        ).astype(BF)
        part = wide_dot(grad_both, mlp_all)
        inner = jnp.sum(part * second_gains * residual_all, axis=1)
        return scale, second, product, grad_both, inner, cut_cols(part, place, size)

    all_b = hops(residual_b.astype(BF), size)
    ready_a = feed_forward(all_a, grad_all[first])
    all_b, ready_a = fence(all_b, ready_a)

    scale_a, second_a, product_a, grad_both_a, inner_a, cut_a = ready_a
    got_a, inners_a = send_cols(cut_a[1], size), hops(inner_a, size)
    ready_b = feed_forward(all_b, grad_all[last])
    got_a, inners_a, ready_b = fence(got_a, inners_a, ready_b)

    def back_residual(at, residual, scale, inner, grad_second):
        return (
            cotangent[at].astype(F32)
            + scale * second_gain * grad_second
            - residual * (scale * scale * scale * inner[:, None] / model)
        )

    scale_b, second_b, product_b, grad_both_b, inner_b, cut_b = ready_b
    got_b, inners_b = send_cols(cut_b[1], size), hops(inner_b, size)
    grad_second_a = add_cols(cut_a[0], got_a)
    back_a = back_residual(first, residual_a, scale_a, sum(inners_a), grad_second_a)
    second = jnp.concatenate([second_a, second_b], axis=0)
    grad_both = jnp.concatenate([grad_both_a, grad_both_b], axis=0)
    product = jnp.concatenate([product_a, product_b], axis=0)
    mlp_part = contract_tokens(second, grad_both).astype(BF)
    mlp_grad = lax.psum_scatter(mlp_part, "row", scatter_dimension=0, tiled=True)
    away_down = away_part(grad_sides, product, rows)
    got_b, inners_b, back_a, mlp_part, away_down = fence(got_b, inners_b, back_a, mlp_part, away_down)

    pieces_a = hops(back_a.astype(BF), size)
    grad_second_b = add_cols(cut_b[0], got_b)
    back_b = back_residual(last, residual_b, scale_b, sum(inners_b), grad_second_b)
    near_down, given_down = near_part(grad_sides, product, away_down, rows)
    pieces_a, back_b, given_down = fence(pieces_a, back_b, given_down)

    pieces_b = hops(back_b.astype(BF), size)
    held_down = hold(near_down, given_down, rows)
    result_cut = cut_cols(wide_dot(product, down_all), place, size)
    back_rows_a = lay_cols(pieces_a, place, size)
    pieces_b, held_down, result_cut, back_rows_a = fence(pieces_b, held_down, result_cut, back_rows_a)

    residual = jnp.concatenate([residual_a, residual_b], axis=0)
    scale = jnp.concatenate([scale_a, scale_b], axis=0)
    grad_residual = jnp.concatenate([back_a, back_b], axis=0)
    second_gain_part = jnp.sum(
        jnp.concatenate([grad_second_a, grad_second_b], axis=0) * residual * scale, axis=0
    )
    back_rows = jnp.concatenate([back_rows_a, lay_cols(pieces_b, place, size)], axis=0)
    grad_mixed = contract_features(back_rows, out_all)
    x_down, y_down = send_chips(held_down, rows)
    out_part = contract_tokens(mixed, back_rows).astype(BF)
    out_part, mlp_grad = fence(out_part, mlp_grad)
    out_grad = lax.psum_scatter(out_part, "row", scatter_dimension=1, tiled=True)
    grad_mixed, result_cut = after((grad_mixed, result_cut), out_part)
    result_got = send_cols(result_cut[1], size)
    lows = mixer_backward(heads, dk, dv, pres, shared, grad_mixed, saved, 0, heads)
    lows, x_down, y_down, result_got = fence(lows, x_down, y_down, result_got)
    *lows, low_small, query_taps, key_taps, value_taps, params_part, gain_part = lows
    low = jnp.concatenate(per_half(lows, [dk, dk, dv, dv]) + [low_small], axis=1)
    down_late = last_step(held_down, x_down, y_down, rows)

    in_part = contract_tokens(hidden, low).astype(BF)
    in_grad = lax.psum_scatter(in_part, "row", scatter_dimension=0, tiled=True)
    hidden_part = contract_features(after(low, in_part), in_all)
    inner = jnp.sum(hidden_part * first_gains * wide_all, axis=1)
    hidden_cut = cut_cols(hidden_part, place, size)
    first_gain_part = jnp.sum(hidden_part * wide_all * first_scale, axis=0)
    notes = [
        jnp.concatenate(
            [inner, lax.dynamic_slice(first_gain_part, ((place + step) % size * width,), (width,)), gain_part[0]]
        )
        for step in range(size)
    ]
    notes, hidden_cut, down_late = fence(notes, hidden_cut, down_late)

    noted = sum([notes[0]] + send_cols(notes[1:], size))
    hidden_got = send_cols(hidden_cut[1], size)
    first_inner, gains = noted[:tokens, None], noted[tokens:]
    sums = [query_taps, key_taps, value_taps, params_part[0:2, :heads], second_gain_part, gains]
    query_taps, key_taps, value_taps, params_grad, second_gain_grad, gains = lax.psum(sums, "row")
    norm_gain_grad, gain_grad = gains[:width], gains[width:]
    result = add_cols(residual + result_cut[0], result_got)
    down_grad = finish(*down_late).T
    mlp_grad = mlp_grad.astype(F32)
    out_grad = out_grad.astype(F32)
    hidden_got, noted, down_grad, mlp_grad, out_grad, query_taps, result = fence(
        hidden_got, noted, down_grad, mlp_grad, out_grad, query_taps, result
    )

    grad_hidden = add_cols(hidden_cut[0], hidden_got)
    grad_inputs = (
        grad_residual
        + first_scale * norm_gain * grad_hidden
        - wide_inputs * (first_scale * first_scale * first_scale * first_inner / model)
    )
    in_grad, result, grad_inputs = fence(in_grad, result, grad_inputs)

    def head_columns(start, stop):
        return jnp.concatenate(
            [in_grad[:, half * span + each * start : half * span + each * stop] for half in (0, 1)], axis=1
        ).astype(F32)

    return (
        result,
        grad_inputs,
        norm_gain_grad,
        head_columns(0, dk),
        head_columns(dk, 2 * dk),
        head_columns(2 * dk, 2 * dk + dv),
        head_columns(2 * dk + dv, wide),
        in_grad[:, 2 * span : 2 * span + heads].astype(F32),
        in_grad[:, 2 * span + heads : 2 * span + 2 * heads].astype(F32),
        query_taps,
        key_taps,
        value_taps,
        params_grad[0],
        params_grad[1],
        gain_grad,
        out_grad,
        second_gain_grad,
        mlp_grad[:, :hidden_units],
        mlp_grad[:, hidden_units:],
        down_grad,
    )


ROW_COL = P("row", "col")
COL_ROW = P("col", "row")
PLACED = (
    ROW_COL, P("row"), P("col"),
    ROW_COL, ROW_COL, ROW_COL, ROW_COL, ROW_COL, ROW_COL,
    P(None, "col"), P(None, "col"), P(None, "col"),
    P("col"), P("col"), P(),
    COL_ROW, P("col"), ROW_COL, ROW_COL, COL_ROW, ROW_COL,
)
MADE = (
    ROW_COL, ROW_COL, P("col"),
    ROW_COL, ROW_COL, ROW_COL, ROW_COL, ROW_COL, ROW_COL,
    P(None, "col"), P(None, "col"), P(None, "col"),
    P("col"), P("col"), P(),
    COL_ROW, P("col"), ROW_COL, ROW_COL, COL_ROW,
)


def solution(mesh):
    return jax.shard_map(per_device, mesh=mesh, in_specs=PLACED, out_specs=MADE, check_vma=False)
```

time: 755 us -> 579 us (0.77)
  waiting for transfers between devices: 307 us -> 197 us
  blocking collectives: 84.5 us -> 25 us
  starting transfers between devices: 98.8 us -> 84.8 us
  matrix products: 103 us -> 89.1 us
  other arithmetic: 17.6 us -> 31.2 us
  local copies, waits for them, and re-layouts: 45 us -> 52.9 us
    psum x2 -> x1, blocking collectives: 84.5 us -> 25 us  [per_device(): lax.psum(sums, 'row')]
    ppermute x33 -> x48, waiting for transfers between devices: 219 us -> 162 us  [hop(): lax.ppermute(values, 'col', [(at, (at + step) % size) for at in range(siz...]
    reduce_scatter x2 -> x1, waiting for transfers between devices: 67 us -> 13.4 us  [per_device(): in_grad = lax.psum_scatter(in_part, 'row', scatter_dimension=0, tiled=True)]
    ppermute x33 -> x48, starting transfers between devices: 98.5 us -> 80.6 us  [hop(): lax.ppermute(values, 'col', [(at, (at + step) % size) for at in range(siz...]
    dot_general x4 -> x5, matrix products: 34.9 us -> 20.3 us  [wide_dot(): return jnp.dot(left, right, preferred_element_type=F32)]
    reshape x11 -> x0, local copies, waits for them, and re-layouts: 10.1 us -> none  [the longest x7 4.96 us: by_head(): a.reshape(lead, heads, -1)]
    convert_element_type x2 -> x16, other arithmetic: 4.42 us -> 14.2 us  [the longest x4 3.89 us: head_columns(): return jnp.concatenate([in_grad[:, half * span + each * start:half * span...]
    unnamed x96 -> x165, local copies, waits for them, and re-layouts: 12.7 us -> 17 us
  transfers between devices with their start and end apart: 41 -> 59, of which waited for: 14 -> 21; matrix products, arithmetic and copies ran while one was open for 15% -> 24% of each run, Pallas kernels for 11% -> 13%
where the time goes in v2:
time: 579 us; the launch traced here: 569 us
  waiting for transfers between devices  197 us (34%)
  matrix products  89.1 us (15%)
  starting transfers between devices  84.8 us (15%)
  Pallas kernels  72.5 us (13%)
  local copies, waits for them, and re-layouts  52.9 us (9%)
  other arithmetic  31.2 us (5%)
  blocking collectives  25 us (4%)
  between operations  16.2 us (3%)
    ppermute x48, waiting for transfers between devices, hop(): lax.ppermute(values, 'col', [(at, (at + step) % size) for at in range(siz...  162 us
    ppermute x48, starting transfers between devices, hop(): lax.ppermute(values, 'col', [(at, (at + step) % size) for at in range(siz...  80.6 us
    dot_general x11, matrix products, dot(): lax.dot_general(left, right, (((lc,), (rc,)), ((), ())), preferred_elemen...  68.8 us
    pallas_call x1, Pallas kernels, mixer_forward(): pl.pallas_call(functools.partial(forward_kernel, heads), grid=(heads,), i...  37.1 us
    pallas_call x1, Pallas kernels, mixer_backward(): pl.pallas_call(functools.partial(backward_kernel, heads, first), grid=(co...  35.4 us
    psum x1, blocking collectives, per_device(): lax.psum(sums, 'row')  25 us
    all_gather x1, waiting for transfers between devices, per_device(): in_all = lax.all_gather(in_weight, 'row', axis=0, tiled=True)  20.6 us
    dot_general x5, matrix products, wide_dot(): return jnp.dot(left, right, preferred_element_type=F32)  20.3 us
  transfers between devices with their start and end apart: 59, of which 21 were waited for; matrix products, arithmetic and copies ran while one was open for 24% of the time, Pallas kernels for 13%

profile of v2, /device:TPU:0, one launch (start us, length us, event | category | flops | bytes accessed | tf_op | source)
XLA Modules:
  0.0 569.0 jit_solution(4953753130963452041)
XLA Ops:
  13.8 3.4 concatenate.107
  20.3 4.1 collective-permute-start.4
  35.2 3.3 collective-permute-start.2
  38.6 16.3 %collective-permute-done = bf16[512,512]{1,0:T(8,128)(2,1)} collective-permute-done((bf16[512,512]{1,0:T(8,128)(2,1)}, bf16[512,512]{1,0:T(8,128)(2,1)}, u32[]{:S(2)}, u32[]{:S(2)}) %collective-permute-start) | collective-permute-done | bytes 524320 | tf_op jit(solution)/shard_map/ppermute | solution.py:486
  56.1 7.9 %collective-permute-done.1 = bf16[512,512]{1,0:T(8,128)(2,1)} collective-permute-done((bf16[512,512]{1,0:T(8,128)(2,1)}, bf16[512,512]{1,0:T(8,128)(2,1)}, u32[]{:S(2)}, u32[]{:S(2)}) %collective-permute-start.1) | collective-permute-done | bytes 524320 | tf_op jit(solution)/shard_map/ppermute | solution.py:486
  65.2 6.1 %collective-permute-done.2 = bf16[512,512]{1,0:T(8,128)(2,1)S(1)} collective-permute-done((bf16[512,512]{1,0:T(8,128)(2,1)}, bf16[512,512]{1,0:T(8,128)(2,1)S(1)}, u32[]{:S(2)}, u32[]{:S(2)}) %collective-permute-start.2) | collective-permute-done | bytes 524320 | tf_op jit(solution)/shard_map/ppermute | solution.py:486
  73.8 20.6 %all-gather.4.cloned.1.call-done.query_weight.key_weight.value_weight.gate_weight.small_weight = bf16[2048,3200]{1,0:T(8,128)(2,1)} async-done(((bf16[256,3200]{1,0:T(8,128)(2,1)}), bf16[2048,3200]{1,0:T(8,128)(2,1)}) %all-gather.4.cloned.1.call-update) | async-done | bytes 13107216 | tf_op jit(solution)/shard_map/all_gather | solution.py:644
  94.4 3.3 collective-permute-start.8
  100.1 37.1 %mixer_forward.1 = (f32[512,512]{1,0:T(8,128)}, f32[512,512]{1,0:T(8,128)}, f32[512,1024]{1,0:T(8,128)}, f32[512,1024]{1,0:T(8,128)}, f32[512,128]{1,0:T(8,128)}...) custom-call(bf16[512,2048]{1,0:T(8,128)(2,1)} %fusion.16.hidden_ref,, ...), custom_call_target="tpu_custom_call" | custom-call | flops 20000000000 | bytes 20000000 | tf_op jit(solution)/shard_map/mixer_forward/pallas_call | solution.py:392
  138.4 5.0 collective-permute-done.7
  144.4 4.1 fusion.42
  148.9 2.9 collective-permute-start.10
  157.6 16.9 %collective-permute-done.10 = bf16[256,512]{1,0:T(8,128)(2,1)S(1)} collective-permute-done((bf16[256,512]{1,0:T(8,128)(2,1)S(1)}, bf16[256,512]{1,0:T(8,128)(2,1)S(1)}, u32[]{:S(2)}, u32[]{:S(2)}) %collective-permute-start.10) | collective-permute-done | bytes 262176 | tf_op jit(solution)/shard_map/ppermute | solution.py:486
  174.8 3.6 collective-permute-start.14
  178.6 7.1 %collective-permute-done.12 = bf16[256,512]{1,0:T(8,128)(2,1)S(1)} collective-permute-done((bf16[256,512]{1,0:T(8,128)(2,1)S(1)}, bf16[256,512]{1,0:T(8,128)(2,1)S(1)}, u32[]{:S(2)}, u32[]{:S(2)}) %collective-permute-start.12) | collective-permute-done | bytes 262176 | tf_op jit(solution)/shard_map/ppermute | solution.py:486
  185.7 9.3 %collective-permute-done.13 = bf16[256,512]{1,0:T(8,128)(2,1)S(1)} collective-permute-done((bf16[256,512]{1,0:T(8,128)(2,1)S(1)}, bf16[256,512]{1,0:T(8,128)(2,1)S(1)}, u32[]{:S(2)}, u32[]{:S(2)}) %collective-permute-start.13) | collective-permute-done | bytes 262176 | tf_op jit(solution)/shard_map/ppermute | solution.py:486
  195.0 5.9 %collective-permute-start.17 = (bf16[256,512]{1,0:T(8,128)(2,1)S(1)}, bf16[256,512]{1,0:T(8,128)(2,1)S(1)}, u32[]{:S(2)}, u32[]{:S(2)}) collective-permute-start(bf16[256,512]{1,0:T(8,128)(2,1)S(1)} %convert_element_type.242), channel_id=1, source_target_pairs={{0,3},{1,0},{2,1},{3,2},{4,7},{5,4},{6,5},{7,6},{8,11},{9,8},{10,9... | collective-permute-start | bytes 786440 | tf_op jit(solution)/shard_map/ppermute | solution.py:486
  201.9 5.8 %collective-permute-done.17 = bf16[256,512]{1,0:T(8,128)(2,1)S(1)} collective-permute-done((bf16[256,512]{1,0:T(8,128)(2,1)S(1)}, bf16[256,512]{1,0:T(8,128)(2,1)S(1)}, u32[]{:S(2)}, u32[]{:S(2)}) %collective-permute-start.17) | collective-permute-done | bytes 262176 | tf_op jit(solution)/shard_map/ppermute | solution.py:486
  207.7 16.2 %collective-permute-done.16 = bf16[256,512]{1,0:T(8,128)(2,1)S(1)} collective-permute-done((bf16[256,512]{1,0:T(8,128)(2,1)S(1)}, bf16[256,512]{1,0:T(8,128)(2,1)S(1)}, u32[]{:S(2)}, u32[]{:S(2)}) %collective-permute-start.16) | collective-permute-done | bytes 262176 | tf_op jit(solution)/shard_map/ppermute | solution.py:486
  229.4 6.4 %fusion.6 = f32[256,2752]{0,1:T(8,128)S(1)} fusion(bf16[256,2048]{1,0:T(8,128)(2,1)} %fusion.25, bf16[4128,2048]{1,0:T(8,128)(2,1)} %all-gather.8.cloned.1.call-done), kind=kOutput, calls=%fused_computation.12 | convolution fusion | flops 2885681152 | bytes 15138816 | tf_op jit(solution)/shard_map/dot_general | solution.py:17
  235.9 5.7 %multiply_convert_fusion.4 = (bf16[256,1376]{0,1:T(8,128)(2,1)S(1)}, bf16[256,1376]{0,1:T(8,128)(2,1)S(1)}, bf16[256,1376]{0,1:T(8,128)(2,1)}) fusion(f32[256,2752]{0,1:T(8,128)S(1)} %fusion.6, bf16[4128,2048]{1,0:T(8,128)(2,1)} %all-gather.8.cloned.1.call-done, bf16[512,2048]{1,0:T(8,128)(2,1)S(1)} %constant_dynamic-update-slice_fusion.21), kind=kOutput, calls=%fused_computation.61 | convolution fusion | flops 1448124416 | bytes 11616256 | tf_op jit(solution)/shard_map/dot_general | solution.py:17
  241.7 3.3 fusion.26
  245.2 2.8 collective-permute-done.19
  258.6 6.0 %fusion.2 = f32[256,2752]{0,1:T(8,128)S(1)} fusion(bf16[256,2048]{1,0:T(8,128)(2,1)S(1)} %fusion.29, bf16[4128,2048]{1,0:T(8,128)(2,1)} %all-gather.8.cloned.1.call-done), kind=kOutput, calls=%fused_computation.8 | convolution fusion | flops 2885681152 | bytes 15138816 | tf_op jit(solution)/shard_map/dot_general | solution.py:17
  264.7 5.7 %multiply_convert_fusion.1 = (bf16[256,1376]{0,1:T(8,128)(2,1)S(1)}, bf16[256,1376]{0,1:T(8,128)(2,1)S(1)}, bf16[256,1376]{0,1:T(8,128)(2,1)}) fusion(f32[256,2752]{0,1:T(8,128)S(1)} %fusion.2, bf16[4128,2048]{1,0:T(8,128)(2,1)} %all-gather.8.cloned.1.call-done, bf16[512,2048]{1,0:T(8,128)(2,1)S(1)} %constant_dynamic-update-slice_fusion.21), kind=kOutput, calls=%fused_computation.56 | convolution fusion | flops 1448124416 | bytes 11616256 | tf_op jit(solution)/shard_map/dot_general | solution.py:17
  270.4 6.1 %fusion.30 = (f32[256]{0:T(256)S(1)}, f32[256,2048]{1,0:T(8,128)S(1)}) fusion(bf16[256,2048]{1,0:T(8,128)(2,1)S(1)} %constant_dynamic-update-slice_fusion.13, f32[2048]{0:T(1024)S(1)} %bitcast.55, bf16[4128,2048]{1,0:T(8,128)(2,1)} %all-gather.8.cloned.1.call-done, bf16[256,1376]{0,1:T(8,128)(2,1)S(1)} %get-tuple-element.385, ...), kind=kOutput, calls=%fused_computation.46 | convolution fusion | flops 2890596096 | bytes 15836160 | tf_op jit(solution)/shard_map/dot_general | solution.py:466
  278.1 4.8 collective-permute-done.24
  282.9 8.7 %convolution_convert_fusion.1 = bf16[2048,2752]{0,1:T(8,128)(2,1)} fusion(bf16[256,2752]{0,1:T(8,128)(2,1)S(1)} %pad_maximum_fusion.3, bf16[256,2752]{0,1:T(8,128)(2,1)S(1)} %pad_maximum_fusion.2, bf16[256,2048]{1,0:T(8,128)(2,1)S(1)} %fusion.29, bf16[256,2048]{1,0:T(8,128)(2,1)S(1)} %copy-done.34), kind=kOutput, calls=%fused_computation.1 | convolution fusion | flops 5786828800 | bytes 16187392 | tf_op jit(solution)/shard_map/dot_general | solution.py:17
  300.9 3.1 collective-permute-start.29
  306.4 7.3 %collective-permute-done.28 = bf16[256,512]{1,0:T(8,128)(2,1)S(1)} collective-permute-done((bf16[256,512]{1,0:T(8,128)(2,1)}, bf16[256,512]{1,0:T(8,128)(2,1)S(1)}, u32[]{:S(2)}, u32[]{:S(2)}) %collective-permute-start.28) | collective-permute-done | bytes 262176 | tf_op jit(solution)/shard_map/ppermute | solution.py:486
  314.5 5.5 fusion.8
  322.4 6.4 %collective-permute-start.35 = (bf16[256,512]{1,0:T(8,128)(2,1)S(1)}, bf16[256,512]{1,0:T(8,128)(2,1)S(1)}, u32[]{:S(2)}, u32[]{:S(2)}) collective-permute-start(bf16[256,512]{1,0:T(8,128)(2,1)S(1)} %convert_element_type.265), channel_id=1, source_target_pairs={{0,3},{1,0},{2,1},{3,2},{4,7},{5,4},{6,5},{7,6},{8,11},{9,8},{10,9... | collective-permute-start | bytes 786440 | tf_op jit(solution)/shard_map/ppermute | solution.py:486
  330.4 5.1 collective-permute-done.35
  335.5 17.2 %collective-permute-done.34 = bf16[256,512]{1,0:T(8,128)(2,1)S(1)} collective-permute-done((bf16[256,512]{1,0:T(8,128)(2,1)S(1)}, bf16[256,512]{1,0:T(8,128)(2,1)S(1)}, u32[]{:S(2)}, u32[]{:S(2)}) %collective-permute-start.34) | collective-permute-done | bytes 262176 | tf_op jit(solution)/shard_map/ppermute | solution.py:486
  358.5 2.7 collective-permute-done.39
  361.3 16.3 %collective-permute-done.38 = bf16[256,512]{1,0:T(8,128)(2,1)S(1)} collective-permute-done((bf16[256,512]{1,0:T(8,128)(2,1)S(1)}, bf16[256,512]{1,0:T(8,128)(2,1)S(1)}, u32[]{:S(2)}, u32[]{:S(2)}) %collective-permute-start.38) | collective-permute-done | bytes 262176 | tf_op jit(solution)/shard_map/ppermute | solution.py:486
  378.8 4.4 convolution_convert_fusion.3
  387.8 5.9 %fusion.36.grad_ref = f32[512,1024]{1,0:T(8,128)} fusion(bf16[1024,2048]{1,0:T(8,128)(2,1)} %all-gather.6.cloned.1.call-done, bf16[256,2048]{1,0:T(8,128)(2,1)S(1)} %copy-done.31, bf16[256,2048]{1,0:T(8,128)(2,1)S(1)} %copy-done.33), kind=kOutput, calls=%fused_computation.65 | convolution fusion | flops 2151677952 | bytes 8388608 | tf_op jit(solution)/shard_map/dot_general | solution.py:17
  395.3 3.1 collective-permute-start.44
  398.4 35.4 %mixer_backward.1 = (bf16[512,512]{1,0:T(8,128)(2,1)}, bf16[512,512]{1,0:T(8,128)(2,1)}, bf16[512,1024]{1,0:T(8,128)(2,1)}, bf16[512,1024]{1,0:T(8,128)(2,1)}, b...) custom-call(f32[512,512]{1,0:T(8,128)} %get-tuple-element.168.query_, ...), custom_call_target="tpu_custom_call" | custom-call | flops 20000000000 | bytes 20000000 | tf_op jit(solution)/shard_map/mixer_backward/pallas_call | solution.py:428
  441.2 10.4 %convolution_convert_fusion = bf16[2048,3200]{1,0:T(8,128)(2,1)} fusion(bf16[512,2048]{1,0:T(8,128)(2,1)S(1)} %copy-done.17, bf16[512,3200]{1,0:T(8,128)(2,1)S(1)} %constant_dynamic-update-slice_fusion.2), kind=kOutput, calls=%fused_computation | convolution fusion | flops 6717440000 | bytes 18481152 | tf_op jit(solution)/shard_map/dot_general | solution.py:17
  456.4 12.2 %fusion.19 = (f32[2048]{0:T(1024)S(1)}, f32[512]{0:T(512)S(1)}, f32[512,2048]{1,0:T(8,128)S(1)}) fusion(bf16[512,2048]{1,0:T(8,128)(2,1)S(1)} %copy-done.1, f32[512]{0:T(512)S(1)} %copy-done.59, f32[2048]{0:T(1024)S(1)} %bitcast.60, bf16[512,3200]{1,0:T(8,128)(2,1)} %copy-done.56, ...), kind=kOutput, calls=%fused_computation.26 | convolution fusion | flops 6718223872 | bytes 22695936 | tf_op jit(solution)/shard_map/dot_general | solution.py:17
  475.5 7.2 %collective-permute-start.50 = (f32[1280]{0:T(1024)S(1)}, f32[1280]{0:T(1024)S(1)}, u32[]{:S(2)}, u32[]{:S(2)}) collective-permute-start(f32[1280]{0:T(1024)S(1)} %get-tuple-element.285), channel_id=1, source_target_pairs={{0,1},{1,2},{2,3},{3,0},{4,5},{5,6},{6,7},{7,4},{8,9},{9,10},{10,1... | collective-permute-start | bytes 15368 | tf_op jit(solution)/shard_map/ppermute | solution.py:486
  482.8 2.7 collective-permute-start.51
  491.2 14.6 %collective-permute-done.51 = f32[1280]{0:T(1024)S(1)} collective-permute-done((f32[1280]{0:T(1024)S(1)}, f32[1280]{0:T(1024)S(1)}, u32[]{:S(2)}, u32[]{:S(2)}) %collective-permute-start.51) | collective-permute-done | bytes 5152 | tf_op jit(solution)/shard_map/ppermute | solution.py:486
  505.9 25.0 %all-reduce.1 = (f32[4,512]{1,0:T(4,128)}, f32[768]{0:T(1024)S(1)}, f32[4,512]{1,0:T(4,128)}, f32[4,1024]{1,0:T(4,128)}, f32[2,4]{1,0:T(2,128)S(1)}, /*index=5*/f32[512]{0:T(512)}) all-reduce(f32[4,512]{1,0:T(4,128)S(1)} %copy-done.65, f32[768]{0:T(1024)S(1)} %slice.337, ...), channel_id=1, replica_groups=mesh['row'=8,'col'=4] {'row'}, use_global_device_ids=true, to_apply=%region_10.11 | all-reduce | flops 9480 | bytes 75840 | tf_op jit(solution)/shard_map/psum | solution.py:787
  534.8 3.1 fusion.37
  539.7 13.4 %reduce-scatter.6.cloned.1.call-done = bf16[256,3200]{1,0:T(8,128)(2,1)} async-done(((bf16[2048,3200]{1,0:T(8,128)(2,1)}), bf16[256,3200]{1,0:T(8,128)(2,1)}) %reduce-scatter.6.cloned.1.call-update) | async-done | bytes 1638416 | tf_op jit(solution)/shard_map/reduce_scatter | solution.py:770
  (394 shorter events, 123.4 us)
Async XLA Ops:
  7.2 87.3 %all-gather.4.cloned.1.call-start = ((), (), s32[]{:S(2)}) async-start(), calls=%async_computation.3 | async-start | bytes 14745600 | tf_op jit(solution)/shard_map/all_gather | solution.py:644
  17.2 127.1 %all-gather.6.cloned.1.call-start = ((), (), s32[]{:S(2)}) async-start(), calls=%async_computation.4 | async-start | bytes 4718592 | tf_op jit(solution)/shard_map/all_gather | solution.py:645
  18.0 211.4 %all-gather.8.cloned.1.call-start = ((), (), s32[]{:S(2)}) async-start(), calls=%async_computation.5 | async-start | bytes 19021824 | tf_op jit(solution)/shard_map/all_gather | solution.py:648
  19.6 364.9 %reduce-scatter.4.cloned.1.call-start = ((), (), s32[]{:S(2)}) async-start(), calls=%async_computation.6 | async-start | bytes 12681216 | tf_op jit(solution)/shard_map/reduce_scatter | solution.py:733
  20.3 18.3 %collective-permute-start.4 = (f32[2,512]{1,0:T(2,128)S(1)}, f32[2,512]{1,0:T(2,128)S(1)}, u32[]{:S(2)}, u32[]{:S(2)}) collective-permute-start(f32[2,512]{1,0:T(2,128)S(1)} %get-tuple-element.454), channel_id=1, source_target_pairs={{0,2},{1,3},{2,0},{3,1},{4,6},{5,7},{6,4},{7,5},{8,10},{9,11},{10,... | collective-permute-start | bytes 12296 | tf_op jit(solution)/shard_map/ppermute | solution.py:486
  28.2 35.9 %collective-permute-start.1 = (bf16[512,512]{1,0:T(8,128)(2,1)}, bf16[512,512]{1,0:T(8,128)(2,1)}, u32[]{:S(2)}, u32[]{:S(2)}) collective-permute-start(bf16[512,512]{1,0:T(8,128)(2,1)} %param.21), channel_id=1, source_target_pairs={{0,2},{1,3},{2,0},{3,1},{4,6},{5,7},{6,4},{7,5},{8,10},{9,11},{10,... | collective-permute-start | bytes 1572872 | tf_op jit(solution)/shard_map/ppermute | solution.py:486
  28.2 26.7 %collective-permute-start = (bf16[512,512]{1,0:T(8,128)(2,1)}, bf16[512,512]{1,0:T(8,128)(2,1)}, u32[]{:S(2)}, u32[]{:S(2)}) collective-permute-start(bf16[512,512]{1,0:T(8,128)(2,1)} %param.21), channel_id=1, source_target_pairs={{0,1},{1,2},{2,3},{3,0},{4,5},{5,6},{6,7},{7,4},{8,9},{9,10},{10,1... | collective-permute-start | bytes 1572872 | tf_op jit(solution)/shard_map/ppermute | solution.py:486
  35.2 36.1 %collective-permute-start.2 = (bf16[512,512]{1,0:T(8,128)(2,1)}, bf16[512,512]{1,0:T(8,128)(2,1)S(1)}, u32[]{:S(2)}, u32[]{:S(2)}) collective-permute-start(bf16[512,512]{1,0:T(8,128)(2,1)} %param.21), channel_id=1, source_target_pairs={{0,3},{1,0},{2,1},{3,2},{4,7},{5,4},{6,5},{7,6},{8,11},{9,8},{10,9... | collective-permute-start | bytes 1572872 | tf_op jit(solution)/shard_map/ppermute | solution.py:486
  94.4 49.0 %collective-permute-start.8 = (bf16[512,512]{1,0:T(8,128)(2,1)}, bf16[512,512]{1,0:T(8,128)(2,1)S(1)}, u32[]{:S(2)}, u32[]{:S(2)}) collective-permute-start(bf16[512,512]{1,0:T(8,128)(2,1)} %param.41), channel_id=1, source_target_pairs={{0,3},{1,0},{2,1},{3,2},{4,7},{5,4},{6,5},{7,6},{8,11},{9,8},{10,9... | collective-permute-start | bytes 1572872 | tf_op jit(solution)/shard_map/ppermute | solution.py:486
  97.8 45.6 %collective-permute-start.7 = (bf16[512,512]{1,0:T(8,128)(2,1)}, bf16[512,512]{1,0:T(8,128)(2,1)S(1)}, u32[]{:S(2)}, u32[]{:S(2)}) collective-permute-start(bf16[512,512]{1,0:T(8,128)(2,1)} %param.41), channel_id=1, source_target_pairs={{0,2},{1,3},{2,0},{3,1},{4,6},{5,7},{6,4},{7,5},{8,10},{9,11},{10,... | collective-permute-start | bytes 1572872 | tf_op jit(solution)/shard_map/ppermute | solution.py:486
  97.8 40.5 %collective-permute-start.6 = (bf16[512,512]{1,0:T(8,128)(2,1)}, bf16[512,512]{1,0:T(8,128)(2,1)S(1)}, u32[]{:S(2)}, u32[]{:S(2)}) collective-permute-start(bf16[512,512]{1,0:T(8,128)(2,1)} %param.41), channel_id=1, source_target_pairs={{0,1},{1,2},{2,3},{3,0},{4,5},{5,6},{6,7},{7,4},{8,9},{9,10},{10,1... | collective-permute-start | bytes 1572872 | tf_op jit(solution)/shard_map/ppermute | solution.py:486
  148.9 25.7 %collective-permute-start.10 = (bf16[256,512]{1,0:T(8,128)(2,1)S(1)}, bf16[256,512]{1,0:T(8,128)(2,1)S(1)}, u32[]{:S(2)}, u32[]{:S(2)}) collective-permute-start(bf16[256,512]{1,0:T(8,128)(2,1)S(1)} %get-tuple-element.422), channel_id=1, source_target_pairs={{0,2},{1,3},{2,0},{3,1},{4,6},{5,7},{6,4},{7,5},{8,10},{9,11},{10,... | collective-permute-start | bytes 786440 | tf_op jit(solution)/shard_map/ppermute | solution.py:486
  151.7 22.8 %collective-permute-start.9 = (bf16[256,512]{1,0:T(8,128)(2,1)S(1)}, bf16[256,512]{1,0:T(8,128)(2,1)S(1)}, u32[]{:S(2)}, u32[]{:S(2)}) collective-permute-start(bf16[256,512]{1,0:T(8,128)(2,1)S(1)} %get-tuple-element.423), channel_id=1, source_target_pairs={{0,1},{1,2},{2,3},{3,0},{4,5},{5,6},{6,7},{7,4},{8,9},{9,10},{10,1... | collective-permute-start | bytes 786440 | tf_op jit(solution)/shard_map/ppermute | solution.py:486
  174.5 20.4 %collective-permute-start.13 = (bf16[256,512]{1,0:T(8,128)(2,1)S(1)}, bf16[256,512]{1,0:T(8,128)(2,1)S(1)}, u32[]{:S(2)}, u32[]{:S(2)}) collective-permute-start(bf16[256,512]{1,0:T(8,128)(2,1)S(1)} %get-tuple-element.178), channel_id=1, source_target_pairs={{0,2},{1,3},{2,0},{3,1},{4,6},{5,7},{6,4},{7,5},{8,10},{9,11},{10,... | collective-permute-start | bytes 786440 | tf_op jit(solution)/shard_map/ppermute | solution.py:486
  174.8 20.2 %collective-permute-start.14 = (bf16[256,512]{1,0:T(8,128)(2,1)S(1)}, bf16[256,512]{1,0:T(8,128)(2,1)S(1)}, u32[]{:S(2)}, u32[]{:S(2)}) collective-permute-start(bf16[256,512]{1,0:T(8,128)(2,1)S(1)} %get-tuple-element.179), channel_id=1, source_target_pairs={{0,3},{1,0},{2,1},{3,2},{4,7},{5,4},{6,5},{7,6},{8,11},{9,8},{10,9... | collective-permute-start | bytes 786440 | tf_op jit(solution)/shard_map/ppermute | solution.py:486
  200.9 23.0 %collective-permute-start.16 = (bf16[256,512]{1,0:T(8,128)(2,1)S(1)}, bf16[256,512]{1,0:T(8,128)(2,1)S(1)}, u32[]{:S(2)}, u32[]{:S(2)}) collective-permute-start(bf16[256,512]{1,0:T(8,128)(2,1)S(1)} %convert_element_type.242), channel_id=1, source_target_pairs={{0,2},{1,3},{2,0},{3,1},{4,6},{5,7},{6,4},{7,5},{8,10},{9,11},{10,... | collective-permute-start | bytes 786440 | tf_op jit(solution)/shard_map/ppermute | solution.py:486
  201.6 22.2 %collective-permute-start.15 = (bf16[256,512]{1,0:T(8,128)(2,1)S(1)}, bf16[256,512]{1,0:T(8,128)(2,1)S(1)}, u32[]{:S(2)}, u32[]{:S(2)}) collective-permute-start(bf16[256,512]{1,0:T(8,128)(2,1)S(1)} %convert_element_type.242), channel_id=1, source_target_pairs={{0,1},{1,2},{2,3},{3,0},{4,5},{5,6},{6,7},{7,4},{8,9},{9,10},{10,1... | collective-permute-start | bytes 786440 | tf_op jit(solution)/shard_map/ppermute | solution.py:486
  223.9 21.3 %collective-permute-start.20 = (bf16[256,512]{1,0:T(8,128)(2,1)S(1)}, bf16[256,512]{1,0:T(8,128)(2,1)}, u32[]{:S(2)}, u32[]{:S(2)}) collective-permute-start(bf16[256,512]{1,0:T(8,128)(2,1)S(1)} %convert_element_type.246), channel_id=1, source_target_pairs={{0,3},{1,0},{2,1},{3,2},{4,7},{5,4},{6,5},{7,6},{8,11},{9,8},{10,9... | collective-permute-start | bytes 786440 | tf_op jit(solution)/shard_map/ppermute | solution.py:486
  223.9 24.0 %collective-permute-start.19 = (bf16[256,512]{1,0:T(8,128)(2,1)S(1)}, bf16[256,512]{1,0:T(8,128)(2,1)}, u32[]{:S(2)}, u32[]{:S(2)}) collective-permute-start(bf16[256,512]{1,0:T(8,128)(2,1)S(1)} %convert_element_type.246), channel_id=1, source_target_pairs={{0,2},{1,3},{2,0},{3,1},{4,6},{5,7},{6,4},{7,5},{8,10},{9,11},{10,... | collective-permute-start | bytes 786440 | tf_op jit(solution)/shard_map/ppermute | solution.py:486
  225.4 22.6 %collective-permute-start.18 = (bf16[256,512]{1,0:T(8,128)(2,1)S(1)}, bf16[256,512]{1,0:T(8,128)(2,1)}, u32[]{:S(2)}, u32[]{:S(2)}) collective-permute-start(bf16[256,512]{1,0:T(8,128)(2,1)S(1)} %convert_element_type.246), channel_id=1, source_target_pairs={{0,1},{1,2},{2,3},{3,0},{4,5},{5,6},{6,7},{7,4},{8,9},{9,10},{10,1... | collective-permute-start | bytes 786440 | tf_op jit(solution)/shard_map/ppermute | solution.py:486
  248.0 29.6 %collective-permute-start.26 = (f32[256]{0:T(256)S(1)}, f32[256]{0:T(256)S(1)}, u32[]{:S(2)}, u32[]{:S(2)}) collective-permute-start(f32[256]{0:T(256)S(1)} %get-tuple-element.214), channel_id=1, source_target_pairs={{0,3},{1,0},{2,1},{3,2},{4,7},{5,4},{6,5},{7,6},{8,11},{9,8},{10,9... | collective-permute-start | bytes 3080 | tf_op jit(solution)/shard_map/ppermute | solution.py:486
  248.6 29.5 %collective-permute-start.25 = (f32[256]{0:T(256)S(1)}, f32[256]{0:T(256)S(1)}, u32[]{:S(2)}, u32[]{:S(2)}) collective-permute-start(f32[256]{0:T(256)S(1)} %get-tuple-element.214), channel_id=1, source_target_pairs={{0,2},{1,3},{2,0},{3,1},{4,6},{5,7},{6,4},{7,5},{8,10},{9,11},{10,... | collective-permute-start | bytes 3080 | tf_op jit(solution)/shard_map/ppermute | solution.py:486
  252.0 30.9 %collective-permute-start.21 = (bf16[256,512]{1,0:T(8,128)(2,1)S(1)}, bf16[256,512]{1,0:T(8,128)(2,1)}, u32[]{:S(2)}, u32[]{:S(2)}) collective-permute-start(bf16[256,512]{1,0:T(8,128)(2,1)S(1)} %get-tuple-element.197), channel_id=1, source_target_pairs={{0,1},{1,2},{2,3},{3,0},{4,5},{5,6},{6,7},{7,4},{8,9},{9,10},{10,1... | collective-permute-start | bytes 786440 | tf_op jit(solution)/shard_map/ppermute | solution.py:486
  254.0 28.9 %collective-permute-start.22 = (bf16[256,512]{1,0:T(8,128)(2,1)S(1)}, bf16[256,512]{1,0:T(8,128)(2,1)}, u32[]{:S(2)}, u32[]{:S(2)}) collective-permute-start(bf16[256,512]{1,0:T(8,128)(2,1)S(1)} %get-tuple-element.198), channel_id=1, source_target_pairs={{0,2},{1,3},{2,0},{3,1},{4,6},{5,7},{6,4},{7,5},{8,10},{9,11},{10,... | collective-permute-start | bytes 786440 | tf_op jit(solution)/shard_map/ppermute | solution.py:486
  256.4 26.5 %collective-permute-start.23 = (bf16[256,512]{1,0:T(8,128)(2,1)S(1)}, bf16[256,512]{1,0:T(8,128)(2,1)}, u32[]{:S(2)}, u32[]{:S(2)}) collective-permute-start(bf16[256,512]{1,0:T(8,128)(2,1)S(1)} %get-tuple-element.199), channel_id=1, source_target_pairs={{0,3},{1,0},{2,1},{3,2},{4,7},{5,4},{6,5},{7,6},{8,11},{9,8},{10,9... | collective-permute-start | bytes 786440 | tf_op jit(solution)/shard_map/ppermute | solution.py:486
  291.7 240.9 %reduce-scatter.8.cloned.1.call-start = ((), (), s32[]{:S(2)}) async-start(), calls=%async_computation.8 | async-start | bytes 4718592 | tf_op jit(solution)/shard_map/reduce_scatter | solution.py:760
  292.9 13.5 %collective-permute-start.31 = (f32[256]{0:T(256)S(1)}, f32[256]{0:T(256)S(1)}, u32[]{:S(2)}, u32[]{:S(2)}) collective-permute-start(f32[256]{0:T(256)S(1)} %get-tuple-element.231), channel_id=1, source_target_pairs={{0,2},{1,3},{2,0},{3,1},{4,6},{5,7},{6,4},{7,5},{8,10},{9,11},{10,... | collective-permute-start | bytes 3080 | tf_op jit(solution)/shard_map/ppermute | solution.py:486
  296.4 17.3 %collective-permute-start.28 = (bf16[256,512]{1,0:T(8,128)(2,1)}, bf16[256,512]{1,0:T(8,128)(2,1)S(1)}, u32[]{:S(2)}, u32[]{:S(2)}) collective-permute-start(bf16[256,512]{1,0:T(8,128)(2,1)} %get-tuple-element.206), channel_id=1, source_target_pairs={{0,2},{1,3},{2,0},{3,1},{4,6},{5,7},{6,4},{7,5},{8,10},{9,11},{10,... | collective-permute-start | bytes 786440 | tf_op jit(solution)/shard_map/ppermute | solution.py:486
  300.9 13.6 %collective-permute-start.29 = (bf16[256,512]{1,0:T(8,128)(2,1)}, bf16[256,512]{1,0:T(8,128)(2,1)S(1)}, u32[]{:S(2)}, u32[]{:S(2)}) collective-permute-start(bf16[256,512]{1,0:T(8,128)(2,1)} %get-tuple-element.207), channel_id=1, source_target_pairs={{0,3},{1,0},{2,1},{3,2},{4,7},{5,4},{6,5},{7,6},{8,11},{9,8},{10,9... | collective-permute-start | bytes 786440 | tf_op jit(solution)/shard_map/ppermute | solution.py:486
  314.5 38.1 %collective-permute-start.36 = (bf16[1024,1376]{0,1:T(8,128)(2,1)S(1)}, bf16[1024,1376]{0,1:T(8,128)(2,1)S(1)}, u32[]{:S(2)}, u32[]{:S(2)}) collective-permute-start(bf16[1024,1376]{0,1:T(8,128)(2,1)S(1)} %convolution_convert_fusion.2), channel_id=1, source_target_pairs={{0,4},{4,0},{8,12},{12,8},{16,20},{20,16},{24,28},{28,24},{1,5},{5... | collective-permute-start | bytes 8454152 | tf_op jit(solution)/shard_map/ppermute | solution.py:528
  328.8 23.9 %collective-permute-start.34 = (bf16[256,512]{1,0:T(8,128)(2,1)S(1)}, bf16[256,512]{1,0:T(8,128)(2,1)S(1)}, u32[]{:S(2)}, u32[]{:S(2)}) collective-permute-start(bf16[256,512]{1,0:T(8,128)(2,1)S(1)} %convert_element_type.265), channel_id=1, source_target_pairs={{0,2},{1,3},{2,0},{3,1},{4,6},{5,7},{6,4},{7,5},{8,10},{9,11},{10,... | collective-permute-start | bytes 786440 | tf_op jit(solution)/shard_map/ppermute | solution.py:486
  329.1 23.5 %collective-permute-start.33 = (bf16[256,512]{1,0:T(8,128)(2,1)S(1)}, bf16[256,512]{1,0:T(8,128)(2,1)S(1)}, u32[]{:S(2)}, u32[]{:S(2)}) collective-permute-start(bf16[256,512]{1,0:T(8,128)(2,1)S(1)} %convert_element_type.265), channel_id=1, source_target_pairs={{0,1},{1,2},{2,3},{3,0},{4,5},{5,6},{6,7},{7,4},{8,9},{9,10},{10,1... | collective-permute-start | bytes 786440 | tf_op jit(solution)/shard_map/ppermute | solution.py:486
  352.8 24.8 %collective-permute-start.38 = (bf16[256,512]{1,0:T(8,128)(2,1)S(1)}, bf16[256,512]{1,0:T(8,128)(2,1)S(1)}, u32[]{:S(2)}, u32[]{:S(2)}) collective-permute-start(bf16[256,512]{1,0:T(8,128)(2,1)S(1)} %convert_element_type.270), channel_id=1, source_target_pairs={{0,2},{1,3},{2,0},{3,1},{4,6},{5,7},{6,4},{7,5},{8,10},{9,11},{10,... | collective-permute-start | bytes 786440 | tf_op jit(solution)/shard_map/ppermute | solution.py:486
  354.6 23.0 %collective-permute-start.37 = (bf16[256,512]{1,0:T(8,128)(2,1)S(1)}, bf16[256,512]{1,0:T(8,128)(2,1)S(1)}, u32[]{:S(2)}, u32[]{:S(2)}) collective-permute-start(bf16[256,512]{1,0:T(8,128)(2,1)S(1)} %convert_element_type.270), channel_id=1, source_target_pairs={{0,1},{1,2},{2,3},{3,0},{4,5},{5,6},{6,7},{7,4},{8,9},{9,10},{10,1... | collective-permute-start | bytes 786440 | tf_op jit(solution)/shard_map/ppermute | solution.py:486
  384.6 168.6 %reduce-scatter.6.cloned.1.call-start = ((), (), s32[]{:S(2)}) async-start(), calls=%async_computation.7 | async-start | bytes 14745600 | tf_op jit(solution)/shard_map/reduce_scatter | solution.py:770
  385.7 48.2 %collective-permute-start.40 = (bf16[256,1376]{0,1:T(8,128)(2,1)S(1)}, bf16[256,1376]{0,1:T(8,128)(2,1)S(1)}, u32[]{:S(2)}, u32[]{:S(2)}) collective-permute-start(bf16[256,1376]{0,1:T(8,128)(2,1)S(1)} %pad_maximum_fusion.8), channel_id=1, source_target_pairs={{0,8},{4,12},{8,0},{12,4},{16,24},{20,28},{24,16},{28,20},{1,9},{5... | collective-permute-start | bytes 2113544 | tf_op jit(solution)/shard_map/ppermute | solution.py:528
  387.3 46.6 %collective-permute-start.41 = (bf16[256,1376]{0,1:T(8,128)(2,1)S(1)}, bf16[256,1376]{0,1:T(8,128)(2,1)S(1)}, u32[]{:S(2)}, u32[]{:S(2)}) collective-permute-start(bf16[256,1376]{0,1:T(8,128)(2,1)S(1)} %pad_maximum_fusion.9), channel_id=1, source_target_pairs={{0,16},{4,20},{8,24},{12,28},{16,0},{20,4},{24,8},{28,12},{1,17},{... | collective-permute-start | bytes 2113544 | tf_op jit(solution)/shard_map/ppermute | solution.py:528
  393.8 40.1 %collective-permute-start.42 = (bf16[512,512]{1,0:T(8,128)(2,1)}, bf16[512,512]{1,0:T(8,128)(2,1)S(1)}, u32[]{:S(2)}, u32[]{:S(2)}) collective-permute-start(bf16[512,512]{1,0:T(8,128)(2,1)} %get-tuple-element.269), channel_id=1, source_target_pairs={{0,1},{1,2},{2,3},{3,0},{4,5},{5,6},{6,7},{7,4},{8,9},{9,10},{10,1... | collective-permute-start | bytes 1572872 | tf_op jit(solution)/shard_map/ppermute | solution.py:486
  393.8 40.1 %collective-permute-start.43 = (bf16[512,512]{1,0:T(8,128)(2,1)S(1)}, bf16[512,512]{1,0:T(8,128)(2,1)S(1)}, u32[]{:S(2)}, u32[]{:S(2)}) collective-permute-start(bf16[512,512]{1,0:T(8,128)(2,1)S(1)} %copy-done.46), channel_id=1, source_target_pairs={{0,2},{1,3},{2,0},{3,1},{4,6},{5,7},{6,4},{7,5},{8,10},{9,11},{10,... | collective-permute-start | bytes 1572872 | tf_op jit(solution)/shard_map/ppermute | solution.py:486
  395.3 38.6 %collective-permute-start.44 = (bf16[512,512]{1,0:T(8,128)(2,1)S(1)}, bf16[512,512]{1,0:T(8,128)(2,1)S(1)}, u32[]{:S(2)}, u32[]{:S(2)}) collective-permute-start(bf16[512,512]{1,0:T(8,128)(2,1)S(1)} %copy-done.43), channel_id=1, source_target_pairs={{0,3},{1,0},{2,1},{3,2},{4,7},{5,4},{6,5},{7,6},{8,11},{9,8},{10,9... | collective-permute-start | bytes 1572872 | tf_op jit(solution)/shard_map/ppermute | solution.py:486
  454.4 21.1 %collective-permute-start.46 = (bf16[128,1376]{0,1:T(8,128)(2,1)S(1)}, bf16[128,1376]{0,1:T(8,128)(2,1)S(1)}, u32[]{:S(2)}, u32[]{:S(2)}) collective-permute-start(bf16[128,1376]{0,1:T(8,128)(2,1)S(1)} %get-tuple-element.396), channel_id=1, source_target_pairs={{0,16},{4,20},{8,24},{12,28},{16,0},{20,4},{24,8},{28,12},{1,17},{... | collective-permute-start | bytes 1056776 | tf_op jit(solution)/shard_map/ppermute | solution.py:528
  455.8 19.7 %collective-permute-start.45 = (bf16[128,1376]{0,1:T(8,128)(2,1)S(1)}, bf16[128,1376]{0,1:T(8,128)(2,1)S(1)}, u32[]{:S(2)}, u32[]{:S(2)}) collective-permute-start(bf16[128,1376]{0,1:T(8,128)(2,1)S(1)} %get-tuple-element.397), channel_id=1, source_target_pairs={{0,8},{4,12},{8,0},{12,4},{16,24},{20,28},{24,16},{28,20},{1,9},{5... | collective-permute-start | bytes 1056776 | tf_op jit(solution)/shard_map/ppermute | solution.py:528
  475.5 13.5 %collective-permute-start.50 = (f32[1280]{0:T(1024)S(1)}, f32[1280]{0:T(1024)S(1)}, u32[]{:S(2)}, u32[]{:S(2)}) collective-permute-start(f32[1280]{0:T(1024)S(1)} %get-tuple-element.285), channel_id=1, source_target_pairs={{0,1},{1,2},{2,3},{3,0},{4,5},{5,6},{6,7},{7,4},{8,9},{9,10},{10,1... | collective-permute-start | bytes 15368 | tf_op jit(solution)/shard_map/ppermute | solution.py:486
  482.8 23.0 %collective-permute-start.51 = (f32[1280]{0:T(1024)S(1)}, f32[1280]{0:T(1024)S(1)}, u32[]{:S(2)}, u32[]{:S(2)}) collective-permute-start(f32[1280]{0:T(1024)S(1)} %get-tuple-element.286), channel_id=1, source_target_pairs={{0,2},{1,3},{2,0},{3,1},{4,6},{5,7},{6,4},{7,5},{8,10},{9,11},{10,... | collective-permute-start | bytes 15368 | tf_op jit(solution)/shard_map/ppermute | solution.py:486
  485.4 20.4 %collective-permute-start.52 = (f32[1280]{0:T(1024)S(1)}, f32[1280]{0:T(1024)S(1)}, u32[]{:S(2)}, u32[]{:S(2)}) collective-permute-start(f32[1280]{0:T(1024)S(1)} %get-tuple-element.287), channel_id=1, source_target_pairs={{0,3},{1,0},{2,1},{3,2},{4,7},{5,4},{6,5},{7,6},{8,11},{9,8},{10,9... | collective-permute-start | bytes 15368 | tf_op jit(solution)/shard_map/ppermute | solution.py:486
  485.4 49.4 %collective-permute-start.47 = (bf16[512,512]{1,0:T(8,128)(2,1)}, bf16[512,512]{1,0:T(8,128)(2,1)}, u32[]{:S(2)}, u32[]{:S(2)}) collective-permute-start(bf16[512,512]{1,0:T(8,128)(2,1)} %get-tuple-element.281), channel_id=1, source_target_pairs={{0,1},{1,2},{2,3},{3,0},{4,5},{5,6},{6,7},{7,4},{8,9},{9,10},{10,1... | collective-permute-start | bytes 1572872 | tf_op jit(solution)/shard_map/ppermute | solution.py:486
  487.5 47.3 %collective-permute-start.48 = (bf16[512,512]{1,0:T(8,128)(2,1)}, bf16[512,512]{1,0:T(8,128)(2,1)}, u32[]{:S(2)}, u32[]{:S(2)}) collective-permute-start(bf16[512,512]{1,0:T(8,128)(2,1)} %get-tuple-element.282), channel_id=1, source_target_pairs={{0,2},{1,3},{2,0},{3,1},{4,6},{5,7},{6,4},{7,5},{8,10},{9,11},{10,... | collective-permute-start | bytes 1572872 | tf_op jit(solution)/shard_map/ppermute | solution.py:486
  489.0 45.8 %collective-permute-start.49 = (bf16[512,512]{1,0:T(8,128)(2,1)}, bf16[512,512]{1,0:T(8,128)(2,1)}, u32[]{:S(2)}, u32[]{:S(2)}) collective-permute-start(bf16[512,512]{1,0:T(8,128)(2,1)} %get-tuple-element.283), channel_id=1, source_target_pairs={{0,3},{1,0},{2,1},{3,2},{4,7},{5,4},{6,5},{7,6},{8,11},{9,8},{10,9... | collective-permute-start | bytes 1572872 | tf_op jit(solution)/shard_map/ppermute | solution.py:486
  (89 other events, 876.9 us)
Sparse Core Ops, SparseCore 0:
  17.4 77.0 all-gather.3
  96.3 37.4 all-gather.5
  135.7 93.6 all-gather.7
  291.8 82.6 reduce-scatter.3
  384.7 49.1 reduce-scatter.7
  451.7 101.3 reduce-scatter.5

commit v3 on v2

--- a/solution.py
+++ b/solution.py
@@ -110,27 +110,30 @@
     return totals
 
 
-def head_inputs(pres, taps_refs, marks):
-    query_taps, key_taps, value_taps = taps_refs
-    dk = pres[0].shape[1]
-    x = jnp.concatenate(pres, axis=1)
-    taps = jnp.concatenate([query_taps[...], key_taps[...], value_taps[...]], axis=1)
-    total, gate = conv_act(x, taps, marks)
-    act = total * gate
-    query_act, key_act, values = act[:, :dk], act[:, dk : 2 * dk], act[:, 2 * dk :]
-    query_scale = lax.rsqrt(jnp.sum(query_act * query_act, axis=1, keepdims=True) + 1e-06)
-    key_scale = lax.rsqrt(jnp.sum(key_act * key_act, axis=1, keepdims=True) + 1e-06)
-    return x, taps, total, gate, query_act, key_act, values, query_scale, key_scale
-
-
-def forward_kernel(heads, hidden_ref, query_weight, key_weight, value_weight, gate_weight, small_weight,
+def head_inputs(pres, taps_refs, marks, dk, dv):
+    heads = []
+    for at in range(pres[0].shape[1] // dk):
+        keyed, valued = slice(at * dk, (at + 1) * dk), slice(at * dv, (at + 1) * dv)
+        spans = (keyed, keyed, valued)
+        x = jnp.concatenate([pre[:, span] for pre, span in zip(pres, spans)], axis=1)
+        taps = jnp.concatenate([ref[:, span] for ref, span in zip(taps_refs, spans)], axis=1)
+        total, gate = conv_act(x, taps, marks)
+        act = total * gate
+        query_act, key_act, values = act[:, :dk], act[:, dk : 2 * dk], act[:, 2 * dk :]
+        query_scale = lax.rsqrt(jnp.sum(query_act * query_act, axis=1, keepdims=True) + 1e-06)
+        key_scale = lax.rsqrt(jnp.sum(key_act * key_act, axis=1, keepdims=True) + 1e-06)
+        heads.append((x, taps, total, gate, query_act, key_act, values, query_scale, key_scale))
+    return heads
+
+
+def forward_kernel(heads, dk, dv, hidden_ref, query_weight, key_weight, value_weight, gate_weight, small_weight,
                    query_taps, key_taps, value_taps, marks_ref, segs_ref, params_ref, gain_ref,
                    query_ref, key_ref, value_ref, gate_ref, small_ref,
                    mixed_ref, out_ref, fresh_ref, mats_ref, states_ref):
-    head = pl.program_id(0)
+    each = heads // 2
     hidden = hidden_ref[...]
 
-    @pl.when(head == 0)
+    @pl.when(pl.program_id(0) == 0)
     def _():
         small_ref[...] = dot(hidden, small_weight[...])
 
@@ -139,68 +142,81 @@
     value_ref[...] = dot(hidden, value_weight[...])
     gate_ref[...] = dot(hidden, gate_weight[...])
     marks = marks_ref[...]
-    _, _, _, _, query_act, key_act, values, query_scale, key_scale = head_inputs(
-        [query_ref[...], key_ref[...], value_ref[...]], (query_taps, key_taps, value_taps), marks
-    )
-    tokens, dk = query_act.shape
-    queries = query_act * (query_scale * dk ** -0.5)
-    keys = key_act * key_scale
-    log_decay, beta = decays(small_ref[...], params_ref[...], head, heads)
+    small, params = small_ref[...], params_ref[...]
+    tokens = hidden.shape[0]
     rows, cols = grids()
     blocks = tokens // BLOCK
     cuts = [slice(index * BLOCK, (index + 1) * BLOCK) for index in range(blocks)]
-    key_parts = [split(keys[at]) for at in cuts]
-    query_parts = [split(queries[at]) for at in cuts]
-    decay_pairs = [
-        block_decay(
-            log_decay[at], head, rows, cols, marks[at, 6:7], segs_ref[0:1, at],
-            marks[index * BLOCK - 1 : index * BLOCK, 6:7] if index else None,
-        )
-        for index, at in enumerate(cuts)
-    ]
-    inners = [
-        jnp.where(rows > cols, dot3(key, key, 1, 1) * pair_of[0], 0.0) for key, pair_of in zip(key_parts, decay_pairs)
-    ]
-    scores = [dot3(query, key, 1, 1) * pair_of[0] for query, key, pair_of in zip(query_parts, key_parts, decay_pairs)]
-    inverses = unit_inverses([beta[at] * inner for at, inner in zip(cuts, inners)], rows, cols)
-    state = None
-    for index, at in enumerate(cuts):
-        decay, carried = decay_pairs[index]
-        inner, score, inverse = inners[index], scores[index], inverses[index]
-        value, strength = values[at], beta[at]
-        mats_ref[at, 0:BLOCK] = inner
-        mats_ref[at, BLOCK : 2 * BLOCK] = score
-        mats_ref[at, 2 * BLOCK :] = inverse
-        if index:
-            state_parts = split(state)
-            source = strength * (value - carried * dot3(key_parts[index], state_parts))
-        else:
-            source = strength * value
-        fresh = dot3(split(inverse), split(source))
-        fresh_parts = split(fresh)
-        output = dot3(split(score), fresh_parts)
-        if index:
-            output = output + carried * dot3(query_parts[index], state_parts)
-        if index + 1 < blocks:
-            grown = dot3(split(keys[at] * lane_pick_row(decay)), fresh_parts, 0, 0)
-            state = grown if state is None else carried[BLOCK - 1 : BLOCK] * state + grown
-            states_ref[index * dk : (index + 1) * dk, :] = state
-        fresh_ref[at, :] = fresh
-        out_ref[at, :] = output
-        scale = lax.rsqrt(jnp.mean(output * output, axis=1, keepdims=True) + 1e-05)
-        gate_pre = gate_ref[at, :]
-        mixed_ref[at, :] = (output * scale * gain_ref[0:1] * (gate_pre * sigmoid(gate_pre))).astype(BF)
+    own = []
+    for at, parts in enumerate(
+        head_inputs([query_ref[...], key_ref[...], value_ref[...]], (query_taps, key_taps, value_taps), marks, dk, dv)
+    ):
+        _, _, _, _, query_act, key_act, values, query_scale, key_scale = parts
+        head = pl.program_id(0) * each + at
+        queries = query_act * (query_scale * dk ** -0.5)
+        keys = key_act * key_scale
+        log_decay, beta = decays(small, params, head, heads)
+        key_parts = [split(keys[cut]) for cut in cuts]
+        query_parts = [split(queries[cut]) for cut in cuts]
+        decay_pairs = [
+            block_decay(
+                log_decay[cut], head, rows, cols, marks[cut, 6:7], segs_ref[0:1, cut],
+                marks[index * BLOCK - 1 : index * BLOCK, 6:7] if index else None,
+            )
+            for index, cut in enumerate(cuts)
+        ]
+        inners = [
+            jnp.where(rows > cols, dot3(key, key, 1, 1) * two[0], 0.0) for key, two in zip(key_parts, decay_pairs)
+        ]
+        scores = [dot3(query, key, 1, 1) * two[0] for query, key, two in zip(query_parts, key_parts, decay_pairs)]
+        own.append((keys, values, beta, key_parts, query_parts, decay_pairs, inners, scores))
+    lowers = [head[2][cut] * inner for head in own for cut, inner in zip(cuts, head[6])]
+    inverses = unit_inverses(lowers, rows, cols)
+    states = [None] * each
+    for index, cut in enumerate(cuts):
+        for at, (keys, values, beta, key_parts, query_parts, decay_pairs, inners, scores) in enumerate(own):
+            decay, carried = decay_pairs[index]
+            score, inverse = scores[index], inverses[at * blocks + index]
+            value, strength = values[cut], beta[cut]
+            valued = slice(at * dv, (at + 1) * dv)
+            mats_ref[cut, (3 * at) * BLOCK : (3 * at + 1) * BLOCK] = inners[index]
+            mats_ref[cut, (3 * at + 1) * BLOCK : (3 * at + 2) * BLOCK] = score
+            mats_ref[cut, (3 * at + 2) * BLOCK : (3 * at + 3) * BLOCK] = inverse
+            if index:
+                state_parts = split(states[at])
+                source = strength * (value - carried * dot3(key_parts[index], state_parts))
+            else:
+                source = strength * value
+            fresh = dot3(split(inverse), split(source))
+            fresh_parts = split(fresh)
+            output = dot3(split(score), fresh_parts)
+            if index:
+                output = output + carried * dot3(query_parts[index], state_parts)
+            if index + 1 < blocks:
+                grown = dot3(split(keys[cut] * lane_pick_row(decay)), fresh_parts, 0, 0)
+                states[at] = grown if index == 0 else carried[BLOCK - 1 : BLOCK] * states[at] + grown
+                states_ref[index * dk : (index + 1) * dk, valued] = states[at]
+            fresh_ref[cut, valued] = fresh
+            out_ref[cut, valued] = output
+            scale = lax.rsqrt(jnp.mean(output * output, axis=1, keepdims=True) + 1e-05)
+            gate_pre = gate_ref[cut, valued]
+            mixed_ref[cut, valued] = (output * scale * gain_ref[0:1] * (gate_pre * sigmoid(gate_pre))).astype(BF)
 
 
 def lane_pick_row(decay):
     return decay.T[:, BLOCK - 1 : BLOCK]
 
 
-def backward_kernel(heads, first, query_ref, key_ref, value_ref, gate_ref, small_ref, query_taps, key_taps, value_taps,
+def in_turn(steps):
+    while steps:
+        steps = [step for step in steps if next(step, steps) is not steps]
+
+
+def backward_kernel(heads, dk, dv, query_ref, key_ref, value_ref, gate_ref, small_ref, query_taps, key_taps, value_taps,
                     marks_ref, segs_ref, params_ref, gain_ref, grad_ref, out_ref, fresh_ref, mats_ref, states_ref,
                     low_query_ref, low_key_ref, low_value_ref, low_gate_ref, low_small_ref,
                     query_taps_grad, key_taps_grad, value_taps_grad, params_grad_ref, gain_grad_ref):
-    head = first + pl.program_id(0)
+    each = heads // 2
 
     @pl.when(pl.program_id(0) == 0)
     def _():
@@ -209,65 +225,116 @@
         gain_grad_ref[...] = jnp.zeros_like(gain_grad_ref)
 
     marks = marks_ref[...]
-    x, taps, total, gate, query_act, key_act, values, query_scale, key_scale = head_inputs(
-        [query_ref[...], key_ref[...], value_ref[...]], (query_taps, key_taps, value_taps), marks
-    )
-    tokens, dk = query_act.shape
-    dv = values.shape[1]
-    queries = query_act * (query_scale * dk ** -0.5)
-    keys = key_act * key_scale
     small = small_ref[...]
     params = params_ref[...]
-    log_decay, beta = decays(small, params, head, heads)
+    inputs = head_inputs(
+        [query_ref[...], key_ref[...], value_ref[...]], (query_taps, key_taps, value_taps), marks, dk, dv
+    )
+    tokens = small.shape[0]
     rows, cols = grids()
     gain = gain_ref[0:1]
     blocks = tokens // BLOCK
     upper = (rows <= cols).astype(BF)
-    d_state = None
-    d_query, d_key, d_value, d_beta, d_decay = [None] * blocks, [None] * blocks, [None] * blocks, [None] * blocks, [None] * blocks
-    d_gain = jnp.zeros((1, dv), F32)
-    for index in reversed(range(blocks)):
-        at = slice(index * BLOCK, (index + 1) * BLOCK)
-        grad = grad_ref[at, :]
-        output = out_ref[at, :]
-        gate_pre = gate_ref[at, :]
+    at_last = lax.broadcasted_iota(jnp.int32, (BLOCK, 1), 0) == BLOCK - 1
+    own = []
+    for at, (_, _, _, _, query_act, key_act, values, query_scale, key_scale) in enumerate(inputs):
+        head = pl.program_id(0) * each + at
+        own.append(
+            (head, query_act * (query_scale * dk ** -0.5), key_act * key_scale, values)
+            + decays(small, params, head, heads)
+        )
+    d_states = [None] * each
+    d_query = [[None] * blocks for _ in range(each)]
+    d_key = [[None] * blocks for _ in range(each)]
+    d_value = [[None] * blocks for _ in range(each)]
+    d_beta = [[None] * blocks for _ in range(each)]
+    d_decay = [[None] * blocks for _ in range(each)]
+    kept = {}
+    gain_sums = []
+
+    def before(index, at):
+        head, queries, keys, values, log_decay, beta = own[at]
+        cut = slice(index * BLOCK, (index + 1) * BLOCK)
+        valued = slice(at * dv, (at + 1) * dv)
+        grad = grad_ref[cut, valued]
+        output = out_ref[cut, valued]
+        gate_pre = gate_ref[cut, valued]
         gate_sig = sigmoid(gate_pre)
         gate_act = gate_pre * gate_sig
         scale = lax.rsqrt(jnp.mean(output * output, axis=1, keepdims=True) + 1e-05)
         normed = output * scale
         both = grad * normed
-        d_gain = d_gain + jnp.sum(both * gate_act, axis=0, keepdims=True)
-        low_gate_ref[at, :] = (
-            both * gain * (gate_sig + gate_act * (1.0 - gate_sig))
-        ).astype(BF)
+        gain_sums.append(jnp.sum(both * gate_act, axis=0, keepdims=True))
+        low_gate_ref[cut, valued] = (both * gain * (gate_sig + gate_act * (1.0 - gate_sig))).astype(BF)
         pulled = grad * gate_act * gain
         d_out = scale * (pulled - normed * jnp.mean(pulled * normed, axis=1, keepdims=True))
-
-        seg_col, seg_row = marks[at, 6:7], segs_ref[0:1, at]
+        yield
         last_seg = marks[index * BLOCK - 1 : index * BLOCK, 6:7] if index else None
-        decay, carried = block_decay(log_decay[at], head, rows, cols, seg_col, seg_row, last_seg)
-        key, query, value, strength = keys[at], queries[at], values[at], beta[at]
-        inner, score, inverse = mats_ref[at, 0:BLOCK], mats_ref[at, BLOCK : 2 * BLOCK], mats_ref[at, 2 * BLOCK :]
-        fresh_parts = split(fresh_ref[at, :])
-        key_parts, query_parts = split(key), split(query)
+        decay, carried = block_decay(
+            log_decay[cut], head, rows, cols, marks[cut, 6:7], segs_ref[0:1, cut], last_seg
+        )
+        yield
+        score = mats_ref[cut, (3 * at + 1) * BLOCK : (3 * at + 2) * BLOCK]
+        fresh_parts = split(fresh_ref[cut, valued])
         out_parts = split(d_out)
         d_fresh = dot3(split(score), out_parts, 0, 0)
+        d_score = dot3(out_parts, fresh_parts, 1, 1)
+        yield
+        key, query = keys[cut], queries[cut]
+        key_parts, query_parts = split(key), split(query)
+        change = d_score * score
+        d_scores = split(d_score * decay)
+        dq = dot3(d_scores, key_parts)
+        dk_ = dot3(d_scores, query_parts, 0, 0)
+        yield
+        state_parts, d_carried, from_query = None, None, None
+        if index:
+            state_parts = split(states_ref[(index - 1) * dk : index * dk, valued])
+            out_back = dot3(out_parts, state_parts, 1, 1)
+            from_query = dot3(query_parts, split(carried * d_out), 0, 0)
+            d_carried = jnp.sum(query * out_back, axis=1, keepdims=True)
+            dq = dq + carried * out_back
+        d_query[at][index] = dq
+        kept[index, at] = (decay, carried, fresh_parts, key_parts, d_fresh, change, dk_, state_parts, d_carried, from_query)
+
+    def through(index, at):
+        _, _, keys, _, _, beta = own[at]
+        cut = slice(index * BLOCK, (index + 1) * BLOCK)
+        decay, carried, _, key_parts, d_fresh, _, _, _, _, from_query = kept[index, at]
+        inverse = mats_ref[cut, (3 * at + 2) * BLOCK : (3 * at + 3) * BLOCK]
+        d_state, tail, state_grad_parts = d_states[at], None, None
         if d_state is not None:
             tail = lane_pick_row(decay)
             state_grad_parts = split(d_state)
-            d_fresh = d_fresh + dot3(split(key * tail), state_grad_parts)
+            d_fresh = d_fresh + dot3(split(keys[cut] * tail), state_grad_parts)
+        yield
         d_source = dot3(split(inverse), split(d_fresh), 0, 0)
+        yield
+        if index:
+            new_state = from_query - dot3(key_parts, split((beta[cut] * carried) * d_source), 0, 0)
+            d_states[at] = new_state if d_state is None else new_state + carried[BLOCK - 1 : BLOCK] * d_state
+        kept[index, at] += (d_state, tail, state_grad_parts, d_source)
+
+    def behind(index, at):
+        _, _, keys, values, _, beta = own[at]
+        cut = slice(index * BLOCK, (index + 1) * BLOCK)
+        valued = slice(at * dv, (at + 1) * dv)
+        (decay, carried, fresh_parts, key_parts, _, change, dk_, state_parts, d_carried, _,
+         d_state, tail, state_grad_parts, d_source) = kept.pop((index, at))
+        key, strength = keys[cut], beta[cut]
+        inner = mats_ref[cut, (3 * at) * BLOCK : (3 * at + 1) * BLOCK]
         source_parts = split(d_source)
-        d_score = dot3(out_parts, fresh_parts, 1, 1)
         d_lower = jnp.where(rows > cols, -dot3(source_parts, fresh_parts, 1, 1), 0.0)
-        d_value[index] = strength * d_source
-        d_strength = jnp.sum(d_source * value, axis=1, keepdims=True) + jnp.sum(d_lower * inner, axis=1, keepdims=True)
-        change = d_score * score + d_lower * (strength * inner)
+        yield
+        d_value[at][index] = strength * d_source
+        d_strength = jnp.sum(d_source * values[cut], axis=1, keepdims=True) + jnp.sum(
+            d_lower * inner, axis=1, keepdims=True
+        )
+        change = change + d_lower * (strength * inner)
         d_run = jnp.sum(change, axis=1, keepdims=True) - jnp.sum(change.T, axis=1, keepdims=True)
-        d_scores = split(d_score * decay)
         d_inners = split(d_lower * (strength * decay))
-        dq = dot3(d_scores, key_parts)
-        dk_ = dot3(d_inners, key_parts) + dot3(d_inners, key_parts, 0, 0) + dot3(d_scores, query_parts, 0, 0)
+        dk_ = dk_ + dot3(d_inners, key_parts) + dot3(d_inners, key_parts, 0, 0)
+        yield
         last_extra = None
         if d_state is not None:
             moved = dot3(fresh_parts, state_grad_parts, 1, 1)
@@ -275,65 +342,67 @@
             d_tail = jnp.sum(key * moved, axis=1, keepdims=True) * tail
             d_run = d_run - d_tail
             last_extra = jnp.sum(d_tail, axis=0, keepdims=True)
+        yield
         if index:
-            state = states_ref[(index - 1) * dk : index * dk, :]
-            state_parts = split(state)
-            out_back = dot3(out_parts, state_parts, 1, 1)
             source_back = dot3(source_parts, state_parts, 1, 1)
             key_source = jnp.sum(key * source_back, axis=1, keepdims=True)
-            d_carried = jnp.sum(query * out_back, axis=1, keepdims=True) - strength * key_source
             d_strength = d_strength - carried * key_source
-            dq = dq + carried * out_back
             dk_ = dk_ - (strength * carried) * source_back
-            d_run = d_run + d_carried * carried
-            keep = carried[BLOCK - 1 : BLOCK]
-            new_state = dot3(query_parts, split(carried * d_out), 0, 0) - dot3(
-                key_parts, split((strength * carried) * d_source), 0, 0
-            )
+            d_run = d_run + (d_carried - strength * key_source) * carried
             if d_state is not None:
-                kept = jnp.sum(jnp.sum(state * d_state, axis=1, keepdims=True), axis=0, keepdims=True)
-                last_extra = last_extra + kept * keep
-                new_state = new_state + keep * d_state
-            d_state = new_state
+                state = states_ref[(index - 1) * dk : index * dk, valued]
+                kept_sum = jnp.sum(jnp.sum(state * d_state, axis=1, keepdims=True), axis=0, keepdims=True)
+                last_extra = last_extra + kept_sum * carried[BLOCK - 1 : BLOCK]
         if last_extra is not None:
-            at_last = lax.broadcasted_iota(jnp.int32, (BLOCK, 1), 0) == BLOCK - 1
             d_run = d_run + jnp.where(at_last, last_extra, 0.0)
-        d_decay[index] = dotx(upper, jnp.broadcast_to(d_run, (BLOCK, BLOCK)))[:, 0:1]
-        d_query[index], d_key[index], d_beta[index] = dq, dk_, d_strength
-
-    dq = jnp.concatenate(d_query, axis=0) * dk ** -0.5
-    dk_ = jnp.concatenate(d_key, axis=0)
-    dv_ = jnp.concatenate(d_value, axis=0)
-    query_pull = jnp.sum(dq * query_act, axis=1, keepdims=True)
-    key_pull = jnp.sum(dk_ * key_act, axis=1, keepdims=True)
-    d_query_act = query_scale * (dq - query_act * (query_scale * query_scale * query_pull))
-    d_key_act = key_scale * (dk_ - key_act * (key_scale * key_scale * key_pull))
-    d_act = jnp.concatenate([d_query_act, d_key_act, dv_], axis=1)
-    d_total = d_act * (gate * (1.0 + total * (1.0 - gate)))
-    d_pre = d_total * taps[3:4]
-    tap_sums = [None, None, None, jnp.sum(d_total * x, axis=0, keepdims=True)]
-    for shift in (1, 2, 3):
-        moved = marks[:, 2 + shift : 3 + shift] * pltpu.roll(d_total, tokens - shift, 0)
-        d_pre = d_pre + moved * taps[3 - shift : 4 - shift]
-        tap_sums[3 - shift] = jnp.sum(moved * x, axis=0, keepdims=True)
-    d_pre = d_pre.astype(BF)
-    low_query_ref[...] = d_pre[:, :dk]
-    low_key_ref[...] = d_pre[:, dk : 2 * dk]
-    low_value_ref[...] = d_pre[:, 2 * dk :]
-    for tap in range(4):
-        query_taps_grad[tap : tap + 1, :] = tap_sums[tap][:, :dk]
-        key_taps_grad[tap : tap + 1, :] = tap_sums[tap][:, dk : 2 * dk]
-        value_taps_grad[tap : tap + 1, :] = tap_sums[tap][:, 2 * dk :]
-
-    d_log = jnp.concatenate(d_decay, axis=0)
-    d_str = jnp.concatenate(d_beta, axis=0)
+        yield
+        d_decay[at][index] = dotx(upper, jnp.broadcast_to(d_run, (BLOCK, BLOCK)))[:, 0:1]
+        d_key[at][index], d_beta[at][index] = dk_, d_strength
+
+    backwards = list(reversed(range(blocks)))
+    for index in backwards:
+        in_turn([before(index, at) for at in range(each)])
+    for index in backwards:
+        in_turn([through(index, at) for at in range(each)])
+    for index in backwards:
+        in_turn([behind(index, at) for at in range(each)])
+    d_gain = sum(gain_sums)
+
     lane = lax.broadcasted_iota(jnp.int32, small.shape, 1)
     rate = jnp.exp(params[0:1])
-    d_decay_pre = jnp.where(lane == head, d_log * (-rate) * sigmoid(small + params[1:2]), 0.0)
-    d_beta_pre = jnp.where(lane == heads + head, d_str * beta * (1.0 - beta), 0.0)
-    low_small_ref[...] += (d_decay_pre + d_beta_pre).astype(BF)
-    params_grad_ref[0:1, :] += jnp.sum(jnp.where(lane == head, d_log * log_decay, 0.0), axis=0, keepdims=True)
-    params_grad_ref[1:2, :] += jnp.sum(d_decay_pre, axis=0, keepdims=True)
+    for at, (x, taps, total, gate, query_act, key_act, values, query_scale, key_scale) in enumerate(inputs):
+        head, _, _, _, log_decay, beta = own[at]
+        keyed, valued = slice(at * dk, (at + 1) * dk), slice(at * dv, (at + 1) * dv)
+        dq = jnp.concatenate(d_query[at], axis=0) * dk ** -0.5
+        dk_ = jnp.concatenate(d_key[at], axis=0)
+        dv_ = jnp.concatenate(d_value[at], axis=0)
+        query_pull = jnp.sum(dq * query_act, axis=1, keepdims=True)
+        key_pull = jnp.sum(dk_ * key_act, axis=1, keepdims=True)
+        d_query_act = query_scale * (dq - query_act * (query_scale * query_scale * query_pull))
+        d_key_act = key_scale * (dk_ - key_act * (key_scale * key_scale * key_pull))
+        d_act = jnp.concatenate([d_query_act, d_key_act, dv_], axis=1)
+        d_total = d_act * (gate * (1.0 + total * (1.0 - gate)))
+        d_pre = d_total * taps[3:4]
+        tap_sums = [None, None, None, jnp.sum(d_total * x, axis=0, keepdims=True)]
+        for shift in (1, 2, 3):
+            moved = marks[:, 2 + shift : 3 + shift] * pltpu.roll(d_total, tokens - shift, 0)
+            d_pre = d_pre + moved * taps[3 - shift : 4 - shift]
+            tap_sums[3 - shift] = jnp.sum(moved * x, axis=0, keepdims=True)
+        d_pre = d_pre.astype(BF)
+        low_query_ref[:, keyed] = d_pre[:, :dk]
+        low_key_ref[:, keyed] = d_pre[:, dk : 2 * dk]
+        low_value_ref[:, valued] = d_pre[:, 2 * dk :]
+        for tap in range(4):
+            query_taps_grad[tap : tap + 1, keyed] = tap_sums[tap][:, :dk]
+            key_taps_grad[tap : tap + 1, keyed] = tap_sums[tap][:, dk : 2 * dk]
+            value_taps_grad[tap : tap + 1, valued] = tap_sums[tap][:, 2 * dk :]
+        d_log = jnp.concatenate(d_decay[at], axis=0)
+        d_str = jnp.concatenate(d_beta[at], axis=0)
+        d_decay_pre = jnp.where(lane == head, d_log * (-rate) * sigmoid(small + params[1:2]), 0.0)
+        d_beta_pre = jnp.where(lane == heads + head, d_str * beta * (1.0 - beta), 0.0)
+        low_small_ref[...] += (d_decay_pre + d_beta_pre).astype(BF)
+        params_grad_ref[0:1, :] += jnp.sum(jnp.where(lane == head, d_log * log_decay, 0.0), axis=0, keepdims=True)
+        params_grad_ref[1:2, :] += jnp.sum(d_decay_pre, axis=0, keepdims=True)
     gain_grad_ref[0:1, :] += d_gain
 
 
@@ -341,16 +410,16 @@
     return (0, 0)
 
 
-def of_head(first):
-    return lambda h: (0, first + h)
-
-
-def shared_specs(tokens, dk, dv, first):
-    own = of_head(first)
+def own_half(g):
+    return (0, g)
+
+
+def shared_specs(tokens, heads, dk, dv):
+    each = heads // 2
     return [
-        pl.BlockSpec((4, dk), own),
-        pl.BlockSpec((4, dk), own),
-        pl.BlockSpec((4, dv), own),
+        pl.BlockSpec((4, each * dk), own_half),
+        pl.BlockSpec((4, each * dk), own_half),
+        pl.BlockSpec((4, each * dv), own_half),
         pl.BlockSpec((tokens, 8), whole),
         pl.BlockSpec((8, tokens), whole),
         pl.BlockSpec((8, 128), whole),
@@ -358,25 +427,25 @@
     ]
 
 
-def pre_specs(tokens, dk, dv, first):
-    own = of_head(first)
+def pre_specs(tokens, heads, dk, dv):
+    each = heads // 2
     return [
-        pl.BlockSpec((tokens, dk), own),
-        pl.BlockSpec((tokens, dk), own),
-        pl.BlockSpec((tokens, dv), own),
-        pl.BlockSpec((tokens, dv), own),
+        pl.BlockSpec((tokens, each * dk), own_half),
+        pl.BlockSpec((tokens, each * dk), own_half),
+        pl.BlockSpec((tokens, each * dv), own_half),
+        pl.BlockSpec((tokens, each * dv), own_half),
         pl.BlockSpec((tokens, 128), whole),
     ]
 
 
-def saved_specs(tokens, dk, dv, first):
-    own = of_head(first)
+def saved_specs(tokens, heads, dk, dv):
+    each = heads // 2
     blocks = tokens // BLOCK
     return [
-        pl.BlockSpec((tokens, dv), own),
-        pl.BlockSpec((tokens, dv), own),
-        pl.BlockSpec((tokens, 3 * BLOCK), own),
-        pl.BlockSpec(((blocks - 1) * dk, dv), own),
+        pl.BlockSpec((tokens, each * dv), own_half),
+        pl.BlockSpec((tokens, each * dv), own_half),
+        pl.BlockSpec((tokens, each * 3 * BLOCK), own_half),
+        pl.BlockSpec(((blocks - 1) * dk, each * dv), own_half),
     ]
 
 
@@ -386,24 +455,24 @@
     each = heads // 2
     wide = 2 * dk + 2 * dv
 
-    def columns(size, before):
-        return lambda h: (0, (h // each * each * wide + each * before) // size + h % each)
+    def columns(before):
+        return lambda g: (0, before + g)
 
     return pl.pallas_call(
-        functools.partial(forward_kernel, heads),
-        grid=(heads,),
+        functools.partial(forward_kernel, heads, dk, dv),
+        grid=(2,),
         in_specs=[
             pl.BlockSpec((tokens, model), whole),
-            pl.BlockSpec((model, dk), columns(dk, 0)),
-            pl.BlockSpec((model, dk), columns(dk, dk)),
-            pl.BlockSpec((model, dv), columns(dv, 2 * dk)),
-            pl.BlockSpec((model, dv), columns(dv, 2 * dk + dv)),
-            pl.BlockSpec((model, 128), lambda h: (0, heads * wide // 128)),
+            pl.BlockSpec((model, each * dk), columns(0)),
+            pl.BlockSpec((model, each * dk), columns(2)),
+            pl.BlockSpec((model, each * dv), columns(4 * dk // dv)),
+            pl.BlockSpec((model, each * dv), columns(4 * dk // dv + 2)),
+            pl.BlockSpec((model, 128), lambda g: (0, heads * wide // 128)),
         ]
-        + shared_specs(tokens, dk, dv, 0),
-        out_specs=pre_specs(tokens, dk, dv, 0)
-        + [pl.BlockSpec((tokens, dv), of_head(0))]
-        + saved_specs(tokens, dk, dv, 0),
+        + shared_specs(tokens, heads, dk, dv),
+        out_specs=pre_specs(tokens, heads, dk, dv)
+        + [pl.BlockSpec((tokens, each * dv), own_half)]
+        + saved_specs(tokens, heads, dk, dv),
         out_shape=[
             jax.ShapeDtypeStruct((tokens, heads * dk), F32),
             jax.ShapeDtypeStruct((tokens, heads * dk), F32),
@@ -422,37 +491,37 @@
     )(hidden, weight, weight, weight, weight, weight, *shared)
 
 
-def mixer_backward(heads, dk, dv, pres, shared, grad, saved, first, count):
+def mixer_backward(heads, dk, dv, pres, shared, grad, saved):
     tokens = grad.shape[0]
-    own = of_head(0)
+    each = heads // 2
     return pl.pallas_call(
-        functools.partial(backward_kernel, heads, first),
-        grid=(count,),
-        in_specs=pre_specs(tokens, dk, dv, first)
-        + shared_specs(tokens, dk, dv, first)
-        + [pl.BlockSpec((tokens, dv), of_head(first))]
-        + saved_specs(tokens, dk, dv, first),
+        functools.partial(backward_kernel, heads, dk, dv),
+        grid=(2,),
+        in_specs=pre_specs(tokens, heads, dk, dv)
+        + shared_specs(tokens, heads, dk, dv)
+        + [pl.BlockSpec((tokens, each * dv), own_half)]
+        + saved_specs(tokens, heads, dk, dv),
         out_specs=[
-            pl.BlockSpec((tokens, dk), own),
-            pl.BlockSpec((tokens, dk), own),
-            pl.BlockSpec((tokens, dv), own),
-            pl.BlockSpec((tokens, dv), own),
+            pl.BlockSpec((tokens, each * dk), own_half),
+            pl.BlockSpec((tokens, each * dk), own_half),
+            pl.BlockSpec((tokens, each * dv), own_half),
+            pl.BlockSpec((tokens, each * dv), own_half),
             pl.BlockSpec((tokens, 128), whole),
-            pl.BlockSpec((4, dk), own),
-            pl.BlockSpec((4, dk), own),
-            pl.BlockSpec((4, dv), own),
+            pl.BlockSpec((4, each * dk), own_half),
+            pl.BlockSpec((4, each * dk), own_half),
+            pl.BlockSpec((4, each * dv), own_half),
             pl.BlockSpec((8, 128), whole),
             pl.BlockSpec((8, dv), whole),
         ],
         out_shape=[
-            jax.ShapeDtypeStruct((tokens, count * dk), BF),
-            jax.ShapeDtypeStruct((tokens, count * dk), BF),
-            jax.ShapeDtypeStruct((tokens, count * dv), BF),
-            jax.ShapeDtypeStruct((tokens, count * dv), BF),
+            jax.ShapeDtypeStruct((tokens, heads * dk), BF),
+            jax.ShapeDtypeStruct((tokens, heads * dk), BF),
+            jax.ShapeDtypeStruct((tokens, heads * dv), BF),
+            jax.ShapeDtypeStruct((tokens, heads * dv), BF),
             jax.ShapeDtypeStruct((tokens, 128), BF),
-            jax.ShapeDtypeStruct((4, count * dk), F32),
-            jax.ShapeDtypeStruct((4, count * dk), F32),
-            jax.ShapeDtypeStruct((4, count * dv), F32),
+            jax.ShapeDtypeStruct((4, heads * dk), F32),
+            jax.ShapeDtypeStruct((4, heads * dk), F32),
+            jax.ShapeDtypeStruct((4, heads * dv), F32),
             jax.ShapeDtypeStruct((8, 128), F32),
             jax.ShapeDtypeStruct((8, dv), F32),
         ],
@@ -483,7 +552,7 @@
 
 
 def hop(values, step, size):
-    return lax.ppermute(values, "col", [(at, (at + step) % size) for at in range(size)])
+    return lax.ppermute(values, "col", [(at, at ^ step) for at in range(size)])
 
 
 def hops(values, size):
@@ -502,7 +571,7 @@
 
 
 def lay_cols(pieces, place, size):
-    return lay(pieces, [(place + size - step) % size for step in range(size)], pieces[0].shape[1])
+    return lay(pieces, [place ^ step for step in range(size)], pieces[0].shape[1])
 
 
 def send_cols(pieces, size):
@@ -519,7 +588,7 @@
     rows, width = partial_sum.shape[0], partial_sum.shape[1] // size
     own = lax.dynamic_slice(partial_sum, (0, place * width), (rows, width))
     return own, [
-        lax.dynamic_slice(partial_sum, (0, (place + step) % size * width), (rows, width)).astype(BF)
+        lax.dynamic_slice(partial_sum, (0, (place ^ step) * width), (rows, width)).astype(BF)
         for step in range(1, size)
     ]
 
@@ -626,17 +695,12 @@
     depth = query_weight.shape[0]
     hidden_units = hidden_gate.shape[1]
     wide = 2 * dk + 2 * dv
-    each = heads // 2
-    span = each * wide
-
-    def per_half(arrays, sizes):
-        return [
-            array[:, half * each * size : (half + 1) * each * size] for half in (0, 1) for array, size in zip(arrays, sizes)
-        ]
 
     in_weight = jnp.concatenate(
-        per_half([query_weight, key_weight, value_weight, gate_weight], [dk, dk, dv, dv])
-        + [decay_weight, beta_weight, jnp.zeros((depth, 128 - 2 * heads), BF)],
+        [
+            query_weight, key_weight, value_weight, gate_weight, decay_weight, beta_weight,
+            jnp.zeros((depth, 128 - 2 * heads), BF),
+        ],
         axis=1,
     )
     inputs_all = gather_cols(inputs, place, size)
@@ -738,7 +802,7 @@
     grad_second_b = add_cols(cut_b[0], got_b)
     back_b = back_residual(last, residual_b, scale_b, sum(inners_b), grad_second_b)
     near_down, given_down = near_part(grad_sides, product, away_down, rows)
-    pieces_a, back_b, given_down = fence(pieces_a, back_b, given_down)
+    pieces_a, back_b, given_down, product = fence(pieces_a, back_b, given_down, product)
 
     pieces_b = hops(back_b.astype(BF), size)
     held_down = hold(near_down, given_down, rows)
@@ -756,14 +820,13 @@
     grad_mixed = contract_features(back_rows, out_all)
     x_down, y_down = send_chips(held_down, rows)
     out_part = contract_tokens(mixed, back_rows).astype(BF)
-    out_part, mlp_grad = fence(out_part, mlp_grad)
+    out_part, mlp_grad, grad_mixed, result_cut = fence(out_part, mlp_grad, grad_mixed, result_cut)
     out_grad = lax.psum_scatter(out_part, "row", scatter_dimension=1, tiled=True)
-    grad_mixed, result_cut = after((grad_mixed, result_cut), out_part)
     result_got = send_cols(result_cut[1], size)
-    lows = mixer_backward(heads, dk, dv, pres, shared, grad_mixed, saved, 0, heads)
+    lows = mixer_backward(heads, dk, dv, pres, shared, grad_mixed, saved)
     lows, x_down, y_down, result_got = fence(lows, x_down, y_down, result_got)
     *lows, low_small, query_taps, key_taps, value_taps, params_part, gain_part = lows
-    low = jnp.concatenate(per_half(lows, [dk, dk, dv, dv]) + [low_small], axis=1)
+    low = jnp.concatenate(lows + [low_small], axis=1)
     down_late = last_step(held_down, x_down, y_down, rows)
 
     in_part = contract_tokens(hidden, low).astype(BF)
@@ -774,7 +837,7 @@
     first_gain_part = jnp.sum(hidden_part * wide_all * first_scale, axis=0)
     notes = [
         jnp.concatenate(
-            [inner, lax.dynamic_slice(first_gain_part, ((place + step) % size * width,), (width,)), gain_part[0]]
+            [inner, lax.dynamic_slice(first_gain_part, ((place ^ step) * width,), (width,)), gain_part[0]]
         )
         for step in range(size)
     ]
@@ -803,9 +866,7 @@
     in_grad, result, grad_inputs = fence(in_grad, result, grad_inputs)
 
     def head_columns(start, stop):
-        return jnp.concatenate(
-            [in_grad[:, half * span + each * start : half * span + each * stop] for half in (0, 1)], axis=1
-        ).astype(F32)
+        return in_grad[:, heads * start : heads * stop].astype(F32)
 
     return (
         result,
@@ -815,8 +876,8 @@
         head_columns(dk, 2 * dk),
         head_columns(2 * dk, 2 * dk + dv),
         head_columns(2 * dk + dv, wide),
-        in_grad[:, 2 * span : 2 * span + heads].astype(F32),
-        in_grad[:, 2 * span + heads : 2 * span + 2 * heads].astype(F32),
+        in_grad[:, heads * wide : heads * wide + heads].astype(F32),
+        in_grad[:, heads * wide + heads : heads * wide + 2 * heads].astype(F32),
         query_taps,
         key_taps,
         value_taps,

time: 579 us -> 558 us (0.964); the launches traced: 569 us -> 554 us
  starting transfers between devices: 84.8 us -> 109 us
  waiting for transfers between devices: 197 us -> 175 us
  Pallas kernels: 72.5 us -> 62.3 us
  local copies, waits for them, and re-layouts: 52.9 us -> 44.5 us
    ppermute x48, waiting for transfers between devices: 162 us -> 127 us  [hop(): return lax.ppermute(values, 'col', [(at, at ^ step) for at in range(size)])]
    ppermute x48, starting transfers between devices: 80.6 us -> 105 us  [hop(): return lax.ppermute(values, 'col', [(at, at ^ step) for at in range(size)])]
    pallas_call x2, Pallas kernels: 72.5 us -> 62.3 us  [the longest x1 31.5 us: mixer_backward(): pl.pallas_call(functools.partial(backward_kernel, heads, dk, dv), grid=(2...]
    reduce_scatter x1, waiting for transfers between devices: 13.4 us -> 21.7 us  [per_device(): in_grad = lax.psum_scatter(in_part, 'row', scatter_dimension=0, tiled=True)]
    unnamed x165 -> x147, local copies, waits for them, and re-layouts: 17 us -> 15.1 us
  transfers between devices with their start and end apart: 59 -> 59, of which waited for: 21 -> 19; matrix products, arithmetic and copies ran while one was open for 24% -> 24% of each run, Pallas kernels for 13% -> 11%
where the time goes in v3:
time: 558 us; the launch traced here: 554 us
  waiting for transfers between devices  175 us (31%)
  starting transfers between devices  109 us (20%)
  matrix products  89.7 us (16%)
  Pallas kernels  62.3 us (11%)
  local copies, waits for them, and re-layouts  44.5 us (8%)
  other arithmetic  31.5 us (6%)
  blocking collectives  26 us (5%)
  between operations  15.7 us (3%)
    ppermute x48, waiting for transfers between devices, hop(): return lax.ppermute(values, 'col', [(at, at ^ step) for at in range(size)])  127 us
    ppermute x48, starting transfers between devices, hop(): return lax.ppermute(values, 'col', [(at, at ^ step) for at in range(size)])  105 us
    dot_general x11, matrix products, dot(): lax.dot_general(left, right, (((lc,), (rc,)), ((), ())), preferred_elemen...  69.7 us
    pallas_call x1, Pallas kernels, mixer_backward(): pl.pallas_call(functools.partial(backward_kernel, heads, dk, dv), grid=(2...  31.5 us
    pallas_call x1, Pallas kernels, mixer_forward(): pl.pallas_call(functools.partial(forward_kernel, heads, dk, dv), grid=(2,...  30.8 us
    psum x1, blocking collectives, per_device(): lax.psum(sums, 'row')  26 us
    all_gather x1, waiting for transfers between devices, per_device(): in_all = lax.all_gather(in_weight, 'row', axis=0, tiled=True)  24.8 us
    reduce_scatter x1, waiting for transfers between devices, per_device(): in_grad = lax.psum_scatter(in_part, 'row', scatter_dimension=0, tiled=True)  21.7 us
  transfers between devices with their start and end apart: 59, of which 19 were waited for; matrix products, arithmetic and copies ran while one was open for 24% of the time, Pallas kernels for 11%

profile of v3, /device:TPU:0, one launch (start us, length us, event | category | flops | bytes accessed | tf_op | source)
XLA Modules:
  0.0 554.0 jit_solution(11989280276584554421)
XLA Ops:
  8.9 4.0 concatenate.95
  16.0 3.1 collective-permute-start.3
  19.0 2.6 collective-permute-start.4
  22.5 3.5 collective-permute-start.1
  32.4 12.9 %collective-permute-done = bf16[512,512]{1,0:T(8,128)(2,1)} collective-permute-done((bf16[512,512]{1,0:T(8,128)(2,1)}, bf16[512,512]{1,0:T(8,128)(2,1)}, u32[]{:S(2)}, u32[]{:S(2)}) %collective-permute-start) | collective-permute-done | bytes 524320 | tf_op jit(solution)/shard_map/ppermute | solution.py:555
  46.4 15.3 %collective-permute-done.1 = bf16[512,512]{1,0:T(8,128)(2,1)} collective-permute-done((bf16[512,512]{1,0:T(8,128)(2,1)}, bf16[512,512]{1,0:T(8,128)(2,1)}, u32[]{:S(2)}, u32[]{:S(2)}) %collective-permute-start.1) | collective-permute-done | bytes 524320 | tf_op jit(solution)/shard_map/ppermute | solution.py:555
  65.3 24.8 %all-gather.4.cloned.1.call-done.query_weight.key_weight.value_weight.gate_weight.small_weight = bf16[2048,3200]{1,0:T(8,128)(2,1)} async-done(((bf16[256,3200]{1,0:T(8,128)(2,1)}), bf16[2048,3200]{1,0:T(8,128)(2,1)}) %all-gather.4.cloned.1.call-update) | async-done | bytes 13107216 | tf_op jit(solution)/shard_map/all_gather | solution.py:708
  95.7 30.8 %mixer_forward.1 = (f32[512,512]{1,0:T(8,128)}, f32[512,512]{1,0:T(8,128)}, f32[512,1024]{1,0:T(8,128)}, f32[512,1024]{1,0:T(8,128)}, f32[512,128]{1,0:T(8,128)}...) custom-call(bf16[512,2048]{1,0:T(8,128)(2,1)} %fusion.16.hidden_ref,, ...), custom_call_target="tpu_custom_call" | custom-call | flops 20000000000 | bytes 20000000 | tf_op jit(solution)/shard_map/mixer_forward/pallas_call | solution.py:461
  131.0 3.7 fusion.42
  134.9 12.1 %collective-permute-start.10 = (bf16[256,512]{1,0:T(8,128)(2,1)S(1)}, bf16[256,512]{1,0:T(8,128)(2,1)S(1)}, u32[]{:S(2)}, u32[]{:S(2)}) collective-permute-start(bf16[256,512]{1,0:T(8,128)(2,1)S(1)} %get-tuple-element.424), channel_id=1, source_target_pairs={{0,2},{1,3},{2,0},{3,1},{4,6},{5,7},{6,4},{7,5},{8,10},{9,11},{10,... | collective-permute-start | bytes 786440 | tf_op jit(solution)/shard_map/ppermute | solution.py:555
  151.8 13.7 %collective-permute-done.10 = bf16[256,512]{1,0:T(8,128)(2,1)S(1)} collective-permute-done((bf16[256,512]{1,0:T(8,128)(2,1)S(1)}, bf16[256,512]{1,0:T(8,128)(2,1)S(1)}, u32[]{:S(2)}, u32[]{:S(2)}) %collective-permute-start.10) | collective-permute-done | bytes 262176 | tf_op jit(solution)/shard_map/ppermute | solution.py:555
  165.5 4.9 collective-permute-start.12
  172.9 6.6 %collective-permute-done.12 = bf16[256,512]{1,0:T(8,128)(2,1)S(1)} collective-permute-done((bf16[256,512]{1,0:T(8,128)(2,1)S(1)}, bf16[256,512]{1,0:T(8,128)(2,1)S(1)}, u32[]{:S(2)}, u32[]{:S(2)}) %collective-permute-start.12) | collective-permute-done | bytes 262176 | tf_op jit(solution)/shard_map/ppermute | solution.py:555
  179.5 12.1 %collective-permute-done.13 = bf16[256,512]{1,0:T(8,128)(2,1)S(1)} collective-permute-done((bf16[256,512]{1,0:T(8,128)(2,1)S(1)}, bf16[256,512]{1,0:T(8,128)(2,1)S(1)}, u32[]{:S(2)}, u32[]{:S(2)}) %collective-permute-start.13) | collective-permute-done | bytes 262176 | tf_op jit(solution)/shard_map/ppermute | solution.py:555
  191.7 3.9 collective-permute-start.15
  198.2 6.0 %collective-permute-done.15 = bf16[256,512]{1,0:T(8,128)(2,1)S(1)} collective-permute-done((bf16[256,512]{1,0:T(8,128)(2,1)S(1)}, bf16[256,512]{1,0:T(8,128)(2,1)S(1)}, u32[]{:S(2)}, u32[]{:S(2)}) %collective-permute-start.15) | collective-permute-done | bytes 262176 | tf_op jit(solution)/shard_map/ppermute | solution.py:555
  204.2 11.6 %collective-permute-done.16 = bf16[256,512]{1,0:T(8,128)(2,1)S(1)} collective-permute-done((bf16[256,512]{1,0:T(8,128)(2,1)S(1)}, bf16[256,512]{1,0:T(8,128)(2,1)S(1)}, u32[]{:S(2)}, u32[]{:S(2)}) %collective-permute-start.16) | collective-permute-done | bytes 262176 | tf_op jit(solution)/shard_map/ppermute | solution.py:555
  215.8 4.0 collective-permute-start.18
  219.9 2.4 collective-permute-start.20
  225.1 6.6 %fusion.6 = f32[256,2752]{0,1:T(8,128)S(1)} fusion(bf16[256,2048]{1,0:T(8,128)(2,1)} %fusion.25, bf16[4128,2048]{1,0:T(8,128)(2,1)} %all-gather.8.cloned.1.call-done), kind=kOutput, calls=%fused_computation.12 | convolution fusion | flops 2885681152 | bytes 15138816 | tf_op jit(solution)/shard_map/dot_general | solution.py:17
  231.8 5.7 %multiply_convert_fusion.4 = (bf16[256,1376]{0,1:T(8,128)(2,1)S(1)}, bf16[256,1376]{0,1:T(8,128)(2,1)S(1)}, bf16[256,1376]{0,1:T(8,128)(2,1)}) fusion(f32[256,2752]{0,1:T(8,128)S(1)} %fusion.6, bf16[4128,2048]{1,0:T(8,128)(2,1)} %all-gather.8.cloned.1.call-done, bf16[512,2048]{1,0:T(8,128)(2,1)S(1)} %constant_dynamic-update-slice_fusion.25), kind=kOutput, calls=%fused_computation.61 | convolution fusion | flops 1448124416 | bytes 11616256 | tf_op jit(solution)/shard_map/dot_general | solution.py:17
  237.6 3.3 fusion.26
  241.1 3.2 collective-permute-start.24
  253.3 6.0 %fusion.2 = f32[256,2752]{0,1:T(8,128)S(1)} fusion(bf16[256,2048]{1,0:T(8,128)(2,1)S(1)} %fusion.29, bf16[4128,2048]{1,0:T(8,128)(2,1)} %all-gather.8.cloned.1.call-done), kind=kOutput, calls=%fused_computation.8 | convolution fusion | flops 2885681152 | bytes 15138816 | tf_op jit(solution)/shard_map/dot_general | solution.py:17
  259.3 5.7 %multiply_convert_fusion.1 = (bf16[256,1376]{0,1:T(8,128)(2,1)S(1)}, bf16[256,1376]{0,1:T(8,128)(2,1)S(1)}, bf16[256,1376]{0,1:T(8,128)(2,1)}) fusion(f32[256,2752]{0,1:T(8,128)S(1)} %fusion.2, bf16[4128,2048]{1,0:T(8,128)(2,1)} %all-gather.8.cloned.1.call-done, bf16[512,2048]{1,0:T(8,128)(2,1)S(1)} %constant_dynamic-update-slice_fusion.25), kind=kOutput, calls=%fused_computation.56 | convolution fusion | flops 1448124416 | bytes 11616256 | tf_op jit(solution)/shard_map/dot_general | solution.py:17
  265.1 6.2 %fusion.30 = (f32[256]{0:T(256)S(1)}, f32[256,2048]{1,0:T(8,128)S(1)}) fusion(bf16[256,2048]{1,0:T(8,128)(2,1)S(1)} %constant_dynamic-update-slice_fusion.17, f32[2048]{0:T(1024)S(1)} %bitcast.55, bf16[4128,2048]{1,0:T(8,128)(2,1)} %all-gather.8.cloned.1.call-done, bf16[256,1376]{0,1:T(8,128)(2,1)S(1)} %get-tuple-element.387, ...), kind=kOutput, calls=%fused_computation.46 | convolution fusion | flops 2890596096 | bytes 15836160 | tf_op jit(solution)/shard_map/dot_general | solution.py:535
  274.0 3.6 collective-permute-done.26
  277.6 9.1 %convolution_convert_fusion.1 = bf16[2048,2752]{0,1:T(8,128)(2,1)} fusion(bf16[256,2752]{0,1:T(8,128)(2,1)S(1)} %pad_maximum_fusion.3, bf16[256,2752]{0,1:T(8,128)(2,1)S(1)} %pad_maximum_fusion.2, bf16[256,2048]{1,0:T(8,128)(2,1)S(1)} %fusion.29, bf16[256,2048]{1,0:T(8,128)(2,1)S(1)} %copy-done.26), kind=kOutput, calls=%fused_computation.1 | convolution fusion | flops 5786828800 | bytes 16187392 | tf_op jit(solution)/shard_map/dot_general | solution.py:17
  304.4 7.3 %collective-permute-done.28 = bf16[256,512]{1,0:T(8,128)(2,1)S(1)} collective-permute-done((bf16[256,512]{1,0:T(8,128)(2,1)}, bf16[256,512]{1,0:T(8,128)(2,1)S(1)}, u32[]{:S(2)}, u32[]{:S(2)}) %collective-permute-start.28) | collective-permute-done | bytes 262176 | tf_op jit(solution)/shard_map/ppermute | solution.py:555
  311.8 4.4 collective-permute-start.33
  319.7 7.9 %collective-permute-done.33 = bf16[256,512]{1,0:T(8,128)(2,1)S(1)} collective-permute-done((bf16[256,512]{1,0:T(8,128)(2,1)S(1)}, bf16[256,512]{1,0:T(8,128)(2,1)S(1)}, u32[]{:S(2)}, u32[]{:S(2)}) %collective-permute-start.33) | collective-permute-done | bytes 262176 | tf_op jit(solution)/shard_map/ppermute | solution.py:555
  327.6 9.9 %collective-permute-done.34 = bf16[256,512]{1,0:T(8,128)(2,1)S(1)} collective-permute-done((bf16[256,512]{1,0:T(8,128)(2,1)S(1)}, bf16[256,512]{1,0:T(8,128)(2,1)S(1)}, u32[]{:S(2)}, u32[]{:S(2)}) %collective-permute-start.34) | collective-permute-done | bytes 262176 | tf_op jit(solution)/shard_map/ppermute | solution.py:555
  337.6 5.5 collective-permute-start.37
  345.8 5.6 %fusion.8 = f32[512,2048]{1,0:T(8,128)S(1)} fusion(bf16[512,1376]{0,1:T(8,128)(2,1)S(1)} %constant_dynamic-update-slice_fusion, bf16[4128,2048]{1,0:T(8,128)(2,1)} %all-gather.8.cloned.1.call-done), kind=kOutput, calls=%fused_computation.15 | convolution fusion | flops 2885681152 | bytes 11239424 | tf_op jit(solution)/shard_map/dot_general | solution.py:535
  356.3 8.2 %collective-permute-done.38 = bf16[256,512]{1,0:T(8,128)(2,1)S(1)} collective-permute-done((bf16[256,512]{1,0:T(8,128)(2,1)S(1)}, bf16[256,512]{1,0:T(8,128)(2,1)S(1)}, u32[]{:S(2)}, u32[]{:S(2)}) %collective-permute-start.38) | collective-permute-done | bytes 262176 | tf_op jit(solution)/shard_map/ppermute | solution.py:555
  365.7 4.4 convolution_convert_fusion.3
  370.1 6.6 %fusion.36.grad_ref = f32[512,1024]{1,0:T(8,128)} fusion(bf16[1024,2048]{1,0:T(8,128)(2,1)} %all-gather.6.cloned.1.call-done, bf16[256,2048]{1,0:T(8,128)(2,1)} %copy-done.24, bf16[256,2048]{1,0:T(8,128)(2,1)} %copy-done.25), kind=kOutput, calls=%fused_computation.65 | convolution fusion | flops 2151677952 | bytes 8388608 | tf_op jit(solution)/shard_map/dot_general | solution.py:17
  379.5 4.3 collective-permute-start.42
  386.2 31.5 %mixer_backward.1 = (bf16[512,512]{1,0:T(8,128)(2,1)}, bf16[512,512]{1,0:T(8,128)(2,1)}, bf16[512,1024]{1,0:T(8,128)(2,1)}, bf16[512,1024]{1,0:T(8,128)(2,1)}, b...) custom-call(f32[512,512]{1,0:T(8,128)} %get-tuple-element.169.query_, ...), custom_call_target="tpu_custom_call" | custom-call | flops 20000000000 | bytes 20000000 | tf_op jit(solution)/shard_map/mixer_backward/pallas_call | solution.py:497
  417.8 4.2 collective-permute-done.43
  428.0 10.3 %convolution_convert_fusion = bf16[2048,3200]{1,0:T(8,128)(2,1)} fusion(bf16[512,2048]{1,0:T(8,128)(2,1)S(1)} %copy-done.17, bf16[512,3200]{1,0:T(8,128)(2,1)S(1)} %constant_dynamic-update-slice_fusion.2), kind=kOutput, calls=%fused_computation | convolution fusion | flops 6717440000 | bytes 18481152 | tf_op jit(solution)/shard_map/dot_general | solution.py:17
  443.9 11.9 %fusion.19 = (f32[2048]{0:T(1024)S(1)}, f32[512]{0:T(512)S(1)}, f32[512,2048]{1,0:T(8,128)S(1)}) fusion(bf16[512,2048]{1,0:T(8,128)(2,1)S(1)} %copy-done.1, f32[512]{0:T(512)S(1)} %copy-done.52, f32[2048]{0:T(1024)S(1)} %bitcast.60, bf16[512,3200]{1,0:T(8,128)(2,1)} %copy-done.46, ...), kind=kOutput, calls=%fused_computation.26 | convolution fusion | flops 6718223872 | bytes 22695936 | tf_op jit(solution)/shard_map/dot_general | solution.py:17
  462.8 9.2 %collective-permute-start.50 = (f32[1280]{0:T(1024)S(1)}, f32[1280]{0:T(1024)S(1)}, u32[]{:S(2)}, u32[]{:S(2)}) collective-permute-start(f32[1280]{0:T(1024)S(1)} %get-tuple-element.286), channel_id=1, source_target_pairs={{0,1},{1,0},{2,3},{3,2},{4,5},{5,4},{6,7},{7,6},{8,9},{9,8},{10,11... | collective-permute-start | bytes 15368 | tf_op jit(solution)/shard_map/ppermute | solution.py:555
  480.1 26.0 %all-reduce.1 = (f32[4,512]{1,0:T(4,128)}, f32[768]{0:T(1024)S(1)}, f32[4,512]{1,0:T(4,128)}, f32[4,1024]{1,0:T(4,128)}, f32[2,4]{1,0:T(2,128)S(1)}, /*index=5*/f32[512]{0:T(512)}) all-reduce(f32[4,512]{1,0:T(4,128)S(1)} %copy-done.58, f32[768]{0:T(1024)S(1)} %slice.257, ...), channel_id=1, replica_groups=mesh['row'=8,'col'=4] {'row'}, use_global_device_ids=true, to_apply=%region_10.11 | all-reduce | flops 9480 | bytes 75840 | tf_op jit(solution)/shard_map/psum | solution.py:850
  510.1 3.1 collective-permute-done.48
  513.2 3.1 fusion.37
  518.0 21.7 %reduce-scatter.6.cloned.1.call-done = bf16[256,3200]{1,0:T(8,128)(2,1)} async-done(((bf16[2048,3200]{1,0:T(8,128)(2,1)}), bf16[256,3200]{1,0:T(8,128)(2,1)}) %reduce-scatter.6.cloned.1.call-update) | async-done | bytes 1638416 | tf_op jit(solution)/shard_map/reduce_scatter | solution.py:833
  539.7 2.8 slice_convert_fusion
  (369 shorter events, 122.8 us)
Async XLA Ops:
  7.2 82.9 %all-gather.4.cloned.1.call-start = ((), (), s32[]{:S(2)}) async-start(), calls=%async_computation.3 | async-start | bytes 14745600 | tf_op jit(solution)/shard_map/all_gather | solution.py:708
  12.9 118.1 %all-gather.6.cloned.1.call-start = ((), (), s32[]{:S(2)}) async-start(), calls=%async_computation.4 | async-start | bytes 4718592 | tf_op jit(solution)/shard_map/all_gather | solution.py:709
  13.7 211.4 %all-gather.8.cloned.1.call-start = ((), (), s32[]{:S(2)}) async-start(), calls=%async_computation.5 | async-start | bytes 19021824 | tf_op jit(solution)/shard_map/all_gather | solution.py:712
  15.3 361.5 %reduce-scatter.4.cloned.1.call-start = ((), (), s32[]{:S(2)}) async-start(), calls=%async_computation.6 | async-start | bytes 12681216 | tf_op jit(solution)/shard_map/reduce_scatter | solution.py:797
  16.0 16.3 %collective-permute-start.3 = (f32[2,512]{1,0:T(2,128)S(1)}, f32[2,512]{1,0:T(2,128)S(1)}, u32[]{:S(2)}, u32[]{:S(2)}) collective-permute-start(f32[2,512]{1,0:T(2,128)S(1)} %get-tuple-element.444), channel_id=1, source_target_pairs={{0,1},{1,0},{2,3},{3,2},{4,5},{5,4},{6,7},{7,6},{8,9},{9,8},{10,11... | collective-permute-start | bytes 12296 | tf_op jit(solution)/shard_map/ppermute | solution.py:555
  21.6 23.6 %collective-permute-start = (bf16[512,512]{1,0:T(8,128)(2,1)}, bf16[512,512]{1,0:T(8,128)(2,1)}, u32[]{:S(2)}, u32[]{:S(2)}) collective-permute-start(bf16[512,512]{1,0:T(8,128)(2,1)} %param.21), channel_id=1, source_target_pairs={{0,1},{1,0},{2,3},{3,2},{4,5},{5,4},{6,7},{7,6},{8,9},{9,8},{10,11... | collective-permute-start | bytes 1572872 | tf_op jit(solution)/shard_map/ppermute | solution.py:555
  22.5 39.1 %collective-permute-start.1 = (bf16[512,512]{1,0:T(8,128)(2,1)}, bf16[512,512]{1,0:T(8,128)(2,1)}, u32[]{:S(2)}, u32[]{:S(2)}) collective-permute-start(bf16[512,512]{1,0:T(8,128)(2,1)} %param.21), channel_id=1, source_target_pairs={{0,2},{1,3},{2,0},{3,1},{4,6},{5,7},{6,4},{7,5},{8,10},{9,11},{10,... | collective-permute-start | bytes 1572872 | tf_op jit(solution)/shard_map/ppermute | solution.py:555
  32.2 30.6 %collective-permute-start.2 = (bf16[512,512]{1,0:T(8,128)(2,1)}, bf16[512,512]{1,0:T(8,128)(2,1)S(1)}, u32[]{:S(2)}, u32[]{:S(2)}) collective-permute-start(bf16[512,512]{1,0:T(8,128)(2,1)} %param.21), channel_id=1, source_target_pairs={{0,3},{1,2},{2,1},{3,0},{4,7},{5,6},{6,5},{7,4},{8,11},{9,10},{10,... | collective-permute-start | bytes 1572872 | tf_op jit(solution)/shard_map/ppermute | solution.py:555
  90.1 37.5 %collective-permute-start.6 = (bf16[512,512]{1,0:T(8,128)(2,1)}, bf16[512,512]{1,0:T(8,128)(2,1)S(1)}, u32[]{:S(2)}, u32[]{:S(2)}) collective-permute-start(bf16[512,512]{1,0:T(8,128)(2,1)} %param.41), channel_id=1, source_target_pairs={{0,1},{1,0},{2,3},{3,2},{4,5},{5,4},{6,7},{7,6},{8,9},{9,8},{10,11... | collective-permute-start | bytes 1572872 | tf_op jit(solution)/shard_map/ppermute | solution.py:555
  91.6 38.4 %collective-permute-start.7 = (bf16[512,512]{1,0:T(8,128)(2,1)}, bf16[512,512]{1,0:T(8,128)(2,1)S(1)}, u32[]{:S(2)}, u32[]{:S(2)}) collective-permute-start(bf16[512,512]{1,0:T(8,128)(2,1)} %param.41), channel_id=1, source_target_pairs={{0,2},{1,3},{2,0},{3,1},{4,6},{5,7},{6,4},{7,5},{8,10},{9,11},{10,... | collective-permute-start | bytes 1572872 | tf_op jit(solution)/shard_map/ppermute | solution.py:555
  94.0 36.1 %collective-permute-start.8 = (bf16[512,512]{1,0:T(8,128)(2,1)}, bf16[512,512]{1,0:T(8,128)(2,1)S(1)}, u32[]{:S(2)}, u32[]{:S(2)}) collective-permute-start(bf16[512,512]{1,0:T(8,128)(2,1)} %param.41), channel_id=1, source_target_pairs={{0,3},{1,2},{2,1},{3,0},{4,7},{5,6},{6,5},{7,4},{8,11},{9,10},{10,... | collective-permute-start | bytes 1572872 | tf_op jit(solution)/shard_map/ppermute | solution.py:555
  134.9 30.6 %collective-permute-start.10 = (bf16[256,512]{1,0:T(8,128)(2,1)S(1)}, bf16[256,512]{1,0:T(8,128)(2,1)S(1)}, u32[]{:S(2)}, u32[]{:S(2)}) collective-permute-start(bf16[256,512]{1,0:T(8,128)(2,1)S(1)} %get-tuple-element.424), channel_id=1, source_target_pairs={{0,2},{1,3},{2,0},{3,1},{4,6},{5,7},{6,4},{7,5},{8,10},{9,11},{10,... | collective-permute-start | bytes 786440 | tf_op jit(solution)/shard_map/ppermute | solution.py:555
  147.0 18.5 %collective-permute-start.11 = (bf16[256,512]{1,0:T(8,128)(2,1)S(1)}, bf16[256,512]{1,0:T(8,128)(2,1)S(1)}, u32[]{:S(2)}, u32[]{:S(2)}) collective-permute-start(bf16[256,512]{1,0:T(8,128)(2,1)S(1)} %get-tuple-element.423), channel_id=1, source_target_pairs={{0,3},{1,2},{2,1},{3,0},{4,7},{5,6},{6,5},{7,4},{8,11},{9,10},{10,... | collective-permute-start | bytes 786440 | tf_op jit(solution)/shard_map/ppermute | solution.py:555
  148.4 17.1 %collective-permute-start.9 = (bf16[256,512]{1,0:T(8,128)(2,1)S(1)}, bf16[256,512]{1,0:T(8,128)(2,1)S(1)}, u32[]{:S(2)}, u32[]{:S(2)}) collective-permute-start(bf16[256,512]{1,0:T(8,128)(2,1)S(1)} %get-tuple-element.425), channel_id=1, source_target_pairs={{0,1},{1,0},{2,3},{3,2},{4,5},{5,4},{6,7},{7,6},{8,9},{9,8},{10,11... | collective-permute-start | bytes 786440 | tf_op jit(solution)/shard_map/ppermute | solution.py:555
  170.4 21.3 %collective-permute-start.13 = (bf16[256,512]{1,0:T(8,128)(2,1)S(1)}, bf16[256,512]{1,0:T(8,128)(2,1)S(1)}, u32[]{:S(2)}, u32[]{:S(2)}) collective-permute-start(bf16[256,512]{1,0:T(8,128)(2,1)S(1)} %get-tuple-element.179), channel_id=1, source_target_pairs={{0,2},{1,3},{2,0},{3,1},{4,6},{5,7},{6,4},{7,5},{8,10},{9,11},{10,... | collective-permute-start | bytes 786440 | tf_op jit(solution)/shard_map/ppermute | solution.py:555
  170.4 21.3 %collective-permute-start.14 = (bf16[256,512]{1,0:T(8,128)(2,1)S(1)}, bf16[256,512]{1,0:T(8,128)(2,1)S(1)}, u32[]{:S(2)}, u32[]{:S(2)}) collective-permute-start(bf16[256,512]{1,0:T(8,128)(2,1)S(1)} %get-tuple-element.180), channel_id=1, source_target_pairs={{0,3},{1,2},{2,1},{3,0},{4,7},{5,6},{6,5},{7,4},{8,11},{9,10},{10,... | collective-permute-start | bytes 786440 | tf_op jit(solution)/shard_map/ppermute | solution.py:555
  195.6 20.2 %collective-permute-start.16 = (bf16[256,512]{1,0:T(8,128)(2,1)S(1)}, bf16[256,512]{1,0:T(8,128)(2,1)S(1)}, u32[]{:S(2)}, u32[]{:S(2)}) collective-permute-start(bf16[256,512]{1,0:T(8,128)(2,1)S(1)} %convert_element_type.242), channel_id=1, source_target_pairs={{0,2},{1,3},{2,0},{3,1},{4,6},{5,7},{6,4},{7,5},{8,10},{9,11},{10,... | collective-permute-start | bytes 786440 | tf_op jit(solution)/shard_map/ppermute | solution.py:555
  195.6 20.2 %collective-permute-start.17 = (bf16[256,512]{1,0:T(8,128)(2,1)S(1)}, bf16[256,512]{1,0:T(8,128)(2,1)S(1)}, u32[]{:S(2)}, u32[]{:S(2)}) collective-permute-start(bf16[256,512]{1,0:T(8,128)(2,1)S(1)} %convert_element_type.242), channel_id=1, source_target_pairs={{0,3},{1,2},{2,1},{3,0},{4,7},{5,6},{6,5},{7,4},{8,11},{9,10},{10,... | collective-permute-start | bytes 786440 | tf_op jit(solution)/shard_map/ppermute | solution.py:555
  215.8 25.2 %collective-permute-start.18 = (bf16[256,512]{1,0:T(8,128)(2,1)S(1)}, bf16[256,512]{1,0:T(8,128)(2,1)}, u32[]{:S(2)}, u32[]{:S(2)}) collective-permute-start(bf16[256,512]{1,0:T(8,128)(2,1)S(1)} %convert_element_type.246), channel_id=1, source_target_pairs={{0,1},{1,0},{2,3},{3,2},{4,5},{5,4},{6,7},{7,6},{8,9},{9,8},{10,11... | collective-permute-start | bytes 786440 | tf_op jit(solution)/shard_map/ppermute | solution.py:555
  219.9 21.2 %collective-permute-start.19 = (bf16[256,512]{1,0:T(8,128)(2,1)S(1)}, bf16[256,512]{1,0:T(8,128)(2,1)}, u32[]{:S(2)}, u32[]{:S(2)}) collective-permute-start(bf16[256,512]{1,0:T(8,128)(2,1)S(1)} %convert_element_type.246), channel_id=1, source_target_pairs={{0,2},{1,3},{2,0},{3,1},{4,6},{5,7},{6,4},{7,5},{8,10},{9,11},{10,... | collective-permute-start | bytes 786440 | tf_op jit(solution)/shard_map/ppermute | solution.py:555
  219.9 21.2 %collective-permute-start.20 = (bf16[256,512]{1,0:T(8,128)(2,1)S(1)}, bf16[256,512]{1,0:T(8,128)(2,1)}, u32[]{:S(2)}, u32[]{:S(2)}) collective-permute-start(bf16[256,512]{1,0:T(8,128)(2,1)S(1)} %convert_element_type.246), channel_id=1, source_target_pairs={{0,3},{1,2},{2,1},{3,0},{4,7},{5,6},{6,5},{7,4},{8,11},{9,10},{10,... | collective-permute-start | bytes 786440 | tf_op jit(solution)/shard_map/ppermute | solution.py:555
  241.1 31.1 %collective-permute-start.24 = (f32[256]{0:T(256)S(1)}, f32[256]{0:T(256)S(1)}, u32[]{:S(2)}, u32[]{:S(2)}) collective-permute-start(f32[256]{0:T(256)S(1)} %get-tuple-element.215), channel_id=1, source_target_pairs={{0,1},{1,0},{2,3},{3,2},{4,5},{5,4},{6,7},{7,6},{8,9},{9,8},{10,11... | collective-permute-start | bytes 3080 | tf_op jit(solution)/shard_map/ppermute | solution.py:555
  244.3 29.7 %collective-permute-start.25 = (f32[256]{0:T(256)S(1)}, f32[256]{0:T(256)S(1)}, u32[]{:S(2)}, u32[]{:S(2)}) collective-permute-start(f32[256]{0:T(256)S(1)} %get-tuple-element.215), channel_id=1, source_target_pairs={{0,2},{1,3},{2,0},{3,1},{4,6},{5,7},{6,4},{7,5},{8,10},{9,11},{10,... | collective-permute-start | bytes 3080 | tf_op jit(solution)/shard_map/ppermute | solution.py:555
  248.8 28.8 %collective-permute-start.21 = (bf16[256,512]{1,0:T(8,128)(2,1)S(1)}, bf16[256,512]{1,0:T(8,128)(2,1)}, u32[]{:S(2)}, u32[]{:S(2)}) collective-permute-start(bf16[256,512]{1,0:T(8,128)(2,1)S(1)} %get-tuple-element.198), channel_id=1, source_target_pairs={{0,1},{1,0},{2,3},{3,2},{4,5},{5,4},{6,7},{7,6},{8,9},{9,8},{10,11... | collective-permute-start | bytes 786440 | tf_op jit(solution)/shard_map/ppermute | solution.py:555
  249.4 28.2 %collective-permute-start.22 = (bf16[256,512]{1,0:T(8,128)(2,1)S(1)}, bf16[256,512]{1,0:T(8,128)(2,1)}, u32[]{:S(2)}, u32[]{:S(2)}) collective-permute-start(bf16[256,512]{1,0:T(8,128)(2,1)S(1)} %get-tuple-element.199), channel_id=1, source_target_pairs={{0,2},{1,3},{2,0},{3,1},{4,6},{5,7},{6,4},{7,5},{8,10},{9,11},{10,... | collective-permute-start | bytes 786440 | tf_op jit(solution)/shard_map/ppermute | solution.py:555
  251.1 26.5 %collective-permute-start.23 = (bf16[256,512]{1,0:T(8,128)(2,1)S(1)}, bf16[256,512]{1,0:T(8,128)(2,1)}, u32[]{:S(2)}, u32[]{:S(2)}) collective-permute-start(bf16[256,512]{1,0:T(8,128)(2,1)S(1)} %get-tuple-element.200), channel_id=1, source_target_pairs={{0,3},{1,2},{2,1},{3,0},{4,7},{5,6},{6,5},{7,4},{8,11},{9,10},{10,... | collective-permute-start | bytes 786440 | tf_op jit(solution)/shard_map/ppermute | solution.py:555
  286.8 221.1 %reduce-scatter.8.cloned.1.call-start = ((), (), s32[]{:S(2)}) async-start(), calls=%async_computation.8 | async-start | bytes 4718592 | tf_op jit(solution)/shard_map/reduce_scatter | solution.py:824
  288.0 14.3 %collective-permute-start.31 = (f32[256]{0:T(256)S(1)}, f32[256]{0:T(256)S(1)}, u32[]{:S(2)}, u32[]{:S(2)}) collective-permute-start(f32[256]{0:T(256)S(1)} %get-tuple-element.232), channel_id=1, source_target_pairs={{0,2},{1,3},{2,0},{3,1},{4,6},{5,7},{6,4},{7,5},{8,10},{9,11},{10,... | collective-permute-start | bytes 3080 | tf_op jit(solution)/shard_map/ppermute | solution.py:555
  292.4 19.3 %collective-permute-start.28 = (bf16[256,512]{1,0:T(8,128)(2,1)}, bf16[256,512]{1,0:T(8,128)(2,1)S(1)}, u32[]{:S(2)}, u32[]{:S(2)}) collective-permute-start(bf16[256,512]{1,0:T(8,128)(2,1)} %get-tuple-element.207), channel_id=1, source_target_pairs={{0,2},{1,3},{2,0},{3,1},{4,6},{5,7},{6,4},{7,5},{8,10},{9,11},{10,... | collective-permute-start | bytes 786440 | tf_op jit(solution)/shard_map/ppermute | solution.py:555
  311.7 25.8 %collective-permute-start.36 = (bf16[1024,1376]{0,1:T(8,128)(2,1)S(1)}, bf16[1024,1376]{0,1:T(8,128)(2,1)S(1)}, u32[]{:S(2)}, u32[]{:S(2)}) collective-permute-start(bf16[1024,1376]{0,1:T(8,128)(2,1)S(1)} %convolution_convert_fusion.2), channel_id=1, source_target_pairs={{0,4},{4,0},{8,12},{12,8},{16,20},{20,16},{24,28},{28,24},{1,5},{5... | collective-permute-start | bytes 8454152 | tf_op jit(solution)/shard_map/ppermute | solution.py:597
  311.8 15.9 %collective-permute-start.33 = (bf16[256,512]{1,0:T(8,128)(2,1)S(1)}, bf16[256,512]{1,0:T(8,128)(2,1)S(1)}, u32[]{:S(2)}, u32[]{:S(2)}) collective-permute-start(bf16[256,512]{1,0:T(8,128)(2,1)S(1)} %convert_element_type.265), channel_id=1, source_target_pairs={{0,1},{1,0},{2,3},{3,2},{4,5},{5,4},{6,7},{7,6},{8,9},{9,8},{10,11... | collective-permute-start | bytes 786440 | tf_op jit(solution)/shard_map/ppermute | solution.py:555
  316.2 21.3 %collective-permute-start.34 = (bf16[256,512]{1,0:T(8,128)(2,1)S(1)}, bf16[256,512]{1,0:T(8,128)(2,1)S(1)}, u32[]{:S(2)}, u32[]{:S(2)}) collective-permute-start(bf16[256,512]{1,0:T(8,128)(2,1)S(1)} %convert_element_type.265), channel_id=1, source_target_pairs={{0,2},{1,3},{2,0},{3,1},{4,6},{5,7},{6,4},{7,5},{8,10},{9,11},{10,... | collective-permute-start | bytes 786440 | tf_op jit(solution)/shard_map/ppermute | solution.py:555
  316.2 21.3 %collective-permute-start.35 = (bf16[256,512]{1,0:T(8,128)(2,1)S(1)}, bf16[256,512]{1,0:T(8,128)(2,1)S(1)}, u32[]{:S(2)}, u32[]{:S(2)}) collective-permute-start(bf16[256,512]{1,0:T(8,128)(2,1)S(1)} %convert_element_type.265), channel_id=1, source_target_pairs={{0,3},{1,2},{2,1},{3,0},{4,7},{5,6},{6,5},{7,4},{8,11},{9,10},{10,... | collective-permute-start | bytes 786440 | tf_op jit(solution)/shard_map/ppermute | solution.py:555
  337.6 18.8 %collective-permute-start.37 = (bf16[256,512]{1,0:T(8,128)(2,1)S(1)}, bf16[256,512]{1,0:T(8,128)(2,1)S(1)}, u32[]{:S(2)}, u32[]{:S(2)}) collective-permute-start(bf16[256,512]{1,0:T(8,128)(2,1)S(1)} %convert_element_type.270), channel_id=1, source_target_pairs={{0,1},{1,0},{2,3},{3,2},{4,5},{5,4},{6,7},{7,6},{8,9},{9,8},{10,11... | collective-permute-start | bytes 786440 | tf_op jit(solution)/shard_map/ppermute | solution.py:555
  343.1 21.4 %collective-permute-start.38 = (bf16[256,512]{1,0:T(8,128)(2,1)S(1)}, bf16[256,512]{1,0:T(8,128)(2,1)S(1)}, u32[]{:S(2)}, u32[]{:S(2)}) collective-permute-start(bf16[256,512]{1,0:T(8,128)(2,1)S(1)} %convert_element_type.270), channel_id=1, source_target_pairs={{0,2},{1,3},{2,0},{3,1},{4,6},{5,7},{6,4},{7,5},{8,10},{9,11},{10,... | collective-permute-start | bytes 786440 | tf_op jit(solution)/shard_map/ppermute | solution.py:555
  343.1 21.3 %collective-permute-start.39 = (bf16[256,512]{1,0:T(8,128)(2,1)S(1)}, bf16[256,512]{1,0:T(8,128)(2,1)S(1)}, u32[]{:S(2)}, u32[]{:S(2)}) collective-permute-start(bf16[256,512]{1,0:T(8,128)(2,1)S(1)} %convert_element_type.270), channel_id=1, source_target_pairs={{0,3},{1,2},{2,1},{3,0},{4,7},{5,6},{6,5},{7,4},{8,11},{9,10},{10,... | collective-permute-start | bytes 786440 | tf_op jit(solution)/shard_map/ppermute | solution.py:555
  376.8 162.9 %reduce-scatter.6.cloned.1.call-start = ((), (), s32[]{:S(2)}) async-start(), calls=%async_computation.7 | async-start | bytes 14745600 | tf_op jit(solution)/shard_map/reduce_scatter | solution.py:833
  377.2 40.5 %collective-permute-start.41 = (bf16[256,1376]{0,1:T(8,128)(2,1)S(1)}, bf16[256,1376]{0,1:T(8,128)(2,1)S(1)}, u32[]{:S(2)}, u32[]{:S(2)}) collective-permute-start(bf16[256,1376]{0,1:T(8,128)(2,1)S(1)} %pad_maximum_fusion.9), channel_id=1, source_target_pairs={{0,16},{4,20},{8,24},{12,28},{16,0},{20,4},{24,8},{28,12},{1,17},{... | collective-permute-start | bytes 2113544 | tf_op jit(solution)/shard_map/ppermute | solution.py:597
  378.0 39.8 %collective-permute-start.40 = (bf16[256,1376]{0,1:T(8,128)(2,1)S(1)}, bf16[256,1376]{0,1:T(8,128)(2,1)S(1)}, u32[]{:S(2)}, u32[]{:S(2)}) collective-permute-start(bf16[256,1376]{0,1:T(8,128)(2,1)S(1)} %pad_maximum_fusion.8), channel_id=1, source_target_pairs={{0,8},{4,12},{8,0},{12,4},{16,24},{20,28},{24,16},{28,20},{1,9},{5... | collective-permute-start | bytes 2113544 | tf_op jit(solution)/shard_map/ppermute | solution.py:597
  379.5 38.4 %collective-permute-start.42 = (bf16[512,512]{1,0:T(8,128)(2,1)S(1)}, bf16[512,512]{1,0:T(8,128)(2,1)S(1)}, u32[]{:S(2)}, u32[]{:S(2)}) collective-permute-start(bf16[512,512]{1,0:T(8,128)(2,1)S(1)} %copy-done.41), channel_id=1, source_target_pairs={{0,1},{1,0},{2,3},{3,2},{4,5},{5,4},{6,7},{7,6},{8,9},{9,8},{10,11... | collective-permute-start | bytes 1572872 | tf_op jit(solution)/shard_map/ppermute | solution.py:555
  383.8 38.2 %collective-permute-start.43 = (bf16[512,512]{1,0:T(8,128)(2,1)S(1)}, bf16[512,512]{1,0:T(8,128)(2,1)S(1)}, u32[]{:S(2)}, u32[]{:S(2)}) collective-permute-start(bf16[512,512]{1,0:T(8,128)(2,1)S(1)} %copy-done.40), channel_id=1, source_target_pairs={{0,2},{1,3},{2,0},{3,1},{4,6},{5,7},{6,4},{7,5},{8,10},{9,11},{10,... | collective-permute-start | bytes 1572872 | tf_op jit(solution)/shard_map/ppermute | solution.py:555
  383.9 38.2 %collective-permute-start.44 = (bf16[512,512]{1,0:T(8,128)(2,1)S(1)}, bf16[512,512]{1,0:T(8,128)(2,1)S(1)}, u32[]{:S(2)}, u32[]{:S(2)}) collective-permute-start(bf16[512,512]{1,0:T(8,128)(2,1)S(1)} %copy-done.39), channel_id=1, source_target_pairs={{0,3},{1,2},{2,1},{3,0},{4,7},{5,6},{6,5},{7,4},{8,11},{9,10},{10,... | collective-permute-start | bytes 1572872 | tf_op jit(solution)/shard_map/ppermute | solution.py:555
  441.1 21.7 %collective-permute-start.45 = (bf16[128,1376]{0,1:T(8,128)(2,1)S(1)}, bf16[128,1376]{0,1:T(8,128)(2,1)S(1)}, u32[]{:S(2)}, u32[]{:S(2)}) collective-permute-start(bf16[128,1376]{0,1:T(8,128)(2,1)S(1)} %get-tuple-element.399), channel_id=1, source_target_pairs={{0,8},{4,12},{8,0},{12,4},{16,24},{20,28},{24,16},{28,20},{1,9},{5... | collective-permute-start | bytes 1056776 | tf_op jit(solution)/shard_map/ppermute | solution.py:597
  441.7 21.1 %collective-permute-start.46 = (bf16[128,1376]{0,1:T(8,128)(2,1)S(1)}, bf16[128,1376]{0,1:T(8,128)(2,1)S(1)}, u32[]{:S(2)}, u32[]{:S(2)}) collective-permute-start(bf16[128,1376]{0,1:T(8,128)(2,1)S(1)} %get-tuple-element.398), channel_id=1, source_target_pairs={{0,16},{4,20},{8,24},{12,28},{16,0},{20,4},{24,8},{28,12},{1,17},{... | collective-permute-start | bytes 1056776 | tf_op jit(solution)/shard_map/ppermute | solution.py:597
  462.8 14.8 %collective-permute-start.50 = (f32[1280]{0:T(1024)S(1)}, f32[1280]{0:T(1024)S(1)}, u32[]{:S(2)}, u32[]{:S(2)}) collective-permute-start(f32[1280]{0:T(1024)S(1)} %get-tuple-element.286), channel_id=1, source_target_pairs={{0,1},{1,0},{2,3},{3,2},{4,5},{5,4},{6,7},{7,6},{8,9},{9,8},{10,11... | collective-permute-start | bytes 15368 | tf_op jit(solution)/shard_map/ppermute | solution.py:555
  474.4 35.7 %collective-permute-start.47 = (bf16[512,512]{1,0:T(8,128)(2,1)}, bf16[512,512]{1,0:T(8,128)(2,1)}, u32[]{:S(2)}, u32[]{:S(2)}) collective-permute-start(bf16[512,512]{1,0:T(8,128)(2,1)} %get-tuple-element.282), channel_id=1, source_target_pairs={{0,1},{1,0},{2,3},{3,2},{4,5},{5,4},{6,7},{7,6},{8,9},{9,8},{10,11... | collective-permute-start | bytes 1572872 | tf_op jit(solution)/shard_map/ppermute | solution.py:555
  475.5 37.7 %collective-permute-start.48 = (bf16[512,512]{1,0:T(8,128)(2,1)}, bf16[512,512]{1,0:T(8,128)(2,1)}, u32[]{:S(2)}, u32[]{:S(2)}) collective-permute-start(bf16[512,512]{1,0:T(8,128)(2,1)} %get-tuple-element.283), channel_id=1, source_target_pairs={{0,2},{1,3},{2,0},{3,1},{4,6},{5,7},{6,4},{7,5},{8,10},{9,11},{10,... | collective-permute-start | bytes 1572872 | tf_op jit(solution)/shard_map/ppermute | solution.py:555
  477.6 35.5 %collective-permute-start.49 = (bf16[512,512]{1,0:T(8,128)(2,1)}, bf16[512,512]{1,0:T(8,128)(2,1)}, u32[]{:S(2)}, u32[]{:S(2)}) collective-permute-start(bf16[512,512]{1,0:T(8,128)(2,1)} %get-tuple-element.284), channel_id=1, source_target_pairs={{0,3},{1,2},{2,1},{3,0},{4,7},{5,6},{6,5},{7,4},{8,11},{9,10},{10,... | collective-permute-start | bytes 1572872 | tf_op jit(solution)/shard_map/ppermute | solution.py:555
  (82 other events, 778.8 us)
Sparse Core Ops, SparseCore 0:
  13.1 77.0 all-gather.3
  92.0 37.4 all-gather.5
  131.4 93.6 all-gather.7
  286.9 84.0 reduce-scatter.3
  376.9 52.2 reduce-scatter.7
  438.4 101.2 reduce-scatter.5

commit v4 on v3

--- a/solution.py
+++ b/solution.py
@@ -822,9 +822,9 @@
     out_part = contract_tokens(mixed, back_rows).astype(BF)
     out_part, mlp_grad, grad_mixed, result_cut = fence(out_part, mlp_grad, grad_mixed, result_cut)
     out_grad = lax.psum_scatter(out_part, "row", scatter_dimension=1, tiled=True)
-    result_got = send_cols(result_cut[1], size)
+    result_a = send_cols([piece[first] for piece in result_cut[1]], size)
     lows = mixer_backward(heads, dk, dv, pres, shared, grad_mixed, saved)
-    lows, x_down, y_down, result_got = fence(lows, x_down, y_down, result_got)
+    lows, x_down, y_down, result_a = fence(lows, x_down, y_down, result_a)
     *lows, low_small, query_taps, key_taps, value_taps, params_part, gain_part = lows
     low = jnp.concatenate(lows + [low_small], axis=1)
     down_late = last_step(held_down, x_down, y_down, rows)
@@ -841,15 +841,17 @@
         )
         for step in range(size)
     ]
-    notes, hidden_cut, down_late = fence(notes, hidden_cut, down_late)
+    notes, hidden_cut, down_late, result_later = fence(notes, hidden_cut, down_late, result_cut[1])
 
     noted = sum([notes[0]] + send_cols(notes[1:], size))
     hidden_got = send_cols(hidden_cut[1], size)
+    result_b = send_cols([piece[last] for piece in result_later], size)
     first_inner, gains = noted[:tokens, None], noted[tokens:]
     sums = [query_taps, key_taps, value_taps, params_part[0:2, :heads], second_gain_part, gains]
     query_taps, key_taps, value_taps, params_grad, second_gain_grad, gains = lax.psum(sums, "row")
     norm_gain_grad, gain_grad = gains[:width], gains[width:]
-    result = add_cols(residual + result_cut[0], result_got)
+    result = residual + result_cut[0]
+    result = jnp.concatenate([add_cols(result[first], result_a), add_cols(result[last], result_b)], axis=0)
     down_grad = finish(*down_late).T
     mlp_grad = mlp_grad.astype(F32)
     out_grad = out_grad.astype(F32)

time: 558 us -> 554 us (level); the launches traced: 554 us -> 543 us
  waiting for transfers between devices: 175 us -> 161 us
    reduce_scatter x1, waiting for transfers between devices: 21.7 us -> 0.45 us  [per_device(): in_grad = lax.psum_scatter(in_part, 'row', scatter_dimension=0, tiled=True)]
    ppermute x48 -> x51, waiting for transfers between devices: 127 us -> 134 us  [hop(): return lax.ppermute(values, 'col', [(at, at ^ step) for at in range(size)])]
    ppermute x48 -> x51, starting transfers between devices: 105 us -> 102 us  [hop(): return lax.ppermute(values, 'col', [(at, at ^ step) for at in range(size)])]
  transfers between devices with their start and end apart: 59 -> 62, of which waited for: 19 -> 18; matrix products, arithmetic and copies ran while one was open for 24% -> 26% of each run, Pallas kernels for 11% -> 11%
where the time goes in v4:
time: 554 us; the launch traced here: 543 us
  waiting for transfers between devices  161 us (29%)
  starting transfers between devices  106 us (19%)
  matrix products  91.9 us (17%)
  Pallas kernels  62 us (11%)
  local copies, waits for them, and re-layouts  46.2 us (8%)
  other arithmetic  34.8 us (6%)
  blocking collectives  25.7 us (5%)
  between operations  15.7 us (3%)
    ppermute x51, waiting for transfers between devices, hop(): return lax.ppermute(values, 'col', [(at, at ^ step) for at in range(size)])  134 us
    ppermute x51, starting transfers between devices, hop(): return lax.ppermute(values, 'col', [(at, at ^ step) for at in range(size)])  102 us
    dot_general x11, matrix products, dot(): lax.dot_general(left, right, (((lc,), (rc,)), ((), ())), preferred_elemen...  71.9 us
    pallas_call x1, Pallas kernels, mixer_backward(): pl.pallas_call(functools.partial(backward_kernel, heads, dk, dv), grid=(2...  31.6 us
    pallas_call x1, Pallas kernels, mixer_forward(): pl.pallas_call(functools.partial(forward_kernel, heads, dk, dv), grid=(2,...  30.4 us
    psum x1, blocking collectives, per_device(): lax.psum(sums, 'row')  25.7 us
    all_gather x1, waiting for transfers between devices, per_device(): in_all = lax.all_gather(in_weight, 'row', axis=0, tiled=True)  24.8 us
    dot_general x5, matrix products, wide_dot(): return jnp.dot(left, right, preferred_element_type=F32)  20 us
  transfers between devices with their start and end apart: 62, of which 18 were waited for; matrix products, arithmetic and copies ran while one was open for 26% of the time, Pallas kernels for 11%

profile of v4, /device:TPU:0, one launch (start us, length us, event | category | flops | bytes accessed | tf_op | source)
XLA Modules:
  0.0 543.3 jit_solution(10858768438850170168)
XLA Ops:
  8.9 3.9 concatenate.98
  15.9 3.1 collective-permute-start.3
  19.0 2.6 collective-permute-start.4
  22.5 3.5 collective-permute-start.1
  32.5 12.7 %collective-permute-done = bf16[512,512]{1,0:T(8,128)(2,1)} collective-permute-done((bf16[512,512]{1,0:T(8,128)(2,1)}, bf16[512,512]{1,0:T(8,128)(2,1)}, u32[]{:S(2)}, u32[]{:S(2)}) %collective-permute-start) | collective-permute-done | bytes 524320 | tf_op jit(solution)/shard_map/ppermute | solution.py:555
  46.4 15.3 %collective-permute-done.1 = bf16[512,512]{1,0:T(8,128)(2,1)} collective-permute-done((bf16[512,512]{1,0:T(8,128)(2,1)}, bf16[512,512]{1,0:T(8,128)(2,1)}, u32[]{:S(2)}, u32[]{:S(2)}) %collective-permute-start.1) | collective-permute-done | bytes 524320 | tf_op jit(solution)/shard_map/ppermute | solution.py:555
  65.3 24.8 %all-gather.4.cloned.1.call-done.query_weight.key_weight.value_weight.gate_weight.small_weight = bf16[2048,3200]{1,0:T(8,128)(2,1)} async-done(((bf16[256,3200]{1,0:T(8,128)(2,1)}), bf16[2048,3200]{1,0:T(8,128)(2,1)}) %all-gather.4.cloned.1.call-update) | async-done | bytes 13107216 | tf_op jit(solution)/shard_map/all_gather | solution.py:708
  95.7 30.4 %mixer_forward.1 = (f32[512,512]{1,0:T(8,128)}, f32[512,512]{1,0:T(8,128)}, f32[512,1024]{1,0:T(8,128)}, f32[512,1024]{1,0:T(8,128)}, f32[512,128]{1,0:T(8,128)}...) custom-call(bf16[512,2048]{1,0:T(8,128)(2,1)} %fusion.16.hidden_ref,, ...), custom_call_target="tpu_custom_call" | custom-call | flops 20000000000 | bytes 20000000 | tf_op jit(solution)/shard_map/mixer_forward/pallas_call | solution.py:461
  127.3 2.7 collective-permute-done.7
  131.0 3.7 fusion.46
  134.8 12.1 %collective-permute-start.10 = (bf16[256,512]{1,0:T(8,128)(2,1)S(1)}, bf16[256,512]{1,0:T(8,128)(2,1)S(1)}, u32[]{:S(2)}, u32[]{:S(2)}) collective-permute-start(bf16[256,512]{1,0:T(8,128)(2,1)S(1)} %get-tuple-element.430), channel_id=1, source_target_pairs={{0,2},{1,3},{2,0},{3,1},{4,6},{5,7},{6,4},{7,5},{8,10},{9,11},{10,... | collective-permute-start | bytes 786440 | tf_op jit(solution)/shard_map/ppermute | solution.py:555
  151.8 13.6 %collective-permute-done.10 = bf16[256,512]{1,0:T(8,128)(2,1)S(1)} collective-permute-done((bf16[256,512]{1,0:T(8,128)(2,1)S(1)}, bf16[256,512]{1,0:T(8,128)(2,1)S(1)}, u32[]{:S(2)}, u32[]{:S(2)}) %collective-permute-start.10) | collective-permute-done | bytes 262176 | tf_op jit(solution)/shard_map/ppermute | solution.py:555
  165.5 4.9 collective-permute-start.12
  172.9 6.6 %collective-permute-done.12 = bf16[256,512]{1,0:T(8,128)(2,1)S(1)} collective-permute-done((bf16[256,512]{1,0:T(8,128)(2,1)S(1)}, bf16[256,512]{1,0:T(8,128)(2,1)S(1)}, u32[]{:S(2)}, u32[]{:S(2)}) %collective-permute-start.12) | collective-permute-done | bytes 262176 | tf_op jit(solution)/shard_map/ppermute | solution.py:555
  179.5 12.1 %collective-permute-done.13 = bf16[256,512]{1,0:T(8,128)(2,1)S(1)} collective-permute-done((bf16[256,512]{1,0:T(8,128)(2,1)S(1)}, bf16[256,512]{1,0:T(8,128)(2,1)S(1)}, u32[]{:S(2)}, u32[]{:S(2)}) %collective-permute-start.13) | collective-permute-done | bytes 262176 | tf_op jit(solution)/shard_map/ppermute | solution.py:555
  191.6 3.9 collective-permute-start.15
  198.2 6.0 %collective-permute-done.15 = bf16[256,512]{1,0:T(8,128)(2,1)S(1)} collective-permute-done((bf16[256,512]{1,0:T(8,128)(2,1)S(1)}, bf16[256,512]{1,0:T(8,128)(2,1)S(1)}, u32[]{:S(2)}, u32[]{:S(2)}) %collective-permute-start.15) | collective-permute-done | bytes 262176 | tf_op jit(solution)/shard_map/ppermute | solution.py:555
  204.2 11.6 %collective-permute-done.16 = bf16[256,512]{1,0:T(8,128)(2,1)S(1)} collective-permute-done((bf16[256,512]{1,0:T(8,128)(2,1)S(1)}, bf16[256,512]{1,0:T(8,128)(2,1)S(1)}, u32[]{:S(2)}, u32[]{:S(2)}) %collective-permute-start.16) | collective-permute-done | bytes 262176 | tf_op jit(solution)/shard_map/ppermute | solution.py:555
  215.8 4.0 collective-permute-start.18
  225.0 6.8 %fusion.6 = f32[256,2752]{0,1:T(8,128)S(1)} fusion(bf16[256,2048]{1,0:T(8,128)(2,1)} %fusion.25, bf16[4128,2048]{1,0:T(8,128)(2,1)} %all-gather.8.cloned.1.call-done), kind=kOutput, calls=%fused_computation.12 | convolution fusion | flops 2885681152 | bytes 15138816 | tf_op jit(solution)/shard_map/dot_general | solution.py:17
  231.9 5.8 %multiply_convert_fusion.4 = (bf16[256,1376]{0,1:T(8,128)(2,1)S(1)}, bf16[256,1376]{0,1:T(8,128)(2,1)S(1)}, bf16[256,1376]{0,1:T(8,128)(2,1)}) fusion(f32[256,2752]{0,1:T(8,128)S(1)} %fusion.6, bf16[4128,2048]{1,0:T(8,128)(2,1)} %all-gather.8.cloned.1.call-done, bf16[512,2048]{1,0:T(8,128)(2,1)S(1)} %constant_dynamic-update-slice_fusion.25), kind=kOutput, calls=%fused_computation.61 | convolution fusion | flops 1448124416 | bytes 11616256 | tf_op jit(solution)/shard_map/dot_general | solution.py:17
  237.7 3.3 fusion.26
  241.2 3.0 collective-permute-start.24
  253.4 6.0 %fusion.2 = f32[256,2752]{0,1:T(8,128)S(1)} fusion(bf16[256,2048]{1,0:T(8,128)(2,1)S(1)} %fusion.29, bf16[4128,2048]{1,0:T(8,128)(2,1)} %all-gather.8.cloned.1.call-done), kind=kOutput, calls=%fused_computation.8 | convolution fusion | flops 2885681152 | bytes 15138816 | tf_op jit(solution)/shard_map/dot_general | solution.py:17
  259.4 5.7 %multiply_convert_fusion.1 = (bf16[256,1376]{0,1:T(8,128)(2,1)S(1)}, bf16[256,1376]{0,1:T(8,128)(2,1)S(1)}, bf16[256,1376]{0,1:T(8,128)(2,1)}) fusion(f32[256,2752]{0,1:T(8,128)S(1)} %fusion.2, bf16[4128,2048]{1,0:T(8,128)(2,1)} %all-gather.8.cloned.1.call-done, bf16[512,2048]{1,0:T(8,128)(2,1)S(1)} %constant_dynamic-update-slice_fusion.25), kind=kOutput, calls=%fused_computation.56 | convolution fusion | flops 1448124416 | bytes 11616256 | tf_op jit(solution)/shard_map/dot_general | solution.py:17
  265.3 6.2 %fusion.30 = (f32[256]{0:T(256)S(1)}, f32[256,2048]{1,0:T(8,128)S(1)}) fusion(bf16[256,2048]{1,0:T(8,128)(2,1)S(1)} %constant_dynamic-update-slice_fusion.17, f32[2048]{0:T(1024)S(1)} %bitcast.55, bf16[4128,2048]{1,0:T(8,128)(2,1)} %all-gather.8.cloned.1.call-done, bf16[256,1376]{0,1:T(8,128)(2,1)S(1)} %get-tuple-element.393, ...), kind=kOutput, calls=%fused_computation.46 | convolution fusion | flops 2890596096 | bytes 15836160 | tf_op jit(solution)/shard_map/dot_general | solution.py:535
  273.9 3.8 collective-permute-done.26
  277.8 8.9 %convolution_convert_fusion.1 = bf16[2048,2752]{0,1:T(8,128)(2,1)} fusion(bf16[256,2752]{0,1:T(8,128)(2,1)S(1)} %pad_maximum_fusion.3, bf16[256,2752]{0,1:T(8,128)(2,1)S(1)} %pad_maximum_fusion.2, bf16[256,2048]{1,0:T(8,128)(2,1)S(1)} %fusion.29, bf16[256,2048]{1,0:T(8,128)(2,1)S(1)} %copy-done.32), kind=kOutput, calls=%fused_computation.1 | convolution fusion | flops 5786828800 | bytes 16187392 | tf_op jit(solution)/shard_map/dot_general | solution.py:17
  304.2 7.5 %collective-permute-done.28 = bf16[256,512]{1,0:T(8,128)(2,1)S(1)} collective-permute-done((bf16[256,512]{1,0:T(8,128)(2,1)}, bf16[256,512]{1,0:T(8,128)(2,1)S(1)}, u32[]{:S(2)}, u32[]{:S(2)}) %collective-permute-start.28) | collective-permute-done | bytes 262176 | tf_op jit(solution)/shard_map/ppermute | solution.py:555
  311.7 4.3 collective-permute-start.33
  319.5 7.9 %collective-permute-done.33 = bf16[256,512]{1,0:T(8,128)(2,1)S(1)} collective-permute-done((bf16[256,512]{1,0:T(8,128)(2,1)S(1)}, bf16[256,512]{1,0:T(8,128)(2,1)S(1)}, u32[]{:S(2)}, u32[]{:S(2)}) %collective-permute-start.33) | collective-permute-done | bytes 262176 | tf_op jit(solution)/shard_map/ppermute | solution.py:555
  327.5 9.9 %collective-permute-done.34 = bf16[256,512]{1,0:T(8,128)(2,1)S(1)} collective-permute-done((bf16[256,512]{1,0:T(8,128)(2,1)S(1)}, bf16[256,512]{1,0:T(8,128)(2,1)S(1)}, u32[]{:S(2)}, u32[]{:S(2)}) %collective-permute-start.34) | collective-permute-done | bytes 262176 | tf_op jit(solution)/shard_map/ppermute | solution.py:555
  337.4 5.5 %collective-permute-start.37 = (bf16[256,512]{1,0:T(8,128)(2,1)S(1)}, bf16[256,512]{1,0:T(8,128)(2,1)S(1)}, u32[]{:S(2)}, u32[]{:S(2)}) collective-permute-start(bf16[256,512]{1,0:T(8,128)(2,1)S(1)} %convert_element_type.279), channel_id=1, source_target_pairs={{0,1},{1,0},{2,3},{3,2},{4,5},{5,4},{6,7},{7,6},{8,9},{9,8},{10,11... | collective-permute-start | bytes 786440 | tf_op jit(solution)/shard_map/ppermute | solution.py:555
  345.6 5.5 %fusion.8 = f32[512,2048]{1,0:T(8,128)S(1)} fusion(bf16[512,1376]{0,1:T(8,128)(2,1)S(1)} %constant_dynamic-update-slice_fusion, bf16[4128,2048]{1,0:T(8,128)(2,1)} %all-gather.8.cloned.1.call-done), kind=kOutput, calls=%fused_computation.15 | convolution fusion | flops 2885681152 | bytes 11239424 | tf_op jit(solution)/shard_map/dot_general | solution.py:535
  356.1 8.3 %collective-permute-done.38 = bf16[256,512]{1,0:T(8,128)(2,1)S(1)} collective-permute-done((bf16[256,512]{1,0:T(8,128)(2,1)S(1)}, bf16[256,512]{1,0:T(8,128)(2,1)S(1)}, u32[]{:S(2)}, u32[]{:S(2)}) %collective-permute-start.38) | collective-permute-done | bytes 262176 | tf_op jit(solution)/shard_map/ppermute | solution.py:555
  365.6 4.4 convolution_convert_fusion.3
  370.0 6.6 %fusion.36.grad_ref = f32[512,1024]{1,0:T(8,128)} fusion(bf16[1024,2048]{1,0:T(8,128)(2,1)} %all-gather.6.cloned.1.call-done, bf16[256,2048]{1,0:T(8,128)(2,1)} %copy-done.30, bf16[256,2048]{1,0:T(8,128)(2,1)} %copy-done.31), kind=kOutput, calls=%fused_computation.65 | convolution fusion | flops 2151677952 | bytes 8388608 | tf_op jit(solution)/shard_map/dot_general | solution.py:17
  379.3 4.4 collective-permute-start.42
  386.3 31.6 %mixer_backward.1 = (bf16[512,512]{1,0:T(8,128)(2,1)}, bf16[512,512]{1,0:T(8,128)(2,1)}, bf16[512,1024]{1,0:T(8,128)(2,1)}, bf16[512,1024]{1,0:T(8,128)(2,1)}, b...) custom-call(f32[512,512]{1,0:T(8,128)} %get-tuple-element.172.query_, ...), custom_call_target="tpu_custom_call" | custom-call | flops 20000000000 | bytes 20000000 | tf_op jit(solution)/shard_map/mixer_backward/pallas_call | solution.py:497
  423.8 10.4 %convolution_convert_fusion = bf16[2048,3200]{1,0:T(8,128)(2,1)} fusion(bf16[512,2048]{1,0:T(8,128)(2,1)S(1)} %copy-done.23, bf16[512,3200]{1,0:T(8,128)(2,1)S(1)} %constant_dynamic-update-slice_fusion.2), kind=kOutput, calls=%fused_computation | convolution fusion | flops 6717440000 | bytes 18481152 | tf_op jit(solution)/shard_map/dot_general | solution.py:17
  443.1 14.1 %fusion.19 = (f32[2048]{0:T(1024)S(1)}, f32[512]{0:T(512)S(1)}, f32[512,2048]{1,0:T(8,128)S(1)}) fusion(bf16[512,2048]{1,0:T(8,128)(2,1)S(1)} %copy-done.1, f32[512]{0:T(512)S(1)} %copy-done.52, f32[2048]{0:T(1024)S(1)} %bitcast.60, bf16[512,3200]{1,0:T(8,128)(2,1)} %copy-done.46, ...), kind=kOutput, calls=%fused_computation.26 | convolution fusion | flops 6718223872 | bytes 22695936 | tf_op jit(solution)/shard_map/dot_general | solution.py:17
  461.9 2.6 collective-permute-start.52
  469.8 2.6 collective-permute-start.55
  474.2 25.7 %all-reduce.1 = (f32[4,512]{1,0:T(4,128)}, f32[768]{0:T(1024)S(1)}, f32[4,512]{1,0:T(4,128)}, f32[4,1024]{1,0:T(4,128)}, f32[2,4]{1,0:T(2,128)S(1)}, /*index=5*/f32[512]{0:T(512)}) all-reduce(f32[4,512]{1,0:T(4,128)S(1)} %copy-done.58, f32[768]{0:T(1024)S(1)} %slice.291, ...), channel_id=1, replica_groups=mesh['row'=8,'col'=4] {'row'}, use_global_device_ids=true, to_apply=%region_10.11 | all-reduce | flops 9480 | bytes 75840 | tf_op jit(solution)/shard_map/psum | solution.py:851
  499.9 2.6 collective-permute-start.49
  509.5 14.1 %collective-permute-done.48 = bf16[512,512]{1,0:T(8,128)(2,1)} collective-permute-done((bf16[512,512]{1,0:T(8,128)(2,1)}, bf16[512,512]{1,0:T(8,128)(2,1)}, u32[]{:S(2)}, u32[]{:S(2)}) %collective-permute-start.48) | collective-permute-done | bytes 524320 | tf_op jit(solution)/shard_map/ppermute | solution.py:555
  523.6 3.2 fusion.37
  529.0 2.8 slice_convert_fusion
  (383 shorter events, 126.6 us)
Async XLA Ops:
  7.2 82.9 %all-gather.4.cloned.1.call-start = ((), (), s32[]{:S(2)}) async-start(), calls=%async_computation.3 | async-start | bytes 14745600 | tf_op jit(solution)/shard_map/all_gather | solution.py:708
  12.9 118.1 %all-gather.6.cloned.1.call-start = ((), (), s32[]{:S(2)}) async-start(), calls=%async_computation.4 | async-start | bytes 4718592 | tf_op jit(solution)/shard_map/all_gather | solution.py:709
  13.6 211.4 %all-gather.8.cloned.1.call-start = ((), (), s32[]{:S(2)}) async-start(), calls=%async_computation.5 | async-start | bytes 19021824 | tf_op jit(solution)/shard_map/all_gather | solution.py:712
  15.3 361.3 %reduce-scatter.4.cloned.1.call-start = ((), (), s32[]{:S(2)}) async-start(), calls=%async_computation.6 | async-start | bytes 12681216 | tf_op jit(solution)/shard_map/reduce_scatter | solution.py:797
  15.9 16.5 %collective-permute-start.3 = (f32[2,512]{1,0:T(2,128)S(1)}, f32[2,512]{1,0:T(2,128)S(1)}, u32[]{:S(2)}, u32[]{:S(2)}) collective-permute-start(f32[2,512]{1,0:T(2,128)S(1)} %get-tuple-element.452), channel_id=1, source_target_pairs={{0,1},{1,0},{2,3},{3,2},{4,5},{5,4},{6,7},{7,6},{8,9},{9,8},{10,11... | collective-permute-start | bytes 12296 | tf_op jit(solution)/shard_map/ppermute | solution.py:555
  21.6 23.6 %collective-permute-start = (bf16[512,512]{1,0:T(8,128)(2,1)}, bf16[512,512]{1,0:T(8,128)(2,1)}, u32[]{:S(2)}, u32[]{:S(2)}) collective-permute-start(bf16[512,512]{1,0:T(8,128)(2,1)} %param.21), channel_id=1, source_target_pairs={{0,1},{1,0},{2,3},{3,2},{4,5},{5,4},{6,7},{7,6},{8,9},{9,8},{10,11... | collective-permute-start | bytes 1572872 | tf_op jit(solution)/shard_map/ppermute | solution.py:555
  22.5 39.1 %collective-permute-start.1 = (bf16[512,512]{1,0:T(8,128)(2,1)}, bf16[512,512]{1,0:T(8,128)(2,1)}, u32[]{:S(2)}, u32[]{:S(2)}) collective-permute-start(bf16[512,512]{1,0:T(8,128)(2,1)} %param.21), channel_id=1, source_target_pairs={{0,2},{1,3},{2,0},{3,1},{4,6},{5,7},{6,4},{7,5},{8,10},{9,11},{10,... | collective-permute-start | bytes 1572872 | tf_op jit(solution)/shard_map/ppermute | solution.py:555
  32.4 30.3 %collective-permute-start.2 = (bf16[512,512]{1,0:T(8,128)(2,1)}, bf16[512,512]{1,0:T(8,128)(2,1)S(1)}, u32[]{:S(2)}, u32[]{:S(2)}) collective-permute-start(bf16[512,512]{1,0:T(8,128)(2,1)} %param.21), channel_id=1, source_target_pairs={{0,3},{1,2},{2,1},{3,0},{4,7},{5,6},{6,5},{7,4},{8,11},{9,10},{10,... | collective-permute-start | bytes 1572872 | tf_op jit(solution)/shard_map/ppermute | solution.py:555
  90.1 37.1 %collective-permute-start.6 = (bf16[512,512]{1,0:T(8,128)(2,1)}, bf16[512,512]{1,0:T(8,128)(2,1)S(1)}, u32[]{:S(2)}, u32[]{:S(2)}) collective-permute-start(bf16[512,512]{1,0:T(8,128)(2,1)} %param.41), channel_id=1, source_target_pairs={{0,1},{1,0},{2,3},{3,2},{4,5},{5,4},{6,7},{7,6},{8,9},{9,8},{10,11... | collective-permute-start | bytes 1572872 | tf_op jit(solution)/shard_map/ppermute | solution.py:555
  91.6 38.4 %collective-permute-start.7 = (bf16[512,512]{1,0:T(8,128)(2,1)}, bf16[512,512]{1,0:T(8,128)(2,1)S(1)}, u32[]{:S(2)}, u32[]{:S(2)}) collective-permute-start(bf16[512,512]{1,0:T(8,128)(2,1)} %param.41), channel_id=1, source_target_pairs={{0,2},{1,3},{2,0},{3,1},{4,6},{5,7},{6,4},{7,5},{8,10},{9,11},{10,... | collective-permute-start | bytes 1572872 | tf_op jit(solution)/shard_map/ppermute | solution.py:555
  94.0 36.1 %collective-permute-start.8 = (bf16[512,512]{1,0:T(8,128)(2,1)}, bf16[512,512]{1,0:T(8,128)(2,1)S(1)}, u32[]{:S(2)}, u32[]{:S(2)}) collective-permute-start(bf16[512,512]{1,0:T(8,128)(2,1)} %param.41), channel_id=1, source_target_pairs={{0,3},{1,2},{2,1},{3,0},{4,7},{5,6},{6,5},{7,4},{8,11},{9,10},{10,... | collective-permute-start | bytes 1572872 | tf_op jit(solution)/shard_map/ppermute | solution.py:555
  134.8 30.6 %collective-permute-start.10 = (bf16[256,512]{1,0:T(8,128)(2,1)S(1)}, bf16[256,512]{1,0:T(8,128)(2,1)S(1)}, u32[]{:S(2)}, u32[]{:S(2)}) collective-permute-start(bf16[256,512]{1,0:T(8,128)(2,1)S(1)} %get-tuple-element.430), channel_id=1, source_target_pairs={{0,2},{1,3},{2,0},{3,1},{4,6},{5,7},{6,4},{7,5},{8,10},{9,11},{10,... | collective-permute-start | bytes 786440 | tf_op jit(solution)/shard_map/ppermute | solution.py:555
  146.9 18.5 %collective-permute-start.11 = (bf16[256,512]{1,0:T(8,128)(2,1)S(1)}, bf16[256,512]{1,0:T(8,128)(2,1)S(1)}, u32[]{:S(2)}, u32[]{:S(2)}) collective-permute-start(bf16[256,512]{1,0:T(8,128)(2,1)S(1)} %get-tuple-element.429), channel_id=1, source_target_pairs={{0,3},{1,2},{2,1},{3,0},{4,7},{5,6},{6,5},{7,4},{8,11},{9,10},{10,... | collective-permute-start | bytes 786440 | tf_op jit(solution)/shard_map/ppermute | solution.py:555
  148.4 17.1 %collective-permute-start.9 = (bf16[256,512]{1,0:T(8,128)(2,1)S(1)}, bf16[256,512]{1,0:T(8,128)(2,1)S(1)}, u32[]{:S(2)}, u32[]{:S(2)}) collective-permute-start(bf16[256,512]{1,0:T(8,128)(2,1)S(1)} %get-tuple-element.431), channel_id=1, source_target_pairs={{0,1},{1,0},{2,3},{3,2},{4,5},{5,4},{6,7},{7,6},{8,9},{9,8},{10,11... | collective-permute-start | bytes 786440 | tf_op jit(solution)/shard_map/ppermute | solution.py:555
  170.3 21.3 %collective-permute-start.13 = (bf16[256,512]{1,0:T(8,128)(2,1)S(1)}, bf16[256,512]{1,0:T(8,128)(2,1)S(1)}, u32[]{:S(2)}, u32[]{:S(2)}) collective-permute-start(bf16[256,512]{1,0:T(8,128)(2,1)S(1)} %get-tuple-element.182), channel_id=1, source_target_pairs={{0,2},{1,3},{2,0},{3,1},{4,6},{5,7},{6,4},{7,5},{8,10},{9,11},{10,... | collective-permute-start | bytes 786440 | tf_op jit(solution)/shard_map/ppermute | solution.py:555
  170.3 21.3 %collective-permute-start.14 = (bf16[256,512]{1,0:T(8,128)(2,1)S(1)}, bf16[256,512]{1,0:T(8,128)(2,1)S(1)}, u32[]{:S(2)}, u32[]{:S(2)}) collective-permute-start(bf16[256,512]{1,0:T(8,128)(2,1)S(1)} %get-tuple-element.183), channel_id=1, source_target_pairs={{0,3},{1,2},{2,1},{3,0},{4,7},{5,6},{6,5},{7,4},{8,11},{9,10},{10,... | collective-permute-start | bytes 786440 | tf_op jit(solution)/shard_map/ppermute | solution.py:555
  195.6 20.2 %collective-permute-start.16 = (bf16[256,512]{1,0:T(8,128)(2,1)S(1)}, bf16[256,512]{1,0:T(8,128)(2,1)S(1)}, u32[]{:S(2)}, u32[]{:S(2)}) collective-permute-start(bf16[256,512]{1,0:T(8,128)(2,1)S(1)} %convert_element_type.251), channel_id=1, source_target_pairs={{0,2},{1,3},{2,0},{3,1},{4,6},{5,7},{6,4},{7,5},{8,10},{9,11},{10,... | collective-permute-start | bytes 786440 | tf_op jit(solution)/shard_map/ppermute | solution.py:555
  195.6 20.2 %collective-permute-start.17 = (bf16[256,512]{1,0:T(8,128)(2,1)S(1)}, bf16[256,512]{1,0:T(8,128)(2,1)S(1)}, u32[]{:S(2)}, u32[]{:S(2)}) collective-permute-start(bf16[256,512]{1,0:T(8,128)(2,1)S(1)} %convert_element_type.251), channel_id=1, source_target_pairs={{0,3},{1,2},{2,1},{3,0},{4,7},{5,6},{6,5},{7,4},{8,11},{9,10},{10,... | collective-permute-start | bytes 786440 | tf_op jit(solution)/shard_map/ppermute | solution.py:555
  215.8 25.4 %collective-permute-start.18 = (bf16[256,512]{1,0:T(8,128)(2,1)S(1)}, bf16[256,512]{1,0:T(8,128)(2,1)}, u32[]{:S(2)}, u32[]{:S(2)}) collective-permute-start(bf16[256,512]{1,0:T(8,128)(2,1)S(1)} %convert_element_type.255), channel_id=1, source_target_pairs={{0,1},{1,0},{2,3},{3,2},{4,5},{5,4},{6,7},{7,6},{8,9},{9,8},{10,11... | collective-permute-start | bytes 786440 | tf_op jit(solution)/shard_map/ppermute | solution.py:555
  219.8 21.4 %collective-permute-start.19 = (bf16[256,512]{1,0:T(8,128)(2,1)S(1)}, bf16[256,512]{1,0:T(8,128)(2,1)}, u32[]{:S(2)}, u32[]{:S(2)}) collective-permute-start(bf16[256,512]{1,0:T(8,128)(2,1)S(1)} %convert_element_type.255), channel_id=1, source_target_pairs={{0,2},{1,3},{2,0},{3,1},{4,6},{5,7},{6,4},{7,5},{8,10},{9,11},{10,... | collective-permute-start | bytes 786440 | tf_op jit(solution)/shard_map/ppermute | solution.py:555
  219.8 21.4 %collective-permute-start.20 = (bf16[256,512]{1,0:T(8,128)(2,1)S(1)}, bf16[256,512]{1,0:T(8,128)(2,1)}, u32[]{:S(2)}, u32[]{:S(2)}) collective-permute-start(bf16[256,512]{1,0:T(8,128)(2,1)S(1)} %convert_element_type.255), channel_id=1, source_target_pairs={{0,3},{1,2},{2,1},{3,0},{4,7},{5,6},{6,5},{7,4},{8,11},{9,10},{10,... | collective-permute-start | bytes 786440 | tf_op jit(solution)/shard_map/ppermute | solution.py:555
  241.2 31.1 %collective-permute-start.24 = (f32[256]{0:T(256)S(1)}, f32[256]{0:T(256)S(1)}, u32[]{:S(2)}, u32[]{:S(2)}) collective-permute-start(f32[256]{0:T(256)S(1)} %get-tuple-element.218), channel_id=1, source_target_pairs={{0,1},{1,0},{2,3},{3,2},{4,5},{5,4},{6,7},{7,6},{8,9},{9,8},{10,11... | collective-permute-start | bytes 3080 | tf_op jit(solution)/shard_map/ppermute | solution.py:555
  244.3 29.6 %collective-permute-start.25 = (f32[256]{0:T(256)S(1)}, f32[256]{0:T(256)S(1)}, u32[]{:S(2)}, u32[]{:S(2)}) collective-permute-start(f32[256]{0:T(256)S(1)} %get-tuple-element.218), channel_id=1, source_target_pairs={{0,2},{1,3},{2,0},{3,1},{4,6},{5,7},{6,4},{7,5},{8,10},{9,11},{10,... | collective-permute-start | bytes 3080 | tf_op jit(solution)/shard_map/ppermute | solution.py:555
  248.9 28.8 %collective-permute-start.21 = (bf16[256,512]{1,0:T(8,128)(2,1)S(1)}, bf16[256,512]{1,0:T(8,128)(2,1)}, u32[]{:S(2)}, u32[]{:S(2)}) collective-permute-start(bf16[256,512]{1,0:T(8,128)(2,1)S(1)} %get-tuple-element.201), channel_id=1, source_target_pairs={{0,1},{1,0},{2,3},{3,2},{4,5},{5,4},{6,7},{7,6},{8,9},{9,8},{10,11... | collective-permute-start | bytes 786440 | tf_op jit(solution)/shard_map/ppermute | solution.py:555
  249.6 28.2 %collective-permute-start.22 = (bf16[256,512]{1,0:T(8,128)(2,1)S(1)}, bf16[256,512]{1,0:T(8,128)(2,1)}, u32[]{:S(2)}, u32[]{:S(2)}) collective-permute-start(bf16[256,512]{1,0:T(8,128)(2,1)S(1)} %get-tuple-element.202), channel_id=1, source_target_pairs={{0,2},{1,3},{2,0},{3,1},{4,6},{5,7},{6,4},{7,5},{8,10},{9,11},{10,... | collective-permute-start | bytes 786440 | tf_op jit(solution)/shard_map/ppermute | solution.py:555
  251.1 26.7 %collective-permute-start.23 = (bf16[256,512]{1,0:T(8,128)(2,1)S(1)}, bf16[256,512]{1,0:T(8,128)(2,1)}, u32[]{:S(2)}, u32[]{:S(2)}) collective-permute-start(bf16[256,512]{1,0:T(8,128)(2,1)S(1)} %get-tuple-element.203), channel_id=1, source_target_pairs={{0,3},{1,2},{2,1},{3,0},{4,7},{5,6},{6,5},{7,4},{8,11},{9,10},{10,... | collective-permute-start | bytes 786440 | tf_op jit(solution)/shard_map/ppermute | solution.py:555
  286.7 220.5 %reduce-scatter.8.cloned.1.call-start = ((), (), s32[]{:S(2)}) async-start(), calls=%async_computation.8 | async-start | bytes 4718592 | tf_op jit(solution)/shard_map/reduce_scatter | solution.py:824
  292.2 19.4 %collective-permute-start.28 = (bf16[256,512]{1,0:T(8,128)(2,1)}, bf16[256,512]{1,0:T(8,128)(2,1)S(1)}, u32[]{:S(2)}, u32[]{:S(2)}) collective-permute-start(bf16[256,512]{1,0:T(8,128)(2,1)} %get-tuple-element.210), channel_id=1, source_target_pairs={{0,2},{1,3},{2,0},{3,1},{4,6},{5,7},{6,4},{7,5},{8,10},{9,11},{10,... | collective-permute-start | bytes 786440 | tf_op jit(solution)/shard_map/ppermute | solution.py:555
  311.7 25.7 %collective-permute-start.36 = (bf16[1024,1376]{0,1:T(8,128)(2,1)S(1)}, bf16[1024,1376]{0,1:T(8,128)(2,1)S(1)}, u32[]{:S(2)}, u32[]{:S(2)}) collective-permute-start(bf16[1024,1376]{0,1:T(8,128)(2,1)S(1)} %convolution_convert_fusion.2), channel_id=1, source_target_pairs={{0,4},{4,0},{8,12},{12,8},{16,20},{20,16},{24,28},{28,24},{1,5},{5... | collective-permute-start | bytes 8454152 | tf_op jit(solution)/shard_map/ppermute | solution.py:597
  316.0 21.3 %collective-permute-start.34 = (bf16[256,512]{1,0:T(8,128)(2,1)S(1)}, bf16[256,512]{1,0:T(8,128)(2,1)S(1)}, u32[]{:S(2)}, u32[]{:S(2)}) collective-permute-start(bf16[256,512]{1,0:T(8,128)(2,1)S(1)} %convert_element_type.274), channel_id=1, source_target_pairs={{0,2},{1,3},{2,0},{3,1},{4,6},{5,7},{6,4},{7,5},{8,10},{9,11},{10,... | collective-permute-start | bytes 786440 | tf_op jit(solution)/shard_map/ppermute | solution.py:555
  316.1 21.3 %collective-permute-start.35 = (bf16[256,512]{1,0:T(8,128)(2,1)S(1)}, bf16[256,512]{1,0:T(8,128)(2,1)S(1)}, u32[]{:S(2)}, u32[]{:S(2)}) collective-permute-start(bf16[256,512]{1,0:T(8,128)(2,1)S(1)} %convert_element_type.274), channel_id=1, source_target_pairs={{0,3},{1,2},{2,1},{3,0},{4,7},{5,6},{6,5},{7,4},{8,11},{9,10},{10,... | collective-permute-start | bytes 786440 | tf_op jit(solution)/shard_map/ppermute | solution.py:555
  337.4 18.7 %collective-permute-start.37 = (bf16[256,512]{1,0:T(8,128)(2,1)S(1)}, bf16[256,512]{1,0:T(8,128)(2,1)S(1)}, u32[]{:S(2)}, u32[]{:S(2)}) collective-permute-start(bf16[256,512]{1,0:T(8,128)(2,1)S(1)} %convert_element_type.279), channel_id=1, source_target_pairs={{0,1},{1,0},{2,3},{3,2},{4,5},{5,4},{6,7},{7,6},{8,9},{9,8},{10,11... | collective-permute-start | bytes 786440 | tf_op jit(solution)/shard_map/ppermute | solution.py:555
  343.0 21.4 %collective-permute-start.38 = (bf16[256,512]{1,0:T(8,128)(2,1)S(1)}, bf16[256,512]{1,0:T(8,128)(2,1)S(1)}, u32[]{:S(2)}, u32[]{:S(2)}) collective-permute-start(bf16[256,512]{1,0:T(8,128)(2,1)S(1)} %convert_element_type.279), channel_id=1, source_target_pairs={{0,2},{1,3},{2,0},{3,1},{4,6},{5,7},{6,4},{7,5},{8,10},{9,11},{10,... | collective-permute-start | bytes 786440 | tf_op jit(solution)/shard_map/ppermute | solution.py:555
  343.0 21.3 %collective-permute-start.39 = (bf16[256,512]{1,0:T(8,128)(2,1)S(1)}, bf16[256,512]{1,0:T(8,128)(2,1)S(1)}, u32[]{:S(2)}, u32[]{:S(2)}) collective-permute-start(bf16[256,512]{1,0:T(8,128)(2,1)S(1)} %convert_element_type.279), channel_id=1, source_target_pairs={{0,3},{1,2},{2,1},{3,0},{4,7},{5,6},{6,5},{7,4},{8,11},{9,10},{10,... | collective-permute-start | bytes 786440 | tf_op jit(solution)/shard_map/ppermute | solution.py:555
  376.6 152.4 %reduce-scatter.6.cloned.1.call-start = ((), (), s32[]{:S(2)}) async-start(), calls=%async_computation.7 | async-start | bytes 14745600 | tf_op jit(solution)/shard_map/reduce_scatter | solution.py:833
  377.0 40.9 %collective-permute-start.41 = (bf16[256,1376]{0,1:T(8,128)(2,1)S(1)}, bf16[256,1376]{0,1:T(8,128)(2,1)S(1)}, u32[]{:S(2)}, u32[]{:S(2)}) collective-permute-start(bf16[256,1376]{0,1:T(8,128)(2,1)S(1)} %pad_maximum_fusion.10), channel_id=1, source_target_pairs={{0,16},{4,20},{8,24},{12,28},{16,0},{20,4},{24,8},{28,12},{1,17},{... | collective-permute-start | bytes 2113544 | tf_op jit(solution)/shard_map/ppermute | solution.py:597
  377.8 40.2 %collective-permute-start.40 = (bf16[256,1376]{0,1:T(8,128)(2,1)S(1)}, bf16[256,1376]{0,1:T(8,128)(2,1)S(1)}, u32[]{:S(2)}, u32[]{:S(2)}) collective-permute-start(bf16[256,1376]{0,1:T(8,128)(2,1)S(1)} %pad_maximum_fusion.9), channel_id=1, source_target_pairs={{0,8},{4,12},{8,0},{12,4},{16,24},{20,28},{24,16},{28,20},{1,9},{5... | collective-permute-start | bytes 2113544 | tf_op jit(solution)/shard_map/ppermute | solution.py:597
  379.3 38.7 %collective-permute-start.42 = (bf16[256,512]{1,0:T(8,128)(2,1)S(1)}, bf16[256,512]{1,0:T(8,128)(2,1)S(1)}, u32[]{:S(2)}, u32[]{:S(2)}) collective-permute-start(bf16[256,512]{1,0:T(8,128)(2,1)S(1)} %slice.247), channel_id=1, source_target_pairs={{0,1},{1,0},{2,3},{3,2},{4,5},{5,4},{6,7},{7,6},{8,9},{9,8},{10,11... | collective-permute-start | bytes 786440 | tf_op jit(solution)/shard_map/ppermute | solution.py:555
  383.7 34.2 %collective-permute-start.43 = (bf16[256,512]{1,0:T(8,128)(2,1)S(1)}, bf16[256,512]{1,0:T(8,128)(2,1)S(1)}, u32[]{:S(2)}, u32[]{:S(2)}) collective-permute-start(bf16[256,512]{1,0:T(8,128)(2,1)S(1)} %slice.248), channel_id=1, source_target_pairs={{0,2},{1,3},{2,0},{3,1},{4,6},{5,7},{6,4},{7,5},{8,10},{9,11},{10,... | collective-permute-start | bytes 786440 | tf_op jit(solution)/shard_map/ppermute | solution.py:555
  383.9 34.2 %collective-permute-start.44 = (bf16[256,512]{1,0:T(8,128)(2,1)S(1)}, bf16[256,512]{1,0:T(8,128)(2,1)S(1)}, u32[]{:S(2)}, u32[]{:S(2)}) collective-permute-start(bf16[256,512]{1,0:T(8,128)(2,1)S(1)} %slice.249), channel_id=1, source_target_pairs={{0,3},{1,2},{2,1},{3,0},{4,7},{5,6},{6,5},{7,4},{8,11},{9,10},{10,... | collective-permute-start | bytes 786440 | tf_op jit(solution)/shard_map/ppermute | solution.py:555
  440.1 19.8 %collective-permute-start.45 = (bf16[128,1376]{0,1:T(8,128)(2,1)S(1)}, bf16[128,1376]{0,1:T(8,128)(2,1)S(1)}, u32[]{:S(2)}, u32[]{:S(2)}) collective-permute-start(bf16[128,1376]{0,1:T(8,128)(2,1)S(1)} %get-tuple-element.405), channel_id=1, source_target_pairs={{0,8},{4,12},{8,0},{12,4},{16,24},{20,28},{24,16},{28,20},{1,9},{5... | collective-permute-start | bytes 1056776 | tf_op jit(solution)/shard_map/ppermute | solution.py:597
  440.2 19.8 %collective-permute-start.46 = (bf16[128,1376]{0,1:T(8,128)(2,1)S(1)}, bf16[128,1376]{0,1:T(8,128)(2,1)S(1)}, u32[]{:S(2)}, u32[]{:S(2)}) collective-permute-start(bf16[128,1376]{0,1:T(8,128)(2,1)S(1)} %get-tuple-element.404), channel_id=1, source_target_pairs={{0,16},{4,20},{8,24},{12,28},{16,0},{20,4},{24,8},{28,12},{1,17},{... | collective-permute-start | bytes 1056776 | tf_op jit(solution)/shard_map/ppermute | solution.py:597
  465.2 34.7 %collective-permute-start.53 = (bf16[256,512]{1,0:T(8,128)(2,1)}, bf16[256,512]{1,0:T(8,128)(2,1)}, u32[]{:S(2)}, u32[]{:S(2)}) collective-permute-start(bf16[256,512]{1,0:T(8,128)(2,1)} %slice.260), channel_id=1, source_target_pairs={{0,1},{1,0},{2,3},{3,2},{4,5},{5,4},{6,7},{7,6},{8,9},{9,8},{10,11... | collective-permute-start | bytes 786440 | tf_op jit(solution)/shard_map/ppermute | solution.py:555
  466.0 38.2 %collective-permute-start.54 = (bf16[256,512]{1,0:T(8,128)(2,1)}, bf16[256,512]{1,0:T(8,128)(2,1)}, u32[]{:S(2)}, u32[]{:S(2)}) collective-permute-start(bf16[256,512]{1,0:T(8,128)(2,1)} %slice.261), channel_id=1, source_target_pairs={{0,2},{1,3},{2,0},{3,1},{4,6},{5,7},{6,4},{7,5},{8,10},{9,11},{10,... | collective-permute-start | bytes 786440 | tf_op jit(solution)/shard_map/ppermute | solution.py:555
  469.8 34.4 %collective-permute-start.55 = (bf16[256,512]{1,0:T(8,128)(2,1)}, bf16[256,512]{1,0:T(8,128)(2,1)}, u32[]{:S(2)}, u32[]{:S(2)}) collective-permute-start(bf16[256,512]{1,0:T(8,128)(2,1)} %slice.262), channel_id=1, source_target_pairs={{0,3},{1,2},{2,1},{3,0},{4,7},{5,6},{6,5},{7,4},{8,11},{9,10},{10,... | collective-permute-start | bytes 786440 | tf_op jit(solution)/shard_map/ppermute | solution.py:555
  472.3 37.2 %collective-permute-start.47 = (bf16[512,512]{1,0:T(8,128)(2,1)}, bf16[512,512]{1,0:T(8,128)(2,1)}, u32[]{:S(2)}, u32[]{:S(2)}) collective-permute-start(bf16[512,512]{1,0:T(8,128)(2,1)} %get-tuple-element.285), channel_id=1, source_target_pairs={{0,1},{1,0},{2,3},{3,2},{4,5},{5,4},{6,7},{7,6},{8,9},{9,8},{10,11... | collective-permute-start | bytes 1572872 | tf_op jit(solution)/shard_map/ppermute | solution.py:555
  472.4 51.2 %collective-permute-start.48 = (bf16[512,512]{1,0:T(8,128)(2,1)}, bf16[512,512]{1,0:T(8,128)(2,1)}, u32[]{:S(2)}, u32[]{:S(2)}) collective-permute-start(bf16[512,512]{1,0:T(8,128)(2,1)} %get-tuple-element.286), channel_id=1, source_target_pairs={{0,2},{1,3},{2,0},{3,1},{4,6},{5,7},{6,4},{7,5},{8,10},{9,11},{10,... | collective-permute-start | bytes 1572872 | tf_op jit(solution)/shard_map/ppermute | solution.py:555
  499.9 23.7 %collective-permute-start.49 = (bf16[512,512]{1,0:T(8,128)(2,1)}, bf16[512,512]{1,0:T(8,128)(2,1)}, u32[]{:S(2)}, u32[]{:S(2)}) collective-permute-start(bf16[512,512]{1,0:T(8,128)(2,1)} %get-tuple-element.287), channel_id=1, source_target_pairs={{0,3},{1,2},{2,1},{3,0},{4,7},{5,6},{6,5},{7,4},{8,11},{9,10},{10,... | collective-permute-start | bytes 1572872 | tf_op jit(solution)/shard_map/ppermute | solution.py:555
  (85 other events, 732.7 us)
Sparse Core Ops, SparseCore 0:
  13.0 77.0 all-gather.3
  92.0 37.4 all-gather.5
  131.3 93.6 all-gather.7
  286.8 83.8 reduce-scatter.3
  376.7 52.3 reduce-scatter.7
  434.4 94.6 reduce-scatter.5
